TPU v7x, 32 devices: a whole 2x2x4 slice. The times are simulated.
32 devices in a mesh: gx: 8 (over z, x), row: 4 (over y, core).
Axes of the slice: x: 2, y: 2, z: 4, core: 2. Of those that a mesh axis runs over, the one named last changes fastest.
Arguments:
- adjoint_vectors: float32 [2, 5, 32, 192, 128], P(None, None, 'gx', 'row'), may hold values from -6 to 6
- base_density: float32 [32, 192, 128], P('gx', 'row'), may hold values from 0.6 to 1.4
- base_velocity: float32 [3, 32, 192, 128], P(None, 'gx', 'row'), may hold values from -3 to 3
- base_pressure: float32 [32, 192, 128], P('gx', 'row'), may hold values from 0.5 to 1.5
Outputs:
- adjoint_out: float32 [2, 5, 32, 192, 128], P(None, None, 'gx', 'row')
All inputs are finite; a program needn't handle non-finite values.
Results may differ from a plain program's by a relative error of at most 0.0003.
Values sent between devices are 32-bit elements; how exact they have to be, the bound alone decides.
No kernel may reach another device: no remote copies, remote signals or barrier semaphores. Data moves between devices by JAX's collectives and lax.ppermute only.
A program may use at most 64 MiB of HBM per device.

v0:
```python
import jax
import jax.numpy as jnp
from jax import lax
from jax.sharding import PartitionSpec as P

gamma_ratio = 1.4
viscosity = 0.1
time_step = 0.3


def with_halo(x, sides, width):
    for axis, dim in sides:
        peers, length = (lax.axis_size(axis), x.shape[dim])
        up = [(i, (i + 1) % peers) for i in range(peers - 1)]
        down = [(j, i) for i, j in up]
        last = lax.slice_in_dim(x, length - width, length, axis=dim)
        initial = lax.slice_in_dim(x, 0, width, axis=dim)
        before = lax.ppermute(last, axis, up)
        after = lax.ppermute(initial, axis, down)
        x = jnp.concatenate([before, x, after], axis=dim)
    return x


def theta_tables(azimuth):
    spacing = 2.0 * jnp.pi / azimuth
    index = jnp.arange(azimuth, dtype=jnp.int32)
    offset = index[:, None] - index[None, :]
    parity = jnp.mod(offset, 2).astype(jnp.float32)
    signs = 1.0 - 2.0 * parity
    angle = offset.astype(jnp.float32) * (spacing / 2.0)
    diagonal = offset == 0
    tangent = jnp.where(diagonal, 1.0, jnp.tan(angle))
    sine = jnp.where(diagonal, 1.0, jnp.sin(angle))
    first_table = jnp.where(diagonal, 0.0, 0.5 * signs * spacing / tangent)
    second_table = jnp.where(
        diagonal, -jnp.pi**2 / 3.0 - spacing**2 / 6.0, -0.5 * signs * spacing**2 / (sine * sine)
    )
    return (first_table, second_table)


def radial_factor(rows, total_rows):
    return (1.0 / (1.0 + (rows.astype(jnp.float32) + 0.5) / total_rows))[:, None]


def shifted(padded, start, axis):
    axis = padded.ndim + axis
    length = padded.shape[axis] - 4
    return lax.slice_in_dim(padded, start, start + length, axis=axis)


def first_diff(padded, axis):
    return (
        8.0 * (shifted(padded, 3, axis) - shifted(padded, 1, axis))
        - (shifted(padded, 4, axis) - shifted(padded, 0, axis))
    ) / 12.0


def second_diff(padded, axis):
    return (
        -shifted(padded, 4, axis)
        + 16.0 * shifted(padded, 3, axis)
        - 30.0 * shifted(padded, 2, axis)
        + 16.0 * shifted(padded, 1, axis)
        - shifted(padded, 0, axis)
    ) / 12.0


def azimuthal(field, table):
    shape = field.shape
    flat = field.reshape(-1, shape[-1])
    return jnp.dot(flat, table.T, precision=lax.Precision.HIGHEST).reshape(shape)


def flux(fields, base, direction):
    comp = 1 + direction
    density = base[0]
    safe_density = jnp.where(density > 0.0, density, 1.0)
    speed = base[comp]
    pressure = base[4]
    parts = []
    for member in range(5):
        value = fields[..., member, :, :, :]
        if member == 0:
            parts.append(speed * value)
        elif member == comp:
            parts.append(
                density * fields[..., 0, :, :, :]
                + speed * value
                + gamma_ratio * pressure * fields[..., 4, :, :, :]
            )
        elif member == 4:
            parts.append(fields[..., comp, :, :, :] / safe_density + speed * value)
        else:
            parts.append(speed * value)
    return jnp.stack(parts, axis=-4)


def combine(
    flux_x, flux_r, fields_x, fields_r, flux_theta, core, first_table, second_table, factor
):
    advect = (
        first_diff(flux_x, -3)
        + first_diff(flux_r, -2)
        + factor * azimuthal(flux_theta, first_table)
    )
    diffuse = second_diff(fields_x, -3) + second_diff(fields_r, -2) + azimuthal(core, second_table)
    return advect + viscosity * diffuse


def local(adjoint_vectors, base_density, base_velocity, base_pressure):
    cells_r = adjoint_vectors.shape[3]
    base = jnp.concatenate([base_density[None], base_velocity, base_pressure[None]], axis=0)
    first_table, second_table = theta_tables(adjoint_vectors.shape[4])
    row_start = lax.axis_index("row") * cells_r
    total_rows = lax.axis_size("row") * cells_r
    factor = radial_factor(row_start + jnp.arange(cells_r, dtype=jnp.int32), total_rows)
    base_padded = with_halo(base, (("gx", 1), ("row", 2)), 2)
    base_x = base_padded[..., :, 2:-2, :]
    base_r = base_padded[..., 2:-2, :, :]

    def section_rhs(fields):
        flux_theta = flux(fields, base, 2)
        fields_x = with_halo(fields, (("gx", 2),), 2)
        fields_r = with_halo(fields, (("row", 3),), 2)
        flux_x = flux(fields_x, base_x, 0)
        flux_r = flux(fields_r, base_r, 1)
        return combine(
            flux_x,
            flux_r,
            fields_x,
            fields_r,
            flux_theta,
            fields,
            first_table,
            second_table,
            factor,
        )

    section_one = adjoint_vectors + 0.5 * time_step * section_rhs(adjoint_vectors)
    return adjoint_vectors + time_step * section_rhs(section_one)


def solution(mesh):
    in_specs = (
        P(None, None, "gx", "row", None),
        P("gx", "row", None),
        P(None, "gx", "row", None),
        P("gx", "row", None),
    )
    out_specs = P(None, None, "gx", "row", None)
    return jax.shard_map(local, mesh=mesh, in_specs=in_specs, out_specs=out_specs, check_vma=False)
```

profile of v0, /device:TPU:17, one launch (start us, length us, event | category | flops | bytes accessed | tf_op | source)
XLA Modules:
  0.0 76.7 jit_solution(11679424322061320740)
XLA Ops:
  0.0 0.0 copy-start
  0.0 1.1 %pad_maximum_fusion.9 = f32[5,4,48,128]{3,2,1,0:T(8,128)S(1)} fusion(f32[1,4,48,128]{3,2,1,0:T(8,128)} %bitcast.45, f32[3,4,48,128]{3,2,1,0:T(8,128)} %param.6, f32[1,4,48,128]{3,2,1,0:T(8,128)} %bitcast.40), kind=kLoop, calls=%fused_computation.92 | loop fusion | flops 245760 | bytes 983040 | tf_op jit(solution)/shard_map/concatenate | solution.py:112
  1.2 0.0 copy-start.1
  1.2 0.0 copy-start.3
  1.2 0.8 fusion.116
  1.9 0.0 copy-start.2
  1.9 3.2 %collective-permute-start = (f32[5,2,48,128]{3,2,1,0:T(8,128)}, f32[5,2,48,128]{3,2,1,0:T(8,128)S(1)}, u32[]{:S(2)}, u32[]{:S(2)}) collective-permute-start(f32[5,2,48,128]{3,2,1,0:T(8,128)} %get-tuple-element.30), channel_id=1, source_target_pairs={{0,4},{4,8},{8,12},{12,16},{16,20},{20,24},{24,28},{1,5},{5,9},{9,... | collective-permute-start | bytes 737288 | tf_op jit(solution)/shard_map/ppermute | solution.py:18
  5.2 3.1 %collective-permute-start.1 = (f32[5,2,48,128]{3,2,1,0:T(8,128)S(1)}, f32[5,2,48,128]{3,2,1,0:T(8,128)S(1)}, u32[]{:S(2)}, u32[]{:S(2)}) collective-permute-start(f32[5,2,48,128]{3,2,1,0:T(8,128)S(1)} %get-tuple-element.31), channel_id=1, source_target_pairs={{4,0},{8,4},{12,8},{16,12},{20,16},{24,20},{28,24},{5,1},{9,5},{13... | collective-permute-start | bytes 737288 | tf_op jit(solution)/shard_map/ppermute | solution.py:19
  8.3 0.0 copy-done
  8.3 1.0 %fusion.114 = (f32[2,5,2,48,128]{4,3,2,1,0:T(8,128)}, f32[2,5,2,48,128]{4,3,2,1,0:T(8,128)}) fusion(f32[2,5,4,48,128]{4,3,2,1,0:T(8,128)S(1)} %copy-done), kind=kLoop, calls=%fused_computation.216 | loop fusion | bytes 1966080 | tf_op jit(solution)/shard_map/slice | solution.py:17
  9.3 2.2 %collective-permute-start.2 = (f32[2,5,2,48,128]{4,3,2,1,0:T(8,128)}, f32[2,5,2,48,128]{4,3,2,1,0:T(8,128)}, u32[]{:S(2)}, u32[]{:S(2)}) collective-permute-start(f32[2,5,2,48,128]{4,3,2,1,0:T(8,128)} %get-tuple-element.23), channel_id=1, source_target_pairs={{0,4},{4,8},{8,12},{12,16},{16,20},{20,24},{24,28},{1,5},{5,9},{9,... | collective-permute-start | bytes 1474568 | tf_op jit(solution)/shard_map/ppermute | solution.py:18
  11.5 0.7 fusion.115
  12.2 4.5 %collective-permute-start.6 = (f32[2,5,4,2,128]{4,3,2,1,0:T(2,128)}, f32[2,5,4,2,128]{4,3,2,1,0:T(2,128)}, u32[]{:S(2)}, u32[]{:S(2)}) collective-permute-start(f32[2,5,4,2,128]{4,3,2,1,0:T(2,128)} %get-tuple-element.25), channel_id=1, source_target_pairs={{0,1},{1,2},{2,3},{4,5},{5,6},{6,7},{8,9},{9,10},{10,11},{12,13},{... | collective-permute-start | bytes 122888 | tf_op jit(solution)/shard_map/ppermute | solution.py:18
  16.7 1.9 %collective-permute-start.7 = (f32[2,5,4,2,128]{4,3,2,1,0:T(2,128)}, f32[2,5,4,2,128]{4,3,2,1,0:T(2,128)S(1)}, u32[]{:S(2)}, u32[]{:S(2)}) collective-permute-start(f32[2,5,4,2,128]{4,3,2,1,0:T(2,128)} %get-tuple-element.24), channel_id=1, source_target_pairs={{1,0},{2,1},{3,2},{5,4},{6,5},{7,6},{9,8},{10,9},{11,10},{13,12},{... | collective-permute-start | bytes 122888 | tf_op jit(solution)/shard_map/ppermute | solution.py:19
  18.7 0.0 copy-done.1
  18.7 0.0 copy-done.3
  18.7 0.0 copy-done.2
  18.8 0.7 multiply_dynamic-update-slice_fusion.7
  19.4 0.7 multiply_dynamic-update-slice_fusion.6
  20.1 0.7 multiply_dynamic-update-slice_fusion.5
  20.8 1.3 %convolution_bitcast_fusion = f32[1920,128]{0,1:T(8,128)S(1)} fusion(f32[1920,128]{1,0:T(8,128)S(1)} %bitcast.39), kind=kOutput, calls=%fused_computation | convolution fusion | flops 377864192 | bytes 1966080 | tf_op jit(solution)/shard_map/dot_general | solution.py:71
  22.1 0.7 add_dynamic-update-slice_fusion.11
  22.9 0.7 add_dynamic-update-slice_fusion.10
  23.6 1.3 %copy.5 = f32[1920,128]{1,0:T(8,128)} copy(f32[1920,128]{0,1:T(8,128)S(1)} %convolution_bitcast_fusion) | data formatting | bytes 1966080 | tf_op jit(solution)/shard_map/dot_general | solution.py:71
  24.9 0.0 collective-permute-done.6
  24.9 4.0 %collective-permute-start.3 = (f32[2,5,2,48,128]{4,3,2,1,0:T(8,128)}, f32[2,5,2,48,128]{4,3,2,1,0:T(8,128)S(1)}, u32[]{:S(2)}, u32[]{:S(2)}) collective-permute-start(f32[2,5,2,48,128]{4,3,2,1,0:T(8,128)} %get-tuple-element.22), channel_id=1, source_target_pairs={{4,0},{8,4},{12,8},{16,12},{20,16},{24,20},{28,24},{5,1},{9,5},{13... | collective-permute-start | bytes 1474568 | tf_op jit(solution)/shard_map/ppermute | solution.py:19
  28.9 0.0 collective-permute-done.7
  28.9 0.9 %pad_maximum_fusion.1 = f32[2,5,4,52,128]{4,3,2,1,0:T(8,128)S(1)} fusion(f32[2,5,4,2,128]{4,3,2,1,0:T(2,128)S(1)} %collective-permute-done.7, f32[2,5,4,48,128]{4,3,2,1,0:T(8,128)S(1)} %copy-done, f32[2,5,4,2,128]{4,3,2,1,0:T(2,128)} %collective-permute-done.6), kind=kLoop, calls=%fused_computation.16 | loop fusion | flops 532480 | bytes 2129920 | tf_op jit(solution)/shard_map/concatenate | solution.py:20
  29.8 0.0 collective-permute-done
  29.8 0.0 collective-permute-done.1
  29.9 3.9 %collective-permute-start.4 = (f32[5,8,2,128]{3,2,1,0:T(2,128)S(1)}, f32[5,8,2,128]{3,2,1,0:T(2,128)S(1)}, u32[]{:S(2)}, u32[]{:S(2)}) collective-permute-start(f32[5,8,2,128]{3,2,1,0:T(2,128)S(1)} %get-tuple-element.20), channel_id=1, source_target_pairs={{0,1},{1,2},{2,3},{4,5},{5,6},{6,7},{8,9},{9,10},{10,11},{12,13},{... | collective-permute-start | bytes 122888 | tf_op jit(solution)/shard_map/ppermute | solution.py:18
  33.8 1.9 %collective-permute-start.5 = (f32[5,8,2,128]{3,2,1,0:T(2,128)S(1)}, f32[5,8,2,128]{3,2,1,0:T(2,128)S(1)}, u32[]{:S(2)}, u32[]{:S(2)}) collective-permute-start(f32[5,8,2,128]{3,2,1,0:T(2,128)S(1)} %get-tuple-element.21), channel_id=1, source_target_pairs={{1,0},{2,1},{3,2},{5,4},{6,5},{7,6},{9,8},{10,9},{11,10},{13,12},{... | collective-permute-start | bytes 122888 | tf_op jit(solution)/shard_map/ppermute | solution.py:19
  35.7 0.1 pad_maximum_fusion.8
  35.8 0.1 fusion.63
  35.9 0.0 collective-permute-done.4
  35.9 3.2 %collective-permute-done.5 = f32[5,8,2,128]{3,2,1,0:T(2,128)S(1)} collective-permute-done((f32[5,8,2,128]{3,2,1,0:T(2,128)S(1)}, f32[5,8,2,128]{3,2,1,0:T(2,128)S(1)}, u32[]{:S(2)}, u32[]{:S(2)}) %collective-permute-start.5) | collective-permute-done | bytes 40992 | tf_op jit(solution)/shard_map/ppermute | solution.py:19
  39.2 0.1 add_dynamic-update-slice_fusion.7
  39.4 0.0 collective-permute-done.2
  39.4 1.1 %constant_dynamic-update-slice_fusion.2 = (f32[2,5,8,48,128]{4,3,2,1,0:T(8,128)S(1)}, f32[2,5,6,48,128]{4,3,2,1,0:T(8,128)S(1)}) fusion(f32[2,5,2,48,128]{4,3,2,1,0:T(8,128)} %collective-permute-done.2), kind=kLoop, calls=%fused_computation.157 | loop fusion | bytes 1474560
  40.5 0.4 constant_dynamic-update-slice_fusion.1
  40.9 0.0 collective-permute-done.3
  40.9 0.1 constant_dynamic-update-slice_fusion
  41.1 0.1 add_dynamic-update-slice_fusion.3
  41.2 0.0 copy-start.4
  41.3 0.1 add_dynamic-update-slice_fusion.2
  41.4 1.0 %copy-done.4 = f32[1920,128]{1,0:T(8,128)S(1)} copy-done((f32[1920,128]{1,0:T(8,128)S(1)}, f32[1920,128]{1,0:T(8,128)}, u32[]{:S(2)}) %copy-start.4) | copy-done | bytes 983064
  42.5 4.0 %fusion.7 = f32[2,5,4,48,128]{4,3,2,1,0:T(8,128)S(1)} fusion(f32[2,5,4,48,128]{4,3,2,1,0:T(8,128)S(1)} %copy-done, f32[2,5,4,48,128]{4,3,2,1,0:T(8,128)} %add_dynamic-update-slice_fusion.10, f32[2,5,4,48,128]{4,3,2,1,0:T(8,128)S(1)} %bitcast.52, f32[2,5,4,2,128]{4,3,2,1,0:T(2,128)} %collective-permute-done.6, ...), kind=kOutput, calls=%fused_computation.15 | convolution fusion | flops 386695168 | bytes 17735872 | tf_op jit(solution)/shard_map/dot_general | solution.py:71
  46.4 0.1 fusion.112
  46.6 1.2 %fusion.74 = f32[2,5,4,48,128]{4,3,2,1,0:T(8,128)S(1)} fusion(f32[2,5,4,48,128]{4,3,2,1,0:T(8,128)S(1)} %fusion.7), kind=kOutput, calls=%fused_computation.168 | convolution fusion | flops 377864192 | bytes 1966080 | tf_op jit(solution)/shard_map/dot_general | solution.py:71
  47.8 2.7 %collective-permute-start.8 = (f32[2,5,2,48,128]{4,3,2,1,0:T(8,128)S(1)}, f32[2,5,2,48,128]{4,3,2,1,0:T(8,128)S(1)}, u32[]{:S(2)}, u32[]{:S(2)}) collective-permute-start(f32[2,5,2,48,128]{4,3,2,1,0:T(8,128)S(1)} %get-tuple-element.9), channel_id=1, source_target_pairs={{0,4},{4,8},{8,12},{12,16},{16,20},{20,24},{24,28},{1,5},{5,9},{9,... | collective-permute-start | bytes 1474568 | tf_op jit(solution)/shard_map/ppermute | solution.py:18
  50.4 3.5 %collective-permute-start.9 = (f32[2,5,2,48,128]{4,3,2,1,0:T(8,128)S(1)}, f32[2,5,2,48,128]{4,3,2,1,0:T(8,128)S(1)}, u32[]{:S(2)}, u32[]{:S(2)}) collective-permute-start(f32[2,5,2,48,128]{4,3,2,1,0:T(8,128)S(1)} %get-tuple-element.8), channel_id=1, source_target_pairs={{4,0},{8,4},{12,8},{16,12},{20,16},{24,20},{28,24},{5,1},{9,5},{13... | collective-permute-start | bytes 1474568 | tf_op jit(solution)/shard_map/ppermute | solution.py:19
  54.0 2.9 %collective-permute-start.10 = (f32[2,5,4,2,128]{4,3,2,1,0:T(2,128)S(1)}, f32[2,5,4,2,128]{4,3,2,1,0:T(2,128)S(1)}, u32[]{:S(2)}, u32[]{:S(2)}) collective-permute-start(f32[2,5,4,2,128]{4,3,2,1,0:T(2,128)S(1)} %get-tuple-element.11), channel_id=1, source_target_pairs={{0,1},{1,2},{2,3},{4,5},{5,6},{6,7},{8,9},{9,10},{10,11},{12,13},{... | collective-permute-start | bytes 122888 | tf_op jit(solution)/shard_map/ppermute | solution.py:18
  56.9 2.1 %collective-permute-start.11 = (f32[2,5,4,2,128]{4,3,2,1,0:T(2,128)S(1)}, f32[2,5,4,2,128]{4,3,2,1,0:T(2,128)S(1)}, u32[]{:S(2)}, u32[]{:S(2)}) collective-permute-start(f32[2,5,4,2,128]{4,3,2,1,0:T(2,128)S(1)} %get-tuple-element.10), channel_id=1, source_target_pairs={{1,0},{2,1},{3,2},{5,4},{6,5},{7,6},{9,8},{10,9},{11,10},{13,12},{... | collective-permute-start | bytes 122888 | tf_op jit(solution)/shard_map/ppermute | solution.py:19
  59.0 0.1 add_dynamic-update-slice_fusion.9
  59.1 0.0 collective-permute-done.10
  59.1 3.3 %collective-permute-done.11 = f32[2,5,4,2,128]{4,3,2,1,0:T(2,128)S(1)} collective-permute-done((f32[2,5,4,2,128]{4,3,2,1,0:T(2,128)S(1)}, f32[2,5,4,2,128]{4,3,2,1,0:T(2,128)S(1)}, u32[]{:S(2)}, u32[]{:S(2)}) %collective-permute-start.11) | collective-permute-done | bytes 40992 | tf_op jit(solution)/shard_map/ppermute | solution.py:19
  62.5 0.1 pad_maximum_fusion.2
  62.7 0.1 add_dynamic-update-slice_fusion.5
  62.8 9.0 %collective-permute-done.8 = f32[2,5,2,48,128]{4,3,2,1,0:T(8,128)S(1)} collective-permute-done((f32[2,5,2,48,128]{4,3,2,1,0:T(8,128)S(1)}, f32[2,5,2,48,128]{4,3,2,1,0:T(8,128)S(1)}, u32[]{:S(2)}, u32[]{:S(2)}) %collective-permute-start.8) | collective-permute-done | bytes 491552 | tf_op jit(solution)/shard_map/ppermute | solution.py:18
  71.8 0.8 %collective-permute-done.9 = f32[2,5,2,48,128]{4,3,2,1,0:T(8,128)S(1)} collective-permute-done((f32[2,5,2,48,128]{4,3,2,1,0:T(8,128)S(1)}, f32[2,5,2,48,128]{4,3,2,1,0:T(8,128)S(1)}, u32[]{:S(2)}, u32[]{:S(2)}) %collective-permute-start.9) | collective-permute-done | bytes 491552 | tf_op jit(solution)/shard_map/ppermute | solution.py:19
  72.6 0.1 pad_maximum_fusion
  72.8 0.1 add_dynamic-update-slice_fusion.1
  73.0 0.1 add_dynamic-update-slice_fusion
  73.1 3.7 %fusion.3 = f32[2,5,4,48,128]{4,3,2,1,0:T(8,128)} fusion(f32[2,5,4,48,128]{4,3,2,1,0:T(8,128)S(1)} %copy-done, f32[2,5,4,48,128]{4,3,2,1,0:T(8,128)S(1)} %add_dynamic-update-slice_fusion.8, f32[2,5,4,48,128]{4,3,2,1,0:T(8,128)S(1)} %fusion.74, f32[2,5,4,2,128]{4,3,2,1,0:T(2,128)S(1)} %collective-permute-done.10, f32[2,5,4,48,128]{4,3,2,1,0:T(8,128)S(1)} %fusion.7, ...), kind=kOutput, calls=%fused_computation.10 | convolution fusion | flops 388169728 | bytes 13844672 | tf_op jit(solution)/shard_map/dot_general | solution.py:71
  (27 shorter events, 0.8 us)
Async XLA Ops:
  0.0 8.3 %copy-start = (f32[2,5,4,48,128]{4,3,2,1,0:T(8,128)S(1)}, f32[2,5,4,48,128]{4,3,2,1,0:T(8,128)}, u32[]{:S(2)}) copy-start(f32[2,5,4,48,128]{4,3,2,1,0:T(8,128)} %param.4) | copy-start | bytes 2949124
  1.2 17.5 %copy-start.1 = (f32[3,4,48,128]{3,2,1,0:T(8,128)S(1)}, f32[3,4,48,128]{3,2,1,0:T(8,128)}, u32[]{:S(2)}) copy-start(f32[3,4,48,128]{3,2,1,0:T(8,128)} %param.6) | copy-start | bytes 884740
  1.2 17.5 %copy-start.3 = (f32[4,48,128]{2,1,0:T(8,128)S(1)}, f32[4,48,128]{2,1,0:T(8,128)}, u32[]{:S(2)}) copy-start(f32[4,48,128]{2,1,0:T(8,128)} %param.7) | copy-start | bytes 294916
  1.9 16.8 %copy-start.2 = (f32[4,48,128]{2,1,0:T(8,128)S(1)}, f32[4,48,128]{2,1,0:T(8,128)}, u32[]{:S(2)}) copy-start(f32[4,48,128]{2,1,0:T(8,128)} %param.5) | copy-start | bytes 294916
  1.9 27.9 %collective-permute-start = (f32[5,2,48,128]{3,2,1,0:T(8,128)}, f32[5,2,48,128]{3,2,1,0:T(8,128)S(1)}, u32[]{:S(2)}, u32[]{:S(2)}) collective-permute-start(f32[5,2,48,128]{3,2,1,0:T(8,128)} %get-tuple-element.30), channel_id=1, source_target_pairs={{0,4},{4,8},{8,12},{12,16},{16,20},{20,24},{24,28},{1,5},{5,9},{9,... | collective-permute-start | bytes 737288 | tf_op jit(solution)/shard_map/ppermute | solution.py:18
  5.2 24.6 %collective-permute-start.1 = (f32[5,2,48,128]{3,2,1,0:T(8,128)S(1)}, f32[5,2,48,128]{3,2,1,0:T(8,128)S(1)}, u32[]{:S(2)}, u32[]{:S(2)}) collective-permute-start(f32[5,2,48,128]{3,2,1,0:T(8,128)S(1)} %get-tuple-element.31), channel_id=1, source_target_pairs={{4,0},{8,4},{12,8},{16,12},{20,16},{24,20},{28,24},{5,1},{9,5},{13... | collective-permute-start | bytes 737288 | tf_op jit(solution)/shard_map/ppermute | solution.py:19
  9.3 30.1 %collective-permute-start.2 = (f32[2,5,2,48,128]{4,3,2,1,0:T(8,128)}, f32[2,5,2,48,128]{4,3,2,1,0:T(8,128)}, u32[]{:S(2)}, u32[]{:S(2)}) collective-permute-start(f32[2,5,2,48,128]{4,3,2,1,0:T(8,128)} %get-tuple-element.23), channel_id=1, source_target_pairs={{0,4},{4,8},{8,12},{12,16},{16,20},{20,24},{24,28},{1,5},{5,9},{9,... | collective-permute-start | bytes 1474568 | tf_op jit(solution)/shard_map/ppermute | solution.py:18
  12.2 12.7 %collective-permute-start.6 = (f32[2,5,4,2,128]{4,3,2,1,0:T(2,128)}, f32[2,5,4,2,128]{4,3,2,1,0:T(2,128)}, u32[]{:S(2)}, u32[]{:S(2)}) collective-permute-start(f32[2,5,4,2,128]{4,3,2,1,0:T(2,128)} %get-tuple-element.25), channel_id=1, source_target_pairs={{0,1},{1,2},{2,3},{4,5},{5,6},{6,7},{8,9},{9,10},{10,11},{12,13},{... | collective-permute-start | bytes 122888 | tf_op jit(solution)/shard_map/ppermute | solution.py:18
  16.7 12.1 %collective-permute-start.7 = (f32[2,5,4,2,128]{4,3,2,1,0:T(2,128)}, f32[2,5,4,2,128]{4,3,2,1,0:T(2,128)S(1)}, u32[]{:S(2)}, u32[]{:S(2)}) collective-permute-start(f32[2,5,4,2,128]{4,3,2,1,0:T(2,128)} %get-tuple-element.24), channel_id=1, source_target_pairs={{1,0},{2,1},{3,2},{5,4},{6,5},{7,6},{9,8},{10,9},{11,10},{13,12},{... | collective-permute-start | bytes 122888 | tf_op jit(solution)/shard_map/ppermute | solution.py:19
  24.9 16.0 %collective-permute-start.3 = (f32[2,5,2,48,128]{4,3,2,1,0:T(8,128)}, f32[2,5,2,48,128]{4,3,2,1,0:T(8,128)S(1)}, u32[]{:S(2)}, u32[]{:S(2)}) collective-permute-start(f32[2,5,2,48,128]{4,3,2,1,0:T(8,128)} %get-tuple-element.22), channel_id=1, source_target_pairs={{4,0},{8,4},{12,8},{16,12},{20,16},{24,20},{28,24},{5,1},{9,5},{13... | collective-permute-start | bytes 1474568 | tf_op jit(solution)/shard_map/ppermute | solution.py:19
  29.9 6.0 %collective-permute-start.4 = (f32[5,8,2,128]{3,2,1,0:T(2,128)S(1)}, f32[5,8,2,128]{3,2,1,0:T(2,128)S(1)}, u32[]{:S(2)}, u32[]{:S(2)}) collective-permute-start(f32[5,8,2,128]{3,2,1,0:T(2,128)S(1)} %get-tuple-element.20), channel_id=1, source_target_pairs={{0,1},{1,2},{2,3},{4,5},{5,6},{6,7},{8,9},{9,10},{10,11},{12,13},{... | collective-permute-start | bytes 122888 | tf_op jit(solution)/shard_map/ppermute | solution.py:18
  33.8 5.3 %collective-permute-start.5 = (f32[5,8,2,128]{3,2,1,0:T(2,128)S(1)}, f32[5,8,2,128]{3,2,1,0:T(2,128)S(1)}, u32[]{:S(2)}, u32[]{:S(2)}) collective-permute-start(f32[5,8,2,128]{3,2,1,0:T(2,128)S(1)} %get-tuple-element.21), channel_id=1, source_target_pairs={{1,0},{2,1},{3,2},{5,4},{6,5},{7,6},{9,8},{10,9},{11,10},{13,12},{... | collective-permute-start | bytes 122888 | tf_op jit(solution)/shard_map/ppermute | solution.py:19
  41.2 1.2 %copy-start.4 = (f32[1920,128]{1,0:T(8,128)S(1)}, f32[1920,128]{1,0:T(8,128)}, u32[]{:S(2)}) copy-start(f32[1920,128]{1,0:T(8,128)} %copy.5) | copy-start | bytes 2949124
  47.8 24.0 %collective-permute-start.8 = (f32[2,5,2,48,128]{4,3,2,1,0:T(8,128)S(1)}, f32[2,5,2,48,128]{4,3,2,1,0:T(8,128)S(1)}, u32[]{:S(2)}, u32[]{:S(2)}) collective-permute-start(f32[2,5,2,48,128]{4,3,2,1,0:T(8,128)S(1)} %get-tuple-element.9), channel_id=1, source_target_pairs={{0,4},{4,8},{8,12},{12,16},{16,20},{20,24},{24,28},{1,5},{5,9},{9,... | collective-permute-start | bytes 1474568 | tf_op jit(solution)/shard_map/ppermute | solution.py:18
  50.4 22.1 %collective-permute-start.9 = (f32[2,5,2,48,128]{4,3,2,1,0:T(8,128)S(1)}, f32[2,5,2,48,128]{4,3,2,1,0:T(8,128)S(1)}, u32[]{:S(2)}, u32[]{:S(2)}) collective-permute-start(f32[2,5,2,48,128]{4,3,2,1,0:T(8,128)S(1)} %get-tuple-element.8), channel_id=1, source_target_pairs={{4,0},{8,4},{12,8},{16,12},{20,16},{24,20},{28,24},{5,1},{9,5},{13... | collective-permute-start | bytes 1474568 | tf_op jit(solution)/shard_map/ppermute | solution.py:19
  54.0 5.2 %collective-permute-start.10 = (f32[2,5,4,2,128]{4,3,2,1,0:T(2,128)S(1)}, f32[2,5,4,2,128]{4,3,2,1,0:T(2,128)S(1)}, u32[]{:S(2)}, u32[]{:S(2)}) collective-permute-start(f32[2,5,4,2,128]{4,3,2,1,0:T(2,128)S(1)} %get-tuple-element.11), channel_id=1, source_target_pairs={{0,1},{1,2},{2,3},{4,5},{5,6},{6,7},{8,9},{9,10},{10,11},{12,13},{... | collective-permute-start | bytes 122888 | tf_op jit(solution)/shard_map/ppermute | solution.py:18
  56.9 5.6 %collective-permute-start.11 = (f32[2,5,4,2,128]{4,3,2,1,0:T(2,128)S(1)}, f32[2,5,4,2,128]{4,3,2,1,0:T(2,128)S(1)}, u32[]{:S(2)}, u32[]{:S(2)}) collective-permute-start(f32[2,5,4,2,128]{4,3,2,1,0:T(2,128)S(1)} %get-tuple-element.10), channel_id=1, source_target_pairs={{1,0},{2,1},{3,2},{5,4},{6,5},{7,6},{9,8},{10,9},{11,10},{13,12},{... | collective-permute-start | bytes 122888 | tf_op jit(solution)/shard_map/ppermute | solution.py:19
where the time goes:
time: 77.5 us; the launch traced here: 76.7 us
  starting transfers between devices  35.9 us (46%)
  waiting for transfers between devices  16.4 us (21%)
  matrix products  10.1 us (13%)
  other arithmetic  7.22 us (9%)
  local copies, waits for them, and re-layouts  6.57 us (8%)
    ppermute x6, starting transfers between devices, with_halo(): before = lax.ppermute(last, axis, up)  19.4 us
    ppermute x6, starting transfers between devices, with_halo(): after = lax.ppermute(initial, axis, down)  16.5 us
    dot_general x4, matrix products, azimuthal(): jnp.dot(flat, table.T, precision=lax.Precision.HIGHEST).reshape(shape)  10.1 us
    ppermute x6, waiting for transfers between devices, with_halo(): before = lax.ppermute(last, axis, up)  8.99 us
    ppermute x6, waiting for transfers between devices, with_halo(): after = lax.ppermute(initial, axis, down)  7.39 us
    unnamed x24, other arithmetic  3.66 us
    unnamed x12, local copies, waits for them, and re-layouts  2.57 us
    slice x4, local copies, waits for them, and re-layouts, with_halo(): initial = lax.slice_in_dim(x, 0, width, axis=dim)  1.8 us
  transfers between devices with their start and end apart: 12, of which 4 were waited for; matrix products, arithmetic and copies ran while one was open for 15% of the time, Pallas kernels for 0%

commit v1 on v0

v1 whole, which is shorter than its diff:
```python
import functools

import jax
import jax.numpy as jnp
import ml_dtypes
import numpy as np
from jax import lax
from jax.experimental import pallas as pl
from jax.experimental.pallas import tpu as pltpu
from jax.sharding import PartitionSpec as P

gamma_ratio = 1.4
viscosity = 0.1
time_step = 0.3

A1 = 8.0 / 12.0
A2 = 1.0 / 12.0
B1 = viscosity * 16.0 / 12.0
B2 = viscosity / 12.0
CENTRE = -2.0 * viscosity * 30.0 / 12.0
PAD = 8


def theta_table(azimuth):
    spacing = 2.0 * np.pi / azimuth
    index = np.arange(azimuth)
    offset = index[:, None] - index[None, :]
    signs = np.where(offset % 2 == 0, 1.0, -1.0)
    angle = offset * (spacing / 2.0)
    diagonal = offset == 0
    tangent = np.where(diagonal, 1.0, np.tan(angle))
    sine = np.where(diagonal, 1.0, np.sin(angle))
    first = np.where(diagonal, 0.0, 0.5 * signs * spacing / tangent)
    second = np.where(
        diagonal, -(np.pi**2) / 3.0 - spacing**2 / 6.0, -0.5 * signs * spacing**2 / (sine * sine)
    )
    table = np.concatenate([first.T, viscosity * second.T], axis=0).astype(np.float32)
    high = table.astype(ml_dtypes.bfloat16)
    low = (table - high.astype(np.float32)).astype(ml_dtypes.bfloat16)
    return np.concatenate([high, low], axis=1)


def section(
    dt, get, start, rho_ref, vel_ref, pr_ref, fac_ref, tab_ref,
    out_ref, xlo_ref, xhi_ref, rlo_ref, rhi_ref,
    wp, fr, fx, xh, xl, ys,
):
    cells, rows, width = rho_ref.shape
    step = 16
    zeros = jnp.zeros((PAD, width), jnp.float32)
    for f in range(5):
        for c in range(cells):
            for buf in (wp, fr):
                buf[f, c, 0:PAD] = zeros
                buf[f, c, PAD + rows : 2 * PAD + rows] = zeros
    for c in range(cells):
        for r in range(0, rows, step):
            at = slice(r, r + step)
            rho = rho_ref[c, at]
            inv = 1.0 / rho
            pg = gamma_ratio * pr_ref[c, at]
            fac = fac_ref[at]
            w = [get(f, c, r, step) for f in range(5)]
            q = rho * w[0] + pg * w[4]
            for d in range(3):
                speed = vel_ref[d, c, at]
                for f in range(5):
                    flow = speed * w[f]
                    if f == 1 + d:
                        flow = flow + q
                    elif f == 4:
                        flow = flow + w[1 + d] * inv
                    if d == 0:
                        fx[f, c, at] = flow
                    elif d == 1:
                        fr[f, c, PAD + r : PAD + r + step] = flow
                    else:
                        flow = flow * fac
                        high = flow.astype(jnp.bfloat16)
                        k = (f * cells + c) * rows + r
                        xh[k : k + step, 0:width] = high
                        xl[k : k + step, 0:width] = (flow - high.astype(jnp.float32)).astype(jnp.bfloat16)
            for f in range(5):
                wp[f, c, PAD + r : PAD + r + step] = w[f]
                high = w[f].astype(jnp.bfloat16)
                k = (f * cells + c) * rows + r
                xh[k : k + step, width : 2 * width] = high
                xl[k : k + step, width : 2 * width] = (w[f] - high.astype(jnp.float32)).astype(jnp.bfloat16)

    def radial(f, c, r, n):
        base = PAD + r
        sh = lambda buf, k: buf[f, c, base + k : base + k + n]
        return (
            A1 * (sh(fr, 1) - sh(fr, -1))
            - A2 * (sh(fr, 2) - sh(fr, -2))
            + B1 * (sh(wp, 1) + sh(wp, -1))
            - B2 * (sh(wp, 2) + sh(wp, -2))
        )

    for f in range(5):
        k = f * cells * rows
        span = cells * rows
        both = jnp.dot(xh[k : k + span], tab_ref[...], preferred_element_type=jnp.float32)
        low = jnp.dot(xl[k : k + span], tab_ref[:, 0:width], preferred_element_type=jnp.float32)
        ys[...] = (both[:, 0:width] + both[:, width:]) + low
        for r in range(0, rows, PAD):
            at = slice(r, r + PAD)
            ws = [wp[f, c, PAD + r : 2 * PAD + r] for c in range(cells)]
            fs = [fx[f, c, at] for c in range(cells)]

            def stream(i):
                total = None
                for k, a, b in ((1, A1, B1), (-1, -A1, B1), (2, -A2, -B2), (-2, A2, -B2)):
                    if 0 <= i + k < cells:
                        term = a * fs[i + k] + b * ws[i + k]
                        total = term if total is None else total + term
                return total

            xlo_ref[f, 0, at] = dt * stream(-2)
            xlo_ref[f, 1, at] = dt * stream(-1)
            xhi_ref[f, 0, at] = dt * stream(cells)
            xhi_ref[f, 1, at] = dt * stream(cells + 1)
            for c in range(cells):
                total = stream(c) + radial(f, c, r, PAD) + CENTRE * ws[c] + ys[c * rows + r : c * rows + r + PAD]
                out_ref[f, c, at] = start(f, c, r, PAD) + dt * total
        for c in range(cells):
            k = 2 * (f * cells + c)
            rlo_ref[k : k + 2] = dt * radial(f, c, -2, 2)
            rhi_ref[k : k + 2] = dt * radial(f, c, rows, 2)


def first_kernel(v, w_ref, rho_ref, vel_ref, pr_ref, fac_ref, tab_ref, *rest):
    get = lambda f, c, r, n: w_ref[v, f, c, r : r + n]
    section(0.5 * time_step, get, get, rho_ref, vel_ref, pr_ref, fac_ref, tab_ref, *rest)


def gather_edges(cells, rows, part_ref, left_ref, right_ref, rlo_ref, rhi_ref, write):
    for f in range(5):
        for c in range(cells):
            value = part_ref[f, c]
            if c < 2:
                value = value + left_ref[f, c]
            if c >= cells - 2:
                value = value + right_ref[f, c - (cells - 2)]
            write(f, c, value)
            k = 2 * (f * cells + c)
            yield f, c, k


def second_kernel(v, w_ref, part_ref, left_ref, right_ref, below_ref, above_ref,
                  rho_ref, vel_ref, pr_ref, fac_ref, tab_ref, *rest):
    *rest, s1 = rest
    cells, rows, width = rho_ref.shape

    def write(f, c, value):
        s1[f, c] = value

    for f, c, k in gather_edges(cells, rows, part_ref, left_ref, right_ref, below_ref, above_ref, write):
        s1[f, c, 0:2] += below_ref[k : k + 2]
        s1[f, c, rows - 2 : rows] += above_ref[k : k + 2]
    get = lambda f, c, r, n: s1[f, c, r : r + n]
    start = lambda f, c, r, n: w_ref[v, f, c, r : r + n]
    section(time_step, get, start, rho_ref, vel_ref, pr_ref, fac_ref, tab_ref, *rest)


def third_kernel(cells, rows, *refs):
    out_ref = refs[-1]
    for v in range(2):
        part_ref, left_ref, right_ref, below_ref, above_ref = refs[5 * v : 5 * v + 5]

        def write(f, c, value):
            out_ref[v, f, c] = value

        for f, c, k in gather_edges(cells, rows, part_ref, left_ref, right_ref, below_ref, above_ref, write):
            out_ref[v, f, c, 0:2] += below_ref[k : k + 2]
            out_ref[v, f, c, rows - 2 : rows] += above_ref[k : k + 2]


VM = pl.BlockSpec(memory_space=pltpu.VMEM)


def section_shapes(cells, rows, width):
    f32 = jnp.float32
    outs = [
        jax.ShapeDtypeStruct((5, cells, rows, width), f32),
        jax.ShapeDtypeStruct((5, 2, rows, width), f32),
        jax.ShapeDtypeStruct((5, 2, rows, width), f32),
        jax.ShapeDtypeStruct((5 * cells * 2, width), f32),
        jax.ShapeDtypeStruct((5 * cells * 2, width), f32),
    ]
    scratch = [
        pltpu.VMEM((5, cells, rows + 2 * PAD, width), f32),
        pltpu.VMEM((5, cells, rows + 2 * PAD, width), f32),
        pltpu.VMEM((5, cells, rows, width), f32),
        pltpu.VMEM((5 * cells * rows, 2 * width), jnp.bfloat16),
        pltpu.VMEM((5 * cells * rows, 2 * width), jnp.bfloat16),
        pltpu.VMEM((cells * rows, width), f32),
    ]
    return outs, scratch


PARAMS = pltpu.CompilerParams(vmem_limit_bytes=40 << 20)


def local(adjoint_vectors, base_density, base_velocity, base_pressure):
    _, _, cells, rows, width = adjoint_vectors.shape
    total_rows = lax.axis_size("row") * rows
    index = lax.axis_index("row") * rows + lax.broadcasted_iota(jnp.int32, (rows, width), 0)
    fac = 1.0 / (1.0 + (index.astype(jnp.float32) + 0.5) / total_rows)
    tab = jnp.asarray(theta_table(width))
    outs, scratch = section_shapes(cells, rows, width)
    steady = (base_density, base_velocity, base_pressure, fac, tab)

    gx, row = lax.axis_size("gx"), lax.axis_size("row")
    up = lambda n: [(i, i + 1) for i in range(n - 1)]
    down = lambda n: [(i + 1, i) for i in range(n - 1)]

    def trade(parts):
        part, xlo, xhi, rlo, rhi = parts
        left = lax.ppermute(xhi, "gx", up(gx))
        right = lax.ppermute(xlo, "gx", down(gx))
        below = lax.ppermute(rhi, "row", up(row))
        above = lax.ppermute(rlo, "row", down(row))
        return part, left, right, below, above

    def first(v):
        return pl.pallas_call(
            functools.partial(first_kernel, v), name=f"one_{v}", out_shape=outs, in_specs=[VM] * 6,
            out_specs=[VM] * 5, scratch_shapes=scratch, compiler_params=PARAMS,
        )(adjoint_vectors, *steady)

    def second(v, traded):
        return pl.pallas_call(
            functools.partial(second_kernel, v), name=f"two_{v}", out_shape=outs, in_specs=[VM] * 11,
            out_specs=[VM] * 5, scratch_shapes=scratch + [pltpu.VMEM((5, cells, rows, width), jnp.float32)],
            compiler_params=PARAMS,
        )(adjoint_vectors, *traded, *steady)

    traded = [trade(first(v)) for v in range(2)]
    traded = [trade(second(v, traded[v])) for v in range(2)]
    return pl.pallas_call(
        functools.partial(third_kernel, cells, rows), name="three",
        out_shape=jax.ShapeDtypeStruct(adjoint_vectors.shape, jnp.float32),
        in_specs=[VM] * 10, out_specs=VM, compiler_params=PARAMS,
    )(*traded[0], *traded[1])


def solution(mesh):
    in_specs = (
        P(None, None, "gx", "row", None),
        P("gx", "row", None),
        P(None, "gx", "row", None),
        P("gx", "row", None),
    )
    out_specs = P(None, None, "gx", "row", None)
    return jax.shard_map(local, mesh=mesh, in_specs=in_specs, out_specs=out_specs, check_vma=False)
```

time: 77.5 us -> 72.6 us (0.937)
  matrix products: 10.1 us -> 0 us
  starting transfers between devices: 35.9 us -> 45.9 us
  other arithmetic: 7.22 us -> 0.01 us
  Pallas kernels: 0 us -> 6.51 us
  waiting for transfers between devices: 16.4 us -> 14.3 us
  local copies, waits for them, and re-layouts: 6.57 us -> 4.93 us
    dot_general x4 -> x0, matrix products: 10.1 us -> none  [azimuthal(): jnp.dot(flat, table.T, precision=lax.Precision.HIGHEST).reshape(shape)]
    ppermute x12 -> x16, starting transfers between devices: 35.9 us -> 45.9 us  [the longest x4 15.4 us: trade(): right = lax.ppermute(xlo, 'gx', down(gx))]
    pallas_call x0 -> x5, Pallas kernels: none -> 6.51 us  [the longest x2 2.78 us: second(): pl.pallas_call(functools.partial(second_kernel, v), name=f'two_{v}', out_...]
    unnamed x24 -> x0, other arithmetic: 3.66 us -> none
    slice x5 -> x0, local copies, waits for them, and re-layouts: 2.56 us -> none  [the longest x4 1.8 us: with_halo(): initial = lax.slice_in_dim(x, 0, width, axis=dim)]
    concatenate x5 -> x0, other arithmetic: 2.4 us -> none  [the longest x4 1.26 us: with_halo(): x = jnp.concatenate([before, x, after], axis=dim)]
    unnamed x12 -> x10, local copies, waits for them, and re-layouts: 2.57 us -> 4.86 us
    ppermute x12 -> x16, waiting for transfers between devices: 16.4 us -> 14.3 us  [the longest x4 11.4 us: trade(): above = lax.ppermute(rlo, 'row', down(row))]
  transfers between devices with their start and end apart: 12 -> 16, of which waited for: 4 -> 6; matrix products, arithmetic and copies ran while one was open for 15% -> 0% of each run, Pallas kernels for 0% -> 6%
where the time goes in v1:
time: 72.6 us; the launch traced here: 71.9 us
  starting transfers between devices  45.9 us (63%)
  waiting for transfers between devices  14.3 us (20%)
  Pallas kernels  6.51 us (9%)
  local copies, waits for them, and re-layouts  4.93 us (7%)
    ppermute x4, starting transfers between devices, trade(): right = lax.ppermute(xlo, 'gx', down(gx))  15.4 us
    ppermute x4, starting transfers between devices, trade(): below = lax.ppermute(rhi, 'row', up(row))  12.9 us
    ppermute x4, waiting for transfers between devices, trade(): above = lax.ppermute(rlo, 'row', down(row))  11.4 us
    ppermute x4, starting transfers between devices, trade(): left = lax.ppermute(xhi, 'gx', up(gx))  9.29 us
    ppermute x4, starting transfers between devices, trade(): above = lax.ppermute(rlo, 'row', down(row))  8.28 us
    unnamed x10, local copies, waits for them, and re-layouts  4.86 us
    ppermute x4, waiting for transfers between devices, trade(): below = lax.ppermute(rhi, 'row', up(row))  2.93 us
    pallas_call x2, Pallas kernels, second(): pl.pallas_call(functools.partial(second_kernel, v), name=f'two_{v}', out_...  2.78 us
  transfers between devices with their start and end apart: 16, of which 6 were waited for; matrix products, arithmetic and copies ran while one was open for 0% of the time, Pallas kernels for 6%

profile of v1, /device:TPU:17, one launch (start us, length us, event | category | flops | bytes accessed | tf_op | source)
XLA Modules:
  0.0 71.9 jit_solution(9293610161521634197)
XLA Ops:
  0.0 0.1 iota.7.fac_ref
  0.1 0.0 copy-start
  0.1 1.2 %copy-done = f32[2,5,4,48,128]{4,3,2,1,0:T(8,128)S(1)} copy-done((f32[2,5,4,48,128]{4,3,2,1,0:T(8,128)S(1)}, f32[2,5,4,48,128]{4,3,2,1,0:T(8,128)}, u32[]{:S(2)}) %copy-start) | copy-done | bytes 983064
  1.3 0.0 copy-start.1
  1.3 1.0 %copy-done.1 = f32[3,4,48,128]{3,2,1,0:T(8,128)S(1)} copy-done((f32[3,4,48,128]{3,2,1,0:T(8,128)S(1)}, f32[3,4,48,128]{3,2,1,0:T(8,128)}, u32[]{:S(2)}) %copy-start.1) | copy-done | bytes 294936
  2.3 0.0 copy-start.2
  2.3 0.9 %copy-done.2 = bf16[256,256]{1,0:T(8,128)(2,1)S(1)} copy-done((bf16[256,256]{1,0:T(8,128)(2,1)S(1)}, bf16[256,256]{1,0:T(8,128)(2,1)}, u32[]{:S(2)}) %copy-start.2) | copy-done | bytes 131096
  3.2 0.0 copy-start.3
  3.2 0.9 %copy-done.3 = f32[4,48,128]{2,1,0:T(8,128)S(1)} copy-done((f32[4,48,128]{2,1,0:T(8,128)S(1)}, f32[4,48,128]{2,1,0:T(8,128)}, u32[]{:S(2)}) %copy-start.3) | copy-done | bytes 98328
  4.1 0.0 copy-start.4
  4.1 0.9 %copy-done.4 = f32[4,48,128]{2,1,0:T(8,128)S(1)} copy-done((f32[4,48,128]{2,1,0:T(8,128)S(1)}, f32[4,48,128]{2,1,0:T(8,128)}, u32[]{:S(2)}) %copy-start.4) | copy-done | bytes 98328
  4.9 1.3 %one_1.1 = (f32[5,4,48,128]{3,2,1,0:T(8,128)S(1)}, f32[5,2,48,128]{3,2,1,0:T(8,128)S(1)}, f32[5,2,48,128]{3,2,1,0:T(8,128)S(1)}, f32[40,128]{1,0:T(8,128)S(1)}, f32[40,128]{1,0:T(8,128)S(1)}) custom-call(f32[2,5,4,48,128]{4,3,2,1,0:T(8,128)S(1)} %copy-done, f32[4,48,128]{2,1,0:T(8,128)S(1)} %copy-done.3, f32[3,4,48,128]{3,2,1,0:T(8,128)S(1)} %copy-done.1, ...), custom_call_target="tpu_custom_call" | custom-call | tf_op jit(solution)/shard_map/one_1/pallas_call | solution.py:227
  6.3 3.1 %collective-permute-start.8 = (f32[5,2,48,128]{3,2,1,0:T(8,128)S(1)}, f32[5,2,48,128]{3,2,1,0:T(8,128)S(1)}, u32[]{:S(2)}, u32[]{:S(2)}) collective-permute-start(f32[5,2,48,128]{3,2,1,0:T(8,128)S(1)} %get-tuple-element.36), channel_id=1, source_target_pairs={{0,4},{4,8},{8,12},{12,16},{16,20},{20,24},{24,28},{1,5},{5,9},{9,... | collective-permute-start | bytes 737288 | tf_op jit(solution)/shard_map/ppermute | solution.py:220
  9.4 3.1 %collective-permute-start.9 = (f32[5,2,48,128]{3,2,1,0:T(8,128)S(1)}, f32[5,2,48,128]{3,2,1,0:T(8,128)S(1)}, u32[]{:S(2)}, u32[]{:S(2)}) collective-permute-start(f32[5,2,48,128]{3,2,1,0:T(8,128)S(1)} %get-tuple-element.37), channel_id=1, source_target_pairs={{4,0},{8,4},{12,8},{16,12},{20,16},{24,20},{28,24},{5,1},{9,5},{13... | collective-permute-start | bytes 737288 | tf_op jit(solution)/shard_map/ppermute | solution.py:221
  12.4 1.3 %one_0.1 = (f32[5,4,48,128]{3,2,1,0:T(8,128)S(1)}, f32[5,2,48,128]{3,2,1,0:T(8,128)S(1)}, f32[5,2,48,128]{3,2,1,0:T(8,128)S(1)}, f32[40,128]{1,0:T(8,128)S(1)}, f32[40,128]{1,0:T(8,128)S(1)}) custom-call(f32[2,5,4,48,128]{4,3,2,1,0:T(8,128)S(1)} %copy-done, f32[4,48,128]{2,1,0:T(8,128)S(1)} %copy-done.3, f32[3,4,48,128]{3,2,1,0:T(8,128)S(1)} %copy-done.1, ...), custom_call_target="tpu_custom_call" | custom-call | tf_op jit(solution)/shard_map/one_0/pallas_call | solution.py:227
  13.8 2.2 %collective-permute-start = (f32[5,2,48,128]{3,2,1,0:T(8,128)S(1)}, f32[5,2,48,128]{3,2,1,0:T(8,128)S(1)}, u32[]{:S(2)}, u32[]{:S(2)}) collective-permute-start(f32[5,2,48,128]{3,2,1,0:T(8,128)S(1)} %get-tuple-element.26), channel_id=1, source_target_pairs={{0,4},{4,8},{8,12},{12,16},{16,20},{20,24},{24,28},{1,5},{5,9},{9,... | collective-permute-start | bytes 737288 | tf_op jit(solution)/shard_map/ppermute | solution.py:220
  16.0 4.0 %collective-permute-start.1 = (f32[5,2,48,128]{3,2,1,0:T(8,128)S(1)}, f32[5,2,48,128]{3,2,1,0:T(8,128)S(1)}, u32[]{:S(2)}, u32[]{:S(2)}) collective-permute-start(f32[5,2,48,128]{3,2,1,0:T(8,128)S(1)} %get-tuple-element.27), channel_id=1, source_target_pairs={{4,0},{8,4},{12,8},{16,12},{20,16},{24,20},{28,24},{5,1},{9,5},{13... | collective-permute-start | bytes 737288 | tf_op jit(solution)/shard_map/ppermute | solution.py:221
  19.9 4.8 %collective-permute-start.10 = (f32[40,128]{1,0:T(8,128)S(1)}, f32[40,128]{1,0:T(8,128)S(1)}, u32[]{:S(2)}, u32[]{:S(2)}) collective-permute-start(f32[40,128]{1,0:T(8,128)S(1)} %get-tuple-element.38), channel_id=1, source_target_pairs={{0,1},{1,2},{2,3},{4,5},{5,6},{6,7},{8,9},{9,10},{10,11},{12,13},{... | collective-permute-start | bytes 61448 | tf_op jit(solution)/shard_map/ppermute | solution.py:222
  24.8 0.9 %collective-permute-done.10.below_ref = f32[40,128]{1,0:T(8,128)S(1)} collective-permute-done((f32[40,128]{1,0:T(8,128)S(1)}, f32[40,128]{1,0:T(8,128)S(1)}, u32[]{:S(2)}, u32[]{:S(2)}) %collective-permute-start.10) | collective-permute-done | bytes 20512 | tf_op jit(solution)/shard_map/ppermute | solution.py:222
  25.7 1.9 %collective-permute-start.11 = (f32[40,128]{1,0:T(8,128)S(1)}, f32[40,128]{1,0:T(8,128)S(1)}, u32[]{:S(2)}, u32[]{:S(2)}) collective-permute-start(f32[40,128]{1,0:T(8,128)S(1)} %get-tuple-element.39), channel_id=1, source_target_pairs={{1,0},{2,1},{3,2},{5,4},{6,5},{7,6},{9,8},{10,9},{11,10},{13,12},{... | collective-permute-start | bytes 61448 | tf_op jit(solution)/shard_map/ppermute | solution.py:223
  27.6 4.0 %collective-permute-done.11.above_ref = f32[40,128]{1,0:T(8,128)S(1)} collective-permute-done((f32[40,128]{1,0:T(8,128)S(1)}, f32[40,128]{1,0:T(8,128)S(1)}, u32[]{:S(2)}, u32[]{:S(2)}) %collective-permute-start.11) | collective-permute-done | bytes 20512 | tf_op jit(solution)/shard_map/ppermute | solution.py:223
  31.6 1.9 %collective-permute-start.2 = (f32[40,128]{1,0:T(8,128)S(1)}, f32[40,128]{1,0:T(8,128)S(1)}, u32[]{:S(2)}, u32[]{:S(2)}) collective-permute-start(f32[40,128]{1,0:T(8,128)S(1)} %get-tuple-element.28), channel_id=1, source_target_pairs={{0,1},{1,2},{2,3},{4,5},{5,6},{6,7},{8,9},{9,10},{10,11},{12,13},{... | collective-permute-start | bytes 61448 | tf_op jit(solution)/shard_map/ppermute | solution.py:222
  33.5 0.0 collective-permute-done.8.left_ref
  33.5 2.4 %collective-permute-start.3 = (f32[40,128]{1,0:T(8,128)S(1)}, f32[40,128]{1,0:T(8,128)S(1)}, u32[]{:S(2)}, u32[]{:S(2)}) collective-permute-start(f32[40,128]{1,0:T(8,128)S(1)} %get-tuple-element.29), channel_id=1, source_target_pairs={{1,0},{2,1},{3,2},{5,4},{6,5},{7,6},{9,8},{10,9},{11,10},{13,12},{... | collective-permute-start | bytes 61448 | tf_op jit(solution)/shard_map/ppermute | solution.py:223
  36.0 0.0 collective-permute-done.9.right_ref
  36.0 1.4 %two_1.1 = (f32[5,4,48,128]{3,2,1,0:T(8,128)S(1)}, f32[5,2,48,128]{3,2,1,0:T(8,128)S(1)}, f32[5,2,48,128]{3,2,1,0:T(8,128)S(1)}, f32[40,128]{1,0:T(8,128)S(1)}, f32[40,128]{1,0:T(8,128)S(1)}) custom-call(f32[2,5,4,48,128]{4,3,2,1,0:T(8,128)S(1)} %copy-done, f32[5,4,48,128]{3,2,1,0:T(8,128)S(1)} %get-tuple-element.35.part_ref, ...), custom_call_target="tpu_custom_call" | custom-call | tf_op jit(solution)/shard_map/two_1/pallas_call | solution.py:233
  37.4 1.9 %collective-permute-start.12 = (f32[5,2,48,128]{3,2,1,0:T(8,128)S(1)}, f32[5,2,48,128]{3,2,1,0:T(8,128)S(1)}, u32[]{:S(2)}, u32[]{:S(2)}) collective-permute-start(f32[5,2,48,128]{3,2,1,0:T(8,128)S(1)} %get-tuple-element.41), channel_id=1, source_target_pairs={{0,4},{4,8},{8,12},{12,16},{16,20},{20,24},{24,28},{1,5},{5,9},{9,... | collective-permute-start | bytes 737288 | tf_op jit(solution)/shard_map/ppermute | solution.py:220
  39.3 0.0 collective-permute-done.2.below_ref
  39.3 4.3 %collective-permute-start.13 = (f32[5,2,48,128]{3,2,1,0:T(8,128)S(1)}, f32[5,2,48,128]{3,2,1,0:T(8,128)S(1)}, u32[]{:S(2)}, u32[]{:S(2)}) collective-permute-start(f32[5,2,48,128]{3,2,1,0:T(8,128)S(1)} %get-tuple-element.42), channel_id=1, source_target_pairs={{4,0},{8,4},{12,8},{16,12},{20,16},{24,20},{28,24},{5,1},{9,5},{13... | collective-permute-start | bytes 737288 | tf_op jit(solution)/shard_map/ppermute | solution.py:221
  43.6 0.0 collective-permute-done.3.above_ref
  43.6 0.0 collective-permute-done.left_ref
  43.6 0.0 collective-permute-done.1.right_ref
  43.6 1.4 %two_0.1 = (f32[5,4,48,128]{3,2,1,0:T(8,128)S(1)}, f32[5,2,48,128]{3,2,1,0:T(8,128)S(1)}, f32[5,2,48,128]{3,2,1,0:T(8,128)S(1)}, f32[40,128]{1,0:T(8,128)S(1)}, f32[40,128]{1,0:T(8,128)S(1)}) custom-call(f32[2,5,4,48,128]{4,3,2,1,0:T(8,128)S(1)} %copy-done, f32[5,4,48,128]{3,2,1,0:T(8,128)S(1)} %get-tuple-element.25.part_ref, ...), custom_call_target="tpu_custom_call" | custom-call | tf_op jit(solution)/shard_map/two_0/pallas_call | solution.py:233
  45.0 2.0 %collective-permute-start.4 = (f32[5,2,48,128]{3,2,1,0:T(8,128)S(1)}, f32[5,2,48,128]{3,2,1,0:T(8,128)S(1)}, u32[]{:S(2)}, u32[]{:S(2)}) collective-permute-start(f32[5,2,48,128]{3,2,1,0:T(8,128)S(1)} %get-tuple-element.31), channel_id=1, source_target_pairs={{0,4},{4,8},{8,12},{12,16},{16,20},{20,24},{24,28},{1,5},{5,9},{9,... | collective-permute-start | bytes 737288 | tf_op jit(solution)/shard_map/ppermute | solution.py:220
  47.1 4.1 %collective-permute-start.5 = (f32[5,2,48,128]{3,2,1,0:T(8,128)S(1)}, f32[5,2,48,128]{3,2,1,0:T(8,128)S(1)}, u32[]{:S(2)}, u32[]{:S(2)}) collective-permute-start(f32[5,2,48,128]{3,2,1,0:T(8,128)S(1)} %get-tuple-element.32), channel_id=1, source_target_pairs={{4,0},{8,4},{12,8},{16,12},{20,16},{24,20},{28,24},{5,1},{9,5},{13... | collective-permute-start | bytes 737288 | tf_op jit(solution)/shard_map/ppermute | solution.py:221
  51.2 4.3 %collective-permute-start.14 = (f32[40,128]{1,0:T(8,128)S(1)}, f32[40,128]{1,0:T(8,128)S(1)}, u32[]{:S(2)}, u32[]{:S(2)}) collective-permute-start(f32[40,128]{1,0:T(8,128)S(1)} %get-tuple-element.43), channel_id=1, source_target_pairs={{0,1},{1,2},{2,3},{4,5},{5,6},{6,7},{8,9},{9,10},{10,11},{12,13},{... | collective-permute-start | bytes 61448 | tf_op jit(solution)/shard_map/ppermute | solution.py:222
  55.5 0.9 %collective-permute-done.14.refs_8_ = f32[40,128]{1,0:T(8,128)S(1)} collective-permute-done((f32[40,128]{1,0:T(8,128)S(1)}, f32[40,128]{1,0:T(8,128)S(1)}, u32[]{:S(2)}, u32[]{:S(2)}) %collective-permute-start.14) | collective-permute-done | bytes 20512 | tf_op jit(solution)/shard_map/ppermute | solution.py:222
  56.4 1.9 %collective-permute-start.15 = (f32[40,128]{1,0:T(8,128)S(1)}, f32[40,128]{1,0:T(8,128)S(1)}, u32[]{:S(2)}, u32[]{:S(2)}) collective-permute-start(f32[40,128]{1,0:T(8,128)S(1)} %get-tuple-element.44), channel_id=1, source_target_pairs={{1,0},{2,1},{3,2},{5,4},{6,5},{7,6},{9,8},{10,9},{11,10},{13,12},{... | collective-permute-start | bytes 61448 | tf_op jit(solution)/shard_map/ppermute | solution.py:223
  58.3 4.0 %collective-permute-done.15.refs_9_ = f32[40,128]{1,0:T(8,128)S(1)} collective-permute-done((f32[40,128]{1,0:T(8,128)S(1)}, f32[40,128]{1,0:T(8,128)S(1)}, u32[]{:S(2)}, u32[]{:S(2)}) %collective-permute-start.15) | collective-permute-done | bytes 20512 | tf_op jit(solution)/shard_map/ppermute | solution.py:223
  62.3 1.9 %collective-permute-start.6 = (f32[40,128]{1,0:T(8,128)S(1)}, f32[40,128]{1,0:T(8,128)S(1)}, u32[]{:S(2)}, u32[]{:S(2)}) collective-permute-start(f32[40,128]{1,0:T(8,128)S(1)} %get-tuple-element.33), channel_id=1, source_target_pairs={{0,1},{1,2},{2,3},{4,5},{5,6},{6,7},{8,9},{9,10},{10,11},{12,13},{... | collective-permute-start | bytes 61448 | tf_op jit(solution)/shard_map/ppermute | solution.py:222
  64.2 1.2 %collective-permute-done.6.refs_3_ = f32[40,128]{1,0:T(8,128)S(1)} collective-permute-done((f32[40,128]{1,0:T(8,128)S(1)}, f32[40,128]{1,0:T(8,128)S(1)}, u32[]{:S(2)}, u32[]{:S(2)}) %collective-permute-start.6) | collective-permute-done | bytes 20512 | tf_op jit(solution)/shard_map/ppermute | solution.py:222
  65.4 2.1 %collective-permute-start.7 = (f32[40,128]{1,0:T(8,128)S(1)}, f32[40,128]{1,0:T(8,128)S(1)}, u32[]{:S(2)}, u32[]{:S(2)}) collective-permute-start(f32[40,128]{1,0:T(8,128)S(1)} %get-tuple-element.34), channel_id=1, source_target_pairs={{1,0},{2,1},{3,2},{5,4},{6,5},{7,6},{9,8},{10,9},{11,10},{13,12},{... | collective-permute-start | bytes 61448 | tf_op jit(solution)/shard_map/ppermute | solution.py:223
  67.5 3.3 %collective-permute-done.7.refs_4_ = f32[40,128]{1,0:T(8,128)S(1)} collective-permute-done((f32[40,128]{1,0:T(8,128)S(1)}, f32[40,128]{1,0:T(8,128)S(1)}, u32[]{:S(2)}, u32[]{:S(2)}) %collective-permute-start.7) | collective-permute-done | bytes 20512 | tf_op jit(solution)/shard_map/ppermute | solution.py:223
  70.8 0.0 collective-permute-done.12.refs_6_
  70.8 0.0 collective-permute-done.13.refs_7_
  70.8 0.0 collective-permute-done.4.refs_1_
  70.8 0.0 collective-permute-done.5.refs_2_
  70.8 1.1 %three.1 = f32[2,5,4,48,128]{4,3,2,1,0:T(8,128)} custom-call(f32[5,4,48,128]{3,2,1,0:T(8,128)S(1)} %get-tuple-element.30.refs_0_, f32[5,2,48,128]{3,2,1,0:T(8,128)S(1)} %collective-permute-done.4.refs_1_, f32[5,2,48,128]{3,2,1,0:T(8,128)S(1)} %collective-permute-done.5.refs_2_, f32[40,128]{1,0:T(8,128)S(1)} %collective-permute-done.6.refs_3_, ...), custom_call_target="tpu_custom_call" | custom-call | tf_op jit(solution)/shard_map/three/pallas_call | solution.py:241
  (1 shorter events, 0.0 us)
Async XLA Ops:
  0.1 1.2 %copy-start = (f32[2,5,4,48,128]{4,3,2,1,0:T(8,128)S(1)}, f32[2,5,4,48,128]{4,3,2,1,0:T(8,128)}, u32[]{:S(2)}) copy-start(f32[2,5,4,48,128]{4,3,2,1,0:T(8,128)} %w_ref.7) | copy-start | bytes 2949124
  1.3 1.0 %copy-start.1 = (f32[3,4,48,128]{3,2,1,0:T(8,128)S(1)}, f32[3,4,48,128]{3,2,1,0:T(8,128)}, u32[]{:S(2)}) copy-start(f32[3,4,48,128]{3,2,1,0:T(8,128)} %vel_ref.7) | copy-start | bytes 884740
  2.3 0.9 %copy-start.2 = (bf16[256,256]{1,0:T(8,128)(2,1)S(1)}, bf16[256,256]{1,0:T(8,128)(2,1)}, u32[]{:S(2)}) copy-start(bf16[256,256]{1,0:T(8,128)(2,1)} %constant.15.clone.tab_ref) | copy-start | bytes 393220
  3.2 0.9 %copy-start.3 = (f32[4,48,128]{2,1,0:T(8,128)S(1)}, f32[4,48,128]{2,1,0:T(8,128)}, u32[]{:S(2)}) copy-start(f32[4,48,128]{2,1,0:T(8,128)} %rho_ref.7) | copy-start | bytes 294916
  4.1 0.9 %copy-start.4 = (f32[4,48,128]{2,1,0:T(8,128)S(1)}, f32[4,48,128]{2,1,0:T(8,128)}, u32[]{:S(2)}) copy-start(f32[4,48,128]{2,1,0:T(8,128)} %pr_ref.7) | copy-start | bytes 294916
  6.3 27.3 %collective-permute-start.8 = (f32[5,2,48,128]{3,2,1,0:T(8,128)S(1)}, f32[5,2,48,128]{3,2,1,0:T(8,128)S(1)}, u32[]{:S(2)}, u32[]{:S(2)}) collective-permute-start(f32[5,2,48,128]{3,2,1,0:T(8,128)S(1)} %get-tuple-element.36), channel_id=1, source_target_pairs={{0,4},{4,8},{8,12},{12,16},{16,20},{20,24},{24,28},{1,5},{5,9},{9,... | collective-permute-start | bytes 737288 | tf_op jit(solution)/shard_map/ppermute | solution.py:220
  9.4 26.6 %collective-permute-start.9 = (f32[5,2,48,128]{3,2,1,0:T(8,128)S(1)}, f32[5,2,48,128]{3,2,1,0:T(8,128)S(1)}, u32[]{:S(2)}, u32[]{:S(2)}) collective-permute-start(f32[5,2,48,128]{3,2,1,0:T(8,128)S(1)} %get-tuple-element.37), channel_id=1, source_target_pairs={{4,0},{8,4},{12,8},{16,12},{20,16},{24,20},{28,24},{5,1},{9,5},{13... | collective-permute-start | bytes 737288 | tf_op jit(solution)/shard_map/ppermute | solution.py:221
  13.8 29.8 %collective-permute-start = (f32[5,2,48,128]{3,2,1,0:T(8,128)S(1)}, f32[5,2,48,128]{3,2,1,0:T(8,128)S(1)}, u32[]{:S(2)}, u32[]{:S(2)}) collective-permute-start(f32[5,2,48,128]{3,2,1,0:T(8,128)S(1)} %get-tuple-element.26), channel_id=1, source_target_pairs={{0,4},{4,8},{8,12},{12,16},{16,20},{20,24},{24,28},{1,5},{5,9},{9,... | collective-permute-start | bytes 737288 | tf_op jit(solution)/shard_map/ppermute | solution.py:220
  16.0 27.6 %collective-permute-start.1 = (f32[5,2,48,128]{3,2,1,0:T(8,128)S(1)}, f32[5,2,48,128]{3,2,1,0:T(8,128)S(1)}, u32[]{:S(2)}, u32[]{:S(2)}) collective-permute-start(f32[5,2,48,128]{3,2,1,0:T(8,128)S(1)} %get-tuple-element.27), channel_id=1, source_target_pairs={{4,0},{8,4},{12,8},{16,12},{20,16},{24,20},{28,24},{5,1},{9,5},{13... | collective-permute-start | bytes 737288 | tf_op jit(solution)/shard_map/ppermute | solution.py:221
  19.9 5.7 %collective-permute-start.10 = (f32[40,128]{1,0:T(8,128)S(1)}, f32[40,128]{1,0:T(8,128)S(1)}, u32[]{:S(2)}, u32[]{:S(2)}) collective-permute-start(f32[40,128]{1,0:T(8,128)S(1)} %get-tuple-element.38), channel_id=1, source_target_pairs={{0,1},{1,2},{2,3},{4,5},{5,6},{6,7},{8,9},{9,10},{10,11},{12,13},{... | collective-permute-start | bytes 61448 | tf_op jit(solution)/shard_map/ppermute | solution.py:222
  25.7 6.0 %collective-permute-start.11 = (f32[40,128]{1,0:T(8,128)S(1)}, f32[40,128]{1,0:T(8,128)S(1)}, u32[]{:S(2)}, u32[]{:S(2)}) collective-permute-start(f32[40,128]{1,0:T(8,128)S(1)} %get-tuple-element.39), channel_id=1, source_target_pairs={{1,0},{2,1},{3,2},{5,4},{6,5},{7,6},{9,8},{10,9},{11,10},{13,12},{... | collective-permute-start | bytes 61448 | tf_op jit(solution)/shard_map/ppermute | solution.py:223
  31.6 7.7 %collective-permute-start.2 = (f32[40,128]{1,0:T(8,128)S(1)}, f32[40,128]{1,0:T(8,128)S(1)}, u32[]{:S(2)}, u32[]{:S(2)}) collective-permute-start(f32[40,128]{1,0:T(8,128)S(1)} %get-tuple-element.28), channel_id=1, source_target_pairs={{0,1},{1,2},{2,3},{4,5},{5,6},{6,7},{8,9},{9,10},{10,11},{12,13},{... | collective-permute-start | bytes 61448 | tf_op jit(solution)/shard_map/ppermute | solution.py:222
  33.5 10.0 %collective-permute-start.3 = (f32[40,128]{1,0:T(8,128)S(1)}, f32[40,128]{1,0:T(8,128)S(1)}, u32[]{:S(2)}, u32[]{:S(2)}) collective-permute-start(f32[40,128]{1,0:T(8,128)S(1)} %get-tuple-element.29), channel_id=1, source_target_pairs={{1,0},{2,1},{3,2},{5,4},{6,5},{7,6},{9,8},{10,9},{11,10},{13,12},{... | collective-permute-start | bytes 61448 | tf_op jit(solution)/shard_map/ppermute | solution.py:223
  37.4 33.4 %collective-permute-start.12 = (f32[5,2,48,128]{3,2,1,0:T(8,128)S(1)}, f32[5,2,48,128]{3,2,1,0:T(8,128)S(1)}, u32[]{:S(2)}, u32[]{:S(2)}) collective-permute-start(f32[5,2,48,128]{3,2,1,0:T(8,128)S(1)} %get-tuple-element.41), channel_id=1, source_target_pairs={{0,4},{4,8},{8,12},{12,16},{16,20},{20,24},{24,28},{1,5},{5,9},{9,... | collective-permute-start | bytes 737288 | tf_op jit(solution)/shard_map/ppermute | solution.py:220
  39.3 31.5 %collective-permute-start.13 = (f32[5,2,48,128]{3,2,1,0:T(8,128)S(1)}, f32[5,2,48,128]{3,2,1,0:T(8,128)S(1)}, u32[]{:S(2)}, u32[]{:S(2)}) collective-permute-start(f32[5,2,48,128]{3,2,1,0:T(8,128)S(1)} %get-tuple-element.42), channel_id=1, source_target_pairs={{4,0},{8,4},{12,8},{16,12},{20,16},{24,20},{28,24},{5,1},{9,5},{13... | collective-permute-start | bytes 737288 | tf_op jit(solution)/shard_map/ppermute | solution.py:221
  45.0 25.8 %collective-permute-start.4 = (f32[5,2,48,128]{3,2,1,0:T(8,128)S(1)}, f32[5,2,48,128]{3,2,1,0:T(8,128)S(1)}, u32[]{:S(2)}, u32[]{:S(2)}) collective-permute-start(f32[5,2,48,128]{3,2,1,0:T(8,128)S(1)} %get-tuple-element.31), channel_id=1, source_target_pairs={{0,4},{4,8},{8,12},{12,16},{16,20},{20,24},{24,28},{1,5},{5,9},{9,... | collective-permute-start | bytes 737288 | tf_op jit(solution)/shard_map/ppermute | solution.py:220
  47.1 23.7 %collective-permute-start.5 = (f32[5,2,48,128]{3,2,1,0:T(8,128)S(1)}, f32[5,2,48,128]{3,2,1,0:T(8,128)S(1)}, u32[]{:S(2)}, u32[]{:S(2)}) collective-permute-start(f32[5,2,48,128]{3,2,1,0:T(8,128)S(1)} %get-tuple-element.32), channel_id=1, source_target_pairs={{4,0},{8,4},{12,8},{16,12},{20,16},{24,20},{28,24},{5,1},{9,5},{13... | collective-permute-start | bytes 737288 | tf_op jit(solution)/shard_map/ppermute | solution.py:221
  51.2 5.2 %collective-permute-start.14 = (f32[40,128]{1,0:T(8,128)S(1)}, f32[40,128]{1,0:T(8,128)S(1)}, u32[]{:S(2)}, u32[]{:S(2)}) collective-permute-start(f32[40,128]{1,0:T(8,128)S(1)} %get-tuple-element.43), channel_id=1, source_target_pairs={{0,1},{1,2},{2,3},{4,5},{5,6},{6,7},{8,9},{9,10},{10,11},{12,13},{... | collective-permute-start | bytes 61448 | tf_op jit(solution)/shard_map/ppermute | solution.py:222
  56.4 6.0 %collective-permute-start.15 = (f32[40,128]{1,0:T(8,128)S(1)}, f32[40,128]{1,0:T(8,128)S(1)}, u32[]{:S(2)}, u32[]{:S(2)}) collective-permute-start(f32[40,128]{1,0:T(8,128)S(1)} %get-tuple-element.44), channel_id=1, source_target_pairs={{1,0},{2,1},{3,2},{5,4},{6,5},{7,6},{9,8},{10,9},{11,10},{13,12},{... | collective-permute-start | bytes 61448 | tf_op jit(solution)/shard_map/ppermute | solution.py:223
  62.3 3.1 %collective-permute-start.6 = (f32[40,128]{1,0:T(8,128)S(1)}, f32[40,128]{1,0:T(8,128)S(1)}, u32[]{:S(2)}, u32[]{:S(2)}) collective-permute-start(f32[40,128]{1,0:T(8,128)S(1)} %get-tuple-element.33), channel_id=1, source_target_pairs={{0,1},{1,2},{2,3},{4,5},{5,6},{6,7},{8,9},{9,10},{10,11},{12,13},{... | collective-permute-start | bytes 61448 | tf_op jit(solution)/shard_map/ppermute | solution.py:222
  65.4 5.4 %collective-permute-start.7 = (f32[40,128]{1,0:T(8,128)S(1)}, f32[40,128]{1,0:T(8,128)S(1)}, u32[]{:S(2)}, u32[]{:S(2)}) collective-permute-start(f32[40,128]{1,0:T(8,128)S(1)} %get-tuple-element.34), channel_id=1, source_target_pairs={{1,0},{2,1},{3,2},{5,4},{6,5},{7,6},{9,8},{10,9},{11,10},{13,12},{... | collective-permute-start | bytes 61448 | tf_op jit(solution)/shard_map/ppermute | solution.py:223

commit v2 on v1

v2 whole, which is shorter than its diff:
```python
import functools

import jax
import jax.numpy as jnp
import ml_dtypes
import numpy as np
from jax import lax
from jax.experimental import pallas as pl
from jax.experimental.pallas import tpu as pltpu
from jax.sharding import PartitionSpec as P

gamma_ratio = 1.4
viscosity = 0.1
time_step = 0.3

A1 = 8.0 / 12.0
A2 = 1.0 / 12.0
B1 = viscosity * 16.0 / 12.0
B2 = viscosity / 12.0
CENTRE = -2.0 * viscosity * 30.0 / 12.0
PAD = 8


def theta_table(azimuth):
    spacing = 2.0 * np.pi / azimuth
    index = np.arange(azimuth)
    offset = index[:, None] - index[None, :]
    signs = np.where(offset % 2 == 0, 1.0, -1.0)
    angle = offset * (spacing / 2.0)
    diagonal = offset == 0
    tangent = np.where(diagonal, 1.0, np.tan(angle))
    sine = np.where(diagonal, 1.0, np.sin(angle))
    first = np.where(diagonal, 0.0, 0.5 * signs * spacing / tangent)
    second = np.where(
        diagonal, -(np.pi**2) / 3.0 - spacing**2 / 6.0, -0.5 * signs * spacing**2 / (sine * sine)
    )
    table = np.concatenate([first.T, viscosity * second.T], axis=0).astype(np.float32)
    high = table.astype(ml_dtypes.bfloat16)
    low = (table - high.astype(np.float32)).astype(ml_dtypes.bfloat16)
    return np.concatenate([high, low], axis=1)


def section(dt, parity, get, start, steady, out_ref, xp_ref, xd_ref, put_edges, wp, fr, fx, xh, xl, ys):
    rho_ref, vel_ref, inv_ref, pg_ref, fac_ref, tab_ref = steady
    cells, rows, width = rho_ref.shape
    step = 16
    zeros = jnp.zeros((PAD, width), jnp.float32)
    for f in range(5):
        for c in range(cells):
            for buf in (wp, fr):
                buf[f, c, 0:PAD] = zeros
                buf[f, c, PAD + rows : 2 * PAD + rows] = zeros
    for c in range(cells):
        for r in range(0, rows, step):
            at = slice(r, r + step)
            rho, inv, pg, fac = rho_ref[c, at], inv_ref[c, at], pg_ref[c, at], fac_ref[at]
            w = [get(f, c, r, step) for f in range(5)]
            q = rho * w[0] + pg * w[4]
            for d in range(3):
                speed = vel_ref[d, c, at]
                for f in range(5):
                    flow = speed * w[f]
                    if f == 1 + d:
                        flow = flow + q
                    elif f == 4:
                        flow = flow + w[1 + d] * inv
                    if d == 0:
                        fx[f, c, at] = flow
                    elif d == 1:
                        fr[f, c, PAD + r : PAD + r + step] = flow
                    else:
                        flow = flow * fac
                        high = flow.astype(jnp.bfloat16)
                        k = (f * cells + c) * rows + r
                        xh[k : k + step, 0:width] = high
                        xl[k : k + step, 0:width] = (flow - high.astype(jnp.float32)).astype(jnp.bfloat16)
            for f in range(5):
                wp[f, c, PAD + r : PAD + r + step] = w[f]
                high = w[f].astype(jnp.bfloat16)
                k = (f * cells + c) * rows + r
                xh[k : k + step, width : 2 * width] = high
                xl[k : k + step, width : 2 * width] = (w[f] - high.astype(jnp.float32)).astype(jnp.bfloat16)

    def radial(f, c, r, n):
        base = PAD + r
        sh = lambda buf, k: buf[f, c, base + k : base + k + n]
        return (
            A1 * (sh(fr, 1) - sh(fr, -1))
            - A2 * (sh(fr, 2) - sh(fr, -2))
            + B1 * (sh(wp, 1) + sh(wp, -1))
            - B2 * (sh(wp, 2) + sh(wp, -2))
        )

    for f in range(5):
        k = f * cells * rows
        span = cells * rows
        both = jnp.dot(xh[k : k + span], tab_ref[...], preferred_element_type=jnp.float32)
        low = jnp.dot(xl[k : k + span], tab_ref[:, 0:width], preferred_element_type=jnp.float32)
        ys[...] = (both[:, 0:width] + both[:, width:]) + low
        for r in range(0, rows, PAD):
            at = slice(r, r + PAD)
            ws = [wp[f, c, PAD + r : 2 * PAD + r] for c in range(cells)]
            fs = [fx[f, c, at] for c in range(cells)]

            def stream(i):
                total = None
                for k, a, b in ((1, A1, B1), (-1, -A1, B1), (2, -A2, -B2), (-2, A2, -B2)):
                    if 0 <= i + k < cells:
                        term = a * fs[i + k] + b * ws[i + k]
                        total = term if total is None else total + term
                return total

            for j in range(2):
                low_face = dt * stream(j - 2)
                high_face = dt * stream(cells + j)
                xp_ref[f, j, at] = jnp.where(parity == 0, high_face, low_face)
                xd_ref[f, j, at] = jnp.where(parity == 0, low_face, high_face)
            for c in range(cells):
                total = stream(c) + radial(f, c, r, PAD) + CENTRE * ws[c] + ys[c * rows + r : c * rows + r + PAD]
                out_ref[f, c, at] = start(f, c, r, PAD) + dt * total
        for c in range(cells):
            put_edges(f, c, dt * radial(f, c, -2, 2), dt * radial(f, c, rows, 2))


def edge_writer(v, cells, parity, rp_ref, rd_ref):
    def put(f, c, low_edge, high_edge):
        k = 2 * ((5 * v + f) * cells + c)
        rp_ref[k : k + 2] = jnp.where(parity == 0, high_edge, low_edge)
        rd_ref[k : k + 2] = jnp.where(parity == 0, low_edge, high_edge)

    return put


def first_kernel(half, total_rows, w_hbm, rho_hbm, vel_hbm, pr_hbm, tab_hbm,
                 part_ref, xp_ref, xd_ref, rp_ref, rd_ref,
                 w_ref, rho_ref, vel_ref, inv_ref, pg_ref, fac_ref, tab_ref,
                 wp, fr, fx, xh, xl, ys, sems):
    cells, rows, width = rho_ref.shape
    pairs = [
        (w_hbm.at[0], w_ref.at[0]), (rho_hbm, rho_ref), (pr_hbm, pg_ref), (vel_hbm, vel_ref),
        (tab_hbm, tab_ref), (w_hbm.at[1], w_ref.at[1]),
    ]
    copies = [pltpu.make_async_copy(a, b, sems.at[i]) for i, (a, b) in enumerate(pairs)]
    for copy in copies:
        copy.start()
    index = lax.axis_index("row") * rows + lax.broadcasted_iota(jnp.int32, (rows, width), 0)
    fac_ref[...] = 1.0 / (1.0 + (index.astype(jnp.float32) + 0.5) / total_rows)
    for copy in copies[:-1]:
        copy.wait()
    inv_ref[...] = 1.0 / rho_ref[...]
    pg_ref[...] = gamma_ratio * pg_ref[...]
    get = lambda f, c, r, n: w_ref[0, f, c, r : r + n]
    put = edge_writer(0, cells, lax.axis_index("row") % 2, rp_ref, rd_ref)
    steady = (rho_ref, vel_ref, inv_ref, pg_ref, fac_ref, tab_ref)
    section(0.5 * time_step, lax.axis_index("gx") % 2, get, get, steady, part_ref, xp_ref, xd_ref, put,
            wp, fr, fx, xh, xl, ys)
    copies[-1].wait()


def next_kernel(w_ref, rp0_ref, rd0_ref, rho_ref, vel_ref, inv_ref, pg_ref, fac_ref, tab_ref,
                part_ref, xp_ref, xd_ref, rp_ref, rd_ref, *scratch):
    cells, rows, width = rho_ref.shape
    half = 10 * cells
    rp_ref[0:half] = rp0_ref[...]
    rd_ref[0:half] = rd0_ref[...]
    get = lambda f, c, r, n: w_ref[1, f, c, r : r + n]
    put = edge_writer(1, cells, lax.axis_index("row") % 2, rp_ref, rd_ref)
    steady = (rho_ref, vel_ref, inv_ref, pg_ref, fac_ref, tab_ref)
    section(0.5 * time_step, lax.axis_index("gx") % 2, get, get, steady, part_ref, xp_ref, xd_ref, put, *scratch)


def add_faces(v, part_ref, xp_ref, xd_ref, rp_ref, rd_ref, out):
    _, cells, rows, _ = part_ref.shape
    column = lax.axis_index("gx") % 2
    line = lax.axis_index("row") % 2
    for f in range(5):
        for c in range(cells):
            out[f, c] = part_ref[f, c]
    for f in range(5):
        for j in range(2):
            out[f, (cells - 2) * (1 - column) + j] += xp_ref[f, j]
            out[f, (cells - 2) * column + j] += xd_ref[f, j]
    for f in range(5):
        for c in range(cells):
            k = 2 * ((5 * v + f) * cells + c)
            rp, rd = rp_ref[k : k + 2], rd_ref[k : k + 2]
            out[f, c, 0:2] += jnp.where(line == 0, rd, rp)
            out[f, c, rows - 2 : rows] += jnp.where(line == 0, rp, rd)


def second_kernel(v, *refs):
    w_ref, part_ref, xp_in, xd_in, rp_in, rd_in = refs[:6]
    refs = refs[6:]
    if v == 1:
        rp0_ref, rd0_ref, *refs = refs
    rho_ref, vel_ref, inv_ref, pg_ref, fac_ref, tab_ref, out_ref, xp_ref, xd_ref, rp_ref, rd_ref, *scratch, s1 = refs
    cells, rows, width = rho_ref.shape
    if v == 1:
        half = 10 * cells
        rp_ref[0:half] = rp0_ref[...]
        rd_ref[0:half] = rd0_ref[...]
    add_faces(v, part_ref, xp_in, xd_in, rp_in, rd_in, s1)
    get = lambda f, c, r, n: s1[f, c, r : r + n]
    start = lambda f, c, r, n: w_ref[v, f, c, r : r + n]
    put = edge_writer(v, cells, lax.axis_index("row") % 2, rp_ref, rd_ref)
    steady = (rho_ref, vel_ref, inv_ref, pg_ref, fac_ref, tab_ref)
    section(time_step, lax.axis_index("gx") % 2, get, start, steady, out_ref, xp_ref, xd_ref, put, *scratch)


def third_kernel(v, part_ref, xp_ref, xd_ref, rp_ref, rd_ref, *refs):
    out_hbm, value, sem = refs[-3:]
    add_faces(v, part_ref, xp_ref, xd_ref, rp_ref, rd_ref, value)
    copy = pltpu.make_async_copy(value, out_hbm.at[v], sem)
    copy.start()
    copy.wait()


VM = pl.BlockSpec(memory_space=pltpu.VMEM)
HB = pl.BlockSpec(memory_space=pltpu.HBM)
PARAMS = pltpu.CompilerParams(vmem_limit_bytes=40 << 20)


def local(adjoint_vectors, base_density, base_velocity, base_pressure):
    _, _, cells, rows, width = adjoint_vectors.shape
    f32 = jnp.float32
    shape = lambda *s: jax.ShapeDtypeStruct(s, f32)
    total_rows = lax.axis_size("row") * rows
    tab = jnp.asarray(theta_table(width))
    edge = 10 * cells
    part = [shape(5, cells, rows, width), shape(5, 2, rows, width), shape(5, 2, rows, width)]
    outs = lambda n: part + [shape(n * edge, width), shape(n * edge, width)]
    scratch = [
        pltpu.VMEM((5, cells, rows + 2 * PAD, width), f32),
        pltpu.VMEM((5, cells, rows + 2 * PAD, width), f32),
        pltpu.VMEM((5, cells, rows, width), f32),
        pltpu.VMEM((5 * cells * rows, 2 * width), jnp.bfloat16),
        pltpu.VMEM((5 * cells * rows, 2 * width), jnp.bfloat16),
        pltpu.VMEM((cells * rows, width), f32),
    ]

    def swap(value, axis, first):
        size = lax.axis_size(axis)
        pairs = [(i, i + 1) for i in range(0 if first else 1, size - 1, 2)]
        return lax.ppermute(value, axis, pairs + [(j, i) for i, j in pairs])

    *one, w, rho, vel, inv, pg, fac, table = pl.pallas_call(
        functools.partial(first_kernel, edge, total_rows), name="one_0",
        out_shape=outs(1) + [
            shape(2, 5, cells, rows, width), shape(cells, rows, width), shape(3, cells, rows, width),
            shape(cells, rows, width), shape(cells, rows, width), shape(rows, width),
            jax.ShapeDtypeStruct(tab.shape, tab.dtype),
        ],
        in_specs=[HB] * 5, out_specs=[VM] * 12, scratch_shapes=scratch + [pltpu.SemaphoreType.DMA((6,))],
        compiler_params=PARAMS,
    )(*(pltpu.with_memory_space_constraint(a, pltpu.HBM)
        for a in (adjoint_vectors, base_density, base_velocity, base_pressure, tab)))
    steady = (rho, vel, inv, pg, fac, table)
    parts = [None, None]
    parts[0], xp, xd, rp, rd = one
    faces = [(swap(xp, "gx", True), swap(xd, "gx", False)), None]
    parts[1], xp, xd, rp, rd = pl.pallas_call(
        next_kernel, name="one_1", out_shape=outs(2), in_specs=[VM] * 9, out_specs=[VM] * 5,
        scratch_shapes=scratch, compiler_params=PARAMS,
    )(w, rp, rd, *steady)
    faces[1] = (swap(xp, "gx", True), swap(xd, "gx", False))
    edges = (swap(rp, "row", True), swap(rd, "row", False))
    more = ()
    for v in range(2):
        parts[v], xp, xd, rp, rd = pl.pallas_call(
            functools.partial(second_kernel, v), name=f"two_{v}", out_shape=outs(1 + v),
            in_specs=[VM] * (12 + 2 * v), out_specs=[VM] * 5,
            scratch_shapes=scratch + [pltpu.VMEM((5, cells, rows, width), f32)], compiler_params=PARAMS,
        )(w, parts[v], *faces[v], *edges, *more, *steady)
        faces[v] = (swap(xp, "gx", True), swap(xd, "gx", False))
        more = (rp, rd)
    edges = (swap(rp, "row", True), swap(rd, "row", False))
    out = ()
    for v in range(2):
        out = (pl.pallas_call(
            functools.partial(third_kernel, v), name=f"three_{v}",
            out_shape=shape(*adjoint_vectors.shape), in_specs=[VM] * 5 + [HB] * v, out_specs=HB,
            scratch_shapes=[pltpu.VMEM((5, cells, rows, width), f32), pltpu.SemaphoreType.DMA],
            input_output_aliases={5: 0} if v else {}, compiler_params=PARAMS,
        )(parts[v], *faces[v], *edges, *out),)
    return out[0]


def solution(mesh):
    in_specs = (
        P(None, None, "gx", "row", None),
        P("gx", "row", None),
        P(None, "gx", "row", None),
        P("gx", "row", None),
    )
    out_specs = P(None, None, "gx", "row", None)
    return jax.shard_map(local, mesh=mesh, in_specs=in_specs, out_specs=out_specs, check_vma=False)
```

time: 72.6 us -> 48.9 us (0.67)
  the two profiles are of different devices: /device:TPU:17 before, /device:TPU:0 now
where the time goes in v2:
time: 48.9 us; the launch traced here: 48.6 us
  waiting for transfers between devices  21.5 us (44%)
  starting transfers between devices  18.1 us (37%)
  Pallas kernels  8.88 us (18%)
    ppermute x12, waiting for transfers between devices, swap(): return lax.ppermute(value, axis, pairs + [(j, i) for i, j in pairs])  21.5 us
    ppermute x12, starting transfers between devices, swap(): return lax.ppermute(value, axis, pairs + [(j, i) for i, j in pairs])  18.1 us
    pallas_call x2, Pallas kernels, local(): pl.pallas_call(functools.partial(second_kernel, v), name=f'two_{v}', out_...  3.1 us
    pallas_call x1, Pallas kernels, local(): pl.pallas_call(functools.partial(first_kernel, edge, total_rows), name='o...  2.63 us
    pallas_call x2, Pallas kernels, local(): pl.pallas_call(functools.partial(third_kernel, v), name=f'three_{v}', out...  1.83 us
    pallas_call x1, Pallas kernels, local(): pl.pallas_call(next_kernel, name='one_1', out_shape=outs(2), in_specs=[VM...  1.32 us
  transfers between devices with their start and end apart: 12, of which 6 were waited for; matrix products, arithmetic and copies ran while one was open for 0% of the time, Pallas kernels for 11%

profile of v2, /device:TPU:0, one launch (start us, length us, event | category | flops | bytes accessed | tf_op | source)
XLA Modules:
  0.0 48.6 jit_solution(12241032277688641381)
XLA Ops:
  0.0 2.6 %one_0.1 = (f32[5,4,48,128]{3,2,1,0:T(8,128)S(1)}, f32[5,2,48,128]{3,2,1,0:T(8,128)S(1)}, f32[5,2,48,128]{3,2,1,0:T(8,128)S(1)}, f32[40,128]{1,0:T(8,128)S(1)}, ...) custom-call(f32[2,5,4,48,128]{4,3,2,1,0:T(8,128)} %w_hbm.1, ...), custom_call_target="tpu_custom_call" | custom-call | tf_op jit(solution)/shard_map/one_0/pallas_call | solution.py:246
  2.6 3.0 %collective-permute-start.4 = (f32[5,2,48,128]{3,2,1,0:T(8,128)S(1)}, f32[5,2,48,128]{3,2,1,0:T(8,128)S(1)}, u32[]{:S(2)}, u32[]{:S(2)}) collective-permute-start(f32[5,2,48,128]{3,2,1,0:T(8,128)S(1)} %get-tuple-element.47), channel_id=1, source_target_pairs={{0,4},{8,12},{16,20},{24,28},{4,0},{12,8},{20,16},{28,24},{1,5},{9... | collective-permute-start | bytes 737288 | tf_op jit(solution)/shard_map/ppermute | solution.py:244
  5.6 0.7 %collective-permute-start.5 = (f32[5,2,48,128]{3,2,1,0:T(8,128)S(1)}, f32[5,2,48,128]{3,2,1,0:T(8,128)S(1)}, u32[]{:S(2)}, u32[]{:S(2)}) collective-permute-start(f32[5,2,48,128]{3,2,1,0:T(8,128)S(1)} %get-tuple-element.48), channel_id=1, source_target_pairs={{4,8},{12,16},{20,24},{8,4},{16,12},{24,20},{5,9},{13,17},{21,25},... | collective-permute-start | bytes 737288 | tf_op jit(solution)/shard_map/ppermute | solution.py:244
  6.3 1.3 %one_1.1 = (f32[5,4,48,128]{3,2,1,0:T(8,128)S(1)}, f32[5,2,48,128]{3,2,1,0:T(8,128)S(1)}, f32[5,2,48,128]{3,2,1,0:T(8,128)S(1)}, f32[80,128]{1,0:T(8,128)S(1)}, f32[80,128]{1,0:T(8,128)S(1)}) custom-call(f32[2,5,4,48,128]{4,3,2,1,0:T(8,128)S(1)} %get-tuple-element.32.w_ref.refs_0_, f32[40,128]{1,0:T(8,128)S(1)} %get-tuple-element.33.rp0_ref, ...), custom_call_target="tpu_custom_call" | custom-call | tf_op jit(solution)/shard_map/one_1/pallas_call | solution.py:261
  7.6 4.3 %collective-permute-start = (f32[5,2,48,128]{3,2,1,0:T(8,128)S(1)}, f32[5,2,48,128]{3,2,1,0:T(8,128)S(1)}, u32[]{:S(2)}, u32[]{:S(2)}) collective-permute-start(f32[5,2,48,128]{3,2,1,0:T(8,128)S(1)} %get-tuple-element.42), channel_id=1, source_target_pairs={{0,4},{8,12},{16,20},{24,28},{4,0},{12,8},{20,16},{28,24},{1,5},{9... | collective-permute-start | bytes 737288 | tf_op jit(solution)/shard_map/ppermute | solution.py:244
  12.0 0.7 %collective-permute-start.1 = (f32[5,2,48,128]{3,2,1,0:T(8,128)S(1)}, f32[5,2,48,128]{3,2,1,0:T(8,128)S(1)}, u32[]{:S(2)}, u32[]{:S(2)}) collective-permute-start(f32[5,2,48,128]{3,2,1,0:T(8,128)S(1)} %get-tuple-element.43), channel_id=1, source_target_pairs={{4,8},{12,16},{20,24},{8,4},{16,12},{24,20},{5,9},{13,17},{21,25},... | collective-permute-start | bytes 737288 | tf_op jit(solution)/shard_map/ppermute | solution.py:244
  12.7 0.1 collective-permute-start.2
  12.7 1.2 %collective-permute-done.2.refs_4_ = f32[80,128]{1,0:T(8,128)S(1)} collective-permute-done((f32[80,128]{1,0:T(8,128)S(1)}, f32[80,128]{1,0:T(8,128)S(1)}, u32[]{:S(2)}, u32[]{:S(2)}) %collective-permute-start.2) | collective-permute-done | bytes 40992 | tf_op jit(solution)/shard_map/ppermute | solution.py:244
  13.9 0.7 %collective-permute-start.3 = (f32[80,128]{1,0:T(8,128)S(1)}, f32[80,128]{1,0:T(8,128)S(1)}, u32[]{:S(2)}, u32[]{:S(2)}) collective-permute-start(f32[80,128]{1,0:T(8,128)S(1)} %get-tuple-element.45), channel_id=1, source_target_pairs={{1,2},{2,1},{5,6},{6,5},{9,10},{10,9},{13,14},{14,13},{17,18},{18,... | collective-permute-start | bytes 122888 | tf_op jit(solution)/shard_map/ppermute | solution.py:244
  14.6 0.0 collective-permute-done.3.refs_5_
  14.6 7.9 %collective-permute-done.4.refs_2_ = f32[5,2,48,128]{3,2,1,0:T(8,128)S(1)} collective-permute-done((f32[5,2,48,128]{3,2,1,0:T(8,128)S(1)}, f32[5,2,48,128]{3,2,1,0:T(8,128)S(1)}, u32[]{:S(2)}, u32[]{:S(2)}) %collective-permute-start.4) | collective-permute-done | bytes 245792 | tf_op jit(solution)/shard_map/ppermute | solution.py:244
  22.5 0.0 collective-permute-done.5.refs_3_
  22.5 1.5 %two_0.1 = (f32[5,4,48,128]{3,2,1,0:T(8,128)S(1)}, f32[5,2,48,128]{3,2,1,0:T(8,128)S(1)}, f32[5,2,48,128]{3,2,1,0:T(8,128)S(1)}, f32[40,128]{1,0:T(8,128)S(1)}, f32[40,128]{1,0:T(8,128)S(1)}) custom-call(f32[2,5,4,48,128]{4,3,2,1,0:T(8,128)S(1)} %get-tuple-element.32.w_ref.refs_0_, f32[5,4,48,128]{3,2,1,0:T(8,128)S(1)} %get-tuple-element.46.refs_1_, ...), custom_call_target="tpu_custom_call" | custom-call | tf_op jit(solution)/shard_map/two_0/pallas_call | solution.py:269
  24.1 2.5 %collective-permute-start.10 = (f32[5,2,48,128]{3,2,1,0:T(8,128)S(1)}, f32[5,2,48,128]{3,2,1,0:T(8,128)S(1)}, u32[]{:S(2)}, u32[]{:S(2)}) collective-permute-start(f32[5,2,48,128]{3,2,1,0:T(8,128)S(1)} %get-tuple-element.57), channel_id=1, source_target_pairs={{0,4},{8,12},{16,20},{24,28},{4,0},{12,8},{20,16},{28,24},{1,5},{9... | collective-permute-start | bytes 737288 | tf_op jit(solution)/shard_map/ppermute | solution.py:244
  26.6 0.7 %collective-permute-start.11 = (f32[5,2,48,128]{3,2,1,0:T(8,128)S(1)}, f32[5,2,48,128]{3,2,1,0:T(8,128)S(1)}, u32[]{:S(2)}, u32[]{:S(2)}) collective-permute-start(f32[5,2,48,128]{3,2,1,0:T(8,128)S(1)} %get-tuple-element.58), channel_id=1, source_target_pairs={{4,8},{12,16},{20,24},{8,4},{16,12},{24,20},{5,9},{13,17},{21,25},... | collective-permute-start | bytes 737288 | tf_op jit(solution)/shard_map/ppermute | solution.py:244
  27.3 0.2 collective-permute-done.refs_2_
  27.5 0.0 collective-permute-done.1.refs_3_
  27.5 1.6 %two_1.1 = (f32[5,4,48,128]{3,2,1,0:T(8,128)S(1)}, f32[5,2,48,128]{3,2,1,0:T(8,128)S(1)}, f32[5,2,48,128]{3,2,1,0:T(8,128)S(1)}, f32[80,128]{1,0:T(8,128)S(1)}, f32[80,128]{1,0:T(8,128)S(1)}) custom-call(f32[2,5,4,48,128]{4,3,2,1,0:T(8,128)S(1)} %get-tuple-element.32.w_ref.refs_0_, f32[5,4,48,128]{3,2,1,0:T(8,128)S(1)} %get-tuple-element.41.refs_1_, ...), custom_call_target="tpu_custom_call" | custom-call | tf_op jit(solution)/shard_map/two_1/pallas_call | solution.py:269
  29.1 4.1 %collective-permute-start.6 = (f32[5,2,48,128]{3,2,1,0:T(8,128)S(1)}, f32[5,2,48,128]{3,2,1,0:T(8,128)S(1)}, u32[]{:S(2)}, u32[]{:S(2)}) collective-permute-start(f32[5,2,48,128]{3,2,1,0:T(8,128)S(1)} %get-tuple-element.52), channel_id=1, source_target_pairs={{0,4},{8,12},{16,20},{24,28},{4,0},{12,8},{20,16},{28,24},{1,5},{9... | collective-permute-start | bytes 737288 | tf_op jit(solution)/shard_map/ppermute | solution.py:244
  33.2 0.7 %collective-permute-start.7 = (f32[5,2,48,128]{3,2,1,0:T(8,128)S(1)}, f32[5,2,48,128]{3,2,1,0:T(8,128)S(1)}, u32[]{:S(2)}, u32[]{:S(2)}) collective-permute-start(f32[5,2,48,128]{3,2,1,0:T(8,128)S(1)} %get-tuple-element.53), channel_id=1, source_target_pairs={{4,8},{12,16},{20,24},{8,4},{16,12},{24,20},{5,9},{13,17},{21,25},... | collective-permute-start | bytes 737288 | tf_op jit(solution)/shard_map/ppermute | solution.py:244
  33.9 0.1 collective-permute-start.8
  34.0 1.2 %collective-permute-done.8.rp_ref = f32[80,128]{1,0:T(8,128)S(1)} collective-permute-done((f32[80,128]{1,0:T(8,128)S(1)}, f32[80,128]{1,0:T(8,128)S(1)}, u32[]{:S(2)}, u32[]{:S(2)}) %collective-permute-start.8) | collective-permute-done | bytes 40992 | tf_op jit(solution)/shard_map/ppermute | solution.py:244
  35.2 0.7 %collective-permute-start.9 = (f32[80,128]{1,0:T(8,128)S(1)}, f32[80,128]{1,0:T(8,128)S(1)}, u32[]{:S(2)}, u32[]{:S(2)}) collective-permute-start(f32[80,128]{1,0:T(8,128)S(1)} %get-tuple-element.55), channel_id=1, source_target_pairs={{1,2},{2,1},{5,6},{6,5},{9,10},{10,9},{13,14},{14,13},{17,18},{18,... | collective-permute-start | bytes 122888 | tf_op jit(solution)/shard_map/ppermute | solution.py:244
  35.9 0.0 collective-permute-done.9.rd_ref
  35.9 7.7 %collective-permute-done.10.xp_ref = f32[5,2,48,128]{3,2,1,0:T(8,128)S(1)} collective-permute-done((f32[5,2,48,128]{3,2,1,0:T(8,128)S(1)}, f32[5,2,48,128]{3,2,1,0:T(8,128)S(1)}, u32[]{:S(2)}, u32[]{:S(2)}) %collective-permute-start.10) | collective-permute-done | bytes 245792 | tf_op jit(solution)/shard_map/ppermute | solution.py:244
  43.6 0.0 collective-permute-done.11.xd_ref
  43.6 0.9 %three_0.1.refs_0_ = f32[2,5,4,48,128]{4,3,2,1,0:T(8,128)} custom-call(f32[5,4,48,128]{3,2,1,0:T(8,128)S(1)} %get-tuple-element.56.part_ref, f32[5,2,48,128]{3,2,1,0:T(8,128)S(1)} %collective-permute-done.10.xp_ref, f32[5,2,48,128]{3,2,1,0:T(8,128)S(1)} %collective-permute-done.11.xd_ref, f32[80,128]{1,0:T(8,128)S(1)} %collective-permute-done.8.rp_ref, ...), custom_call_target="tpu_custom_call" | custom-call | tf_op jit(solution)/shard_map/three_0/pallas_call | solution.py:279
  44.5 3.2 %collective-permute-done.6.xp_ref = f32[5,2,48,128]{3,2,1,0:T(8,128)S(1)} collective-permute-done((f32[5,2,48,128]{3,2,1,0:T(8,128)S(1)}, f32[5,2,48,128]{3,2,1,0:T(8,128)S(1)}, u32[]{:S(2)}, u32[]{:S(2)}) %collective-permute-start.6) | collective-permute-done | bytes 245792 | tf_op jit(solution)/shard_map/ppermute | solution.py:244
  47.7 0.0 collective-permute-done.7.xd_ref
  47.7 0.9 %three_1.1 = f32[2,5,4,48,128]{4,3,2,1,0:T(8,128)} custom-call(f32[5,4,48,128]{3,2,1,0:T(8,128)S(1)} %get-tuple-element.51.part_ref, f32[5,2,48,128]{3,2,1,0:T(8,128)S(1)} %collective-permute-done.6.xp_ref, f32[5,2,48,128]{3,2,1,0:T(8,128)S(1)} %collective-permute-done.7.xd_ref, ...), custom_call_target="tpu_custom_call", output_to_operand_aliasing={{}: (5, {})} | custom-call | tf_op jit(solution)/shard_map/three_1/pallas_call | solution.py:279
Async XLA Ops:
  2.6 19.9 %collective-permute-start.4 = (f32[5,2,48,128]{3,2,1,0:T(8,128)S(1)}, f32[5,2,48,128]{3,2,1,0:T(8,128)S(1)}, u32[]{:S(2)}, u32[]{:S(2)}) collective-permute-start(f32[5,2,48,128]{3,2,1,0:T(8,128)S(1)} %get-tuple-element.47), channel_id=1, source_target_pairs={{0,4},{8,12},{16,20},{24,28},{4,0},{12,8},{20,16},{28,24},{1,5},{9... | collective-permute-start | bytes 737288 | tf_op jit(solution)/shard_map/ppermute | solution.py:244
  5.6 16.9 %collective-permute-start.5 = (f32[5,2,48,128]{3,2,1,0:T(8,128)S(1)}, f32[5,2,48,128]{3,2,1,0:T(8,128)S(1)}, u32[]{:S(2)}, u32[]{:S(2)}) collective-permute-start(f32[5,2,48,128]{3,2,1,0:T(8,128)S(1)} %get-tuple-element.48), channel_id=1, source_target_pairs={{4,8},{12,16},{20,24},{8,4},{16,12},{24,20},{5,9},{13,17},{21,25},... | collective-permute-start | bytes 737288 | tf_op jit(solution)/shard_map/ppermute | solution.py:244
  7.6 19.9 %collective-permute-start = (f32[5,2,48,128]{3,2,1,0:T(8,128)S(1)}, f32[5,2,48,128]{3,2,1,0:T(8,128)S(1)}, u32[]{:S(2)}, u32[]{:S(2)}) collective-permute-start(f32[5,2,48,128]{3,2,1,0:T(8,128)S(1)} %get-tuple-element.42), channel_id=1, source_target_pairs={{0,4},{8,12},{16,20},{24,28},{4,0},{12,8},{20,16},{28,24},{1,5},{9... | collective-permute-start | bytes 737288 | tf_op jit(solution)/shard_map/ppermute | solution.py:244
  12.0 15.6 %collective-permute-start.1 = (f32[5,2,48,128]{3,2,1,0:T(8,128)S(1)}, f32[5,2,48,128]{3,2,1,0:T(8,128)S(1)}, u32[]{:S(2)}, u32[]{:S(2)}) collective-permute-start(f32[5,2,48,128]{3,2,1,0:T(8,128)S(1)} %get-tuple-element.43), channel_id=1, source_target_pairs={{4,8},{12,16},{20,24},{8,4},{16,12},{24,20},{5,9},{13,17},{21,25},... | collective-permute-start | bytes 737288 | tf_op jit(solution)/shard_map/ppermute | solution.py:244
  12.7 1.3 %collective-permute-start.2 = (f32[80,128]{1,0:T(8,128)S(1)}, f32[80,128]{1,0:T(8,128)S(1)}, u32[]{:S(2)}, u32[]{:S(2)}) collective-permute-start(f32[80,128]{1,0:T(8,128)S(1)} %get-tuple-element.44), channel_id=1, source_target_pairs={{0,1},{2,3},{1,0},{3,2},{4,5},{6,7},{5,4},{7,6},{8,9},{10,11},{9,8... | collective-permute-start | bytes 122888 | tf_op jit(solution)/shard_map/ppermute | solution.py:244
  13.9 0.7 %collective-permute-start.3 = (f32[80,128]{1,0:T(8,128)S(1)}, f32[80,128]{1,0:T(8,128)S(1)}, u32[]{:S(2)}, u32[]{:S(2)}) collective-permute-start(f32[80,128]{1,0:T(8,128)S(1)} %get-tuple-element.45), channel_id=1, source_target_pairs={{1,2},{2,1},{5,6},{6,5},{9,10},{10,9},{13,14},{14,13},{17,18},{18,... | collective-permute-start | bytes 122888 | tf_op jit(solution)/shard_map/ppermute | solution.py:244
  24.1 19.5 %collective-permute-start.10 = (f32[5,2,48,128]{3,2,1,0:T(8,128)S(1)}, f32[5,2,48,128]{3,2,1,0:T(8,128)S(1)}, u32[]{:S(2)}, u32[]{:S(2)}) collective-permute-start(f32[5,2,48,128]{3,2,1,0:T(8,128)S(1)} %get-tuple-element.57), channel_id=1, source_target_pairs={{0,4},{8,12},{16,20},{24,28},{4,0},{12,8},{20,16},{28,24},{1,5},{9... | collective-permute-start | bytes 737288 | tf_op jit(solution)/shard_map/ppermute | solution.py:244
  26.6 16.9 %collective-permute-start.11 = (f32[5,2,48,128]{3,2,1,0:T(8,128)S(1)}, f32[5,2,48,128]{3,2,1,0:T(8,128)S(1)}, u32[]{:S(2)}, u32[]{:S(2)}) collective-permute-start(f32[5,2,48,128]{3,2,1,0:T(8,128)S(1)} %get-tuple-element.58), channel_id=1, source_target_pairs={{4,8},{12,16},{20,24},{8,4},{16,12},{24,20},{5,9},{13,17},{21,25},... | collective-permute-start | bytes 737288 | tf_op jit(solution)/shard_map/ppermute | solution.py:244
  29.1 18.6 %collective-permute-start.6 = (f32[5,2,48,128]{3,2,1,0:T(8,128)S(1)}, f32[5,2,48,128]{3,2,1,0:T(8,128)S(1)}, u32[]{:S(2)}, u32[]{:S(2)}) collective-permute-start(f32[5,2,48,128]{3,2,1,0:T(8,128)S(1)} %get-tuple-element.52), channel_id=1, source_target_pairs={{0,4},{8,12},{16,20},{24,28},{4,0},{12,8},{20,16},{28,24},{1,5},{9... | collective-permute-start | bytes 737288 | tf_op jit(solution)/shard_map/ppermute | solution.py:244
  33.2 14.5 %collective-permute-start.7 = (f32[5,2,48,128]{3,2,1,0:T(8,128)S(1)}, f32[5,2,48,128]{3,2,1,0:T(8,128)S(1)}, u32[]{:S(2)}, u32[]{:S(2)}) collective-permute-start(f32[5,2,48,128]{3,2,1,0:T(8,128)S(1)} %get-tuple-element.53), channel_id=1, source_target_pairs={{4,8},{12,16},{20,24},{8,4},{16,12},{24,20},{5,9},{13,17},{21,25},... | collective-permute-start | bytes 737288 | tf_op jit(solution)/shard_map/ppermute | solution.py:244
  33.9 1.3 %collective-permute-start.8 = (f32[80,128]{1,0:T(8,128)S(1)}, f32[80,128]{1,0:T(8,128)S(1)}, u32[]{:S(2)}, u32[]{:S(2)}) collective-permute-start(f32[80,128]{1,0:T(8,128)S(1)} %get-tuple-element.54), channel_id=1, source_target_pairs={{0,1},{2,3},{1,0},{3,2},{4,5},{6,7},{5,4},{7,6},{8,9},{10,11},{9,8... | collective-permute-start | bytes 122888 | tf_op jit(solution)/shard_map/ppermute | solution.py:244
  35.2 0.7 %collective-permute-start.9 = (f32[80,128]{1,0:T(8,128)S(1)}, f32[80,128]{1,0:T(8,128)S(1)}, u32[]{:S(2)}, u32[]{:S(2)}) collective-permute-start(f32[80,128]{1,0:T(8,128)S(1)} %get-tuple-element.55), channel_id=1, source_target_pairs={{1,2},{2,1},{5,6},{6,5},{9,10},{10,9},{13,14},{14,13},{17,18},{18,... | collective-permute-start | bytes 122888 | tf_op jit(solution)/shard_map/ppermute | solution.py:244

commit v3 on v0

v3 whole, which is shorter than its diff:
```python
import functools

import jax
import jax.numpy as jnp
import ml_dtypes
import numpy as np
from jax import lax
from jax.experimental import pallas as pl
from jax.experimental.pallas import tpu as pltpu
from jax.sharding import PartitionSpec as P

gamma_ratio = 1.4
viscosity = 0.1
time_step = 0.3

A1 = 8.0 / 12.0
A2 = 1.0 / 12.0
B1 = viscosity * 16.0 / 12.0
B2 = viscosity / 12.0
CENTRE = -2.0 * viscosity * 30.0 / 12.0
PAD = 8


def theta_table(azimuth):
    spacing = 2.0 * np.pi / azimuth
    index = np.arange(azimuth)
    offset = index[:, None] - index[None, :]
    signs = np.where(offset % 2 == 0, 1.0, -1.0)
    angle = offset * (spacing / 2.0)
    diagonal = offset == 0
    tangent = np.where(diagonal, 1.0, np.tan(angle))
    sine = np.where(diagonal, 1.0, np.sin(angle))
    first = np.where(diagonal, 0.0, 0.5 * signs * spacing / tangent)
    second = np.where(
        diagonal, -(np.pi**2) / 3.0 - spacing**2 / 6.0, -0.5 * signs * spacing**2 / (sine * sine)
    )
    table = np.concatenate([first.T, viscosity * second.T], axis=0).astype(np.float32)
    high = table.astype(ml_dtypes.bfloat16)
    low = (table - high.astype(np.float32)).astype(ml_dtypes.bfloat16)
    return np.concatenate([high, low], axis=1)


def fluxes(base_ref, c, at, w, directions):
    rho, pr = base_ref[0, c, at], base_ref[4, c, at]
    inv = 1.0 / rho
    pg = gamma_ratio * pr
    flows = []
    for v in range(2):
        q = rho * w[v][0] + pg * w[v][4]
        rows = []
        for d in directions:
            speed = base_ref[1 + d, c, at]
            flow = [speed * w[v][f] for f in range(5)]
            flow[1 + d] = flow[1 + d] + q
            flow[4] = flow[4] + w[v][1 + d] * inv
            rows.append(flow)
        flows.append(rows)
    return flows


def radial(fr, wp, v, f, c, r, n):
    base = PAD + r
    sh = lambda buf, k: buf[v, f, c, base + k : base + k + n]
    return (
        A1 * (sh(fr, 1) - sh(fr, -1))
        - A2 * (sh(fr, 2) - sh(fr, -2))
        + B1 * (sh(wp, 1) + sh(wp, -1))
        - B2 * (sh(wp, 2) + sh(wp, -2))
    )


def clear_pads(fr, wp):
    _, _, cells, padded, width = fr.shape
    zeros = jnp.zeros((PAD, width), jnp.float32)
    for v in range(2):
        for f in range(5):
            for c in range(cells):
                for buf in (wp, fr):
                    buf[v, f, c, 0:PAD] = zeros
                    buf[v, f, c, padded - PAD : padded] = zeros


def put_edges(dt, line, fr, wp, rp_ref, rd_ref):
    _, _, cells, padded, _ = fr.shape
    for v in range(2):
        for f in range(5):
            for c in range(cells):
                low = dt * radial(fr, wp, v, f, c, -2, 2)
                high = dt * radial(fr, wp, v, f, c, padded - 2 * PAD, 2)
                k = 2 * ((5 * v + f) * cells + c)
                rp_ref[k : k + 2] = jnp.where(line == 0, high, low)
                rd_ref[k : k + 2] = jnp.where(line == 0, low, high)


def section(dt, parity, line, half, get, start, base_ref, tab_ref, put, xp_ref, xd_ref, rp_ref, rd_ref,
            wp, fr, fx, xh, xl, ys):
    _, cells, rows, width = base_ref.shape
    total_rows = 2 * rows * lax.axis_size("row")
    row_start = lax.axis_index("row") * (2 * rows) + half * rows
    span = 2 * cells * rows
    clear_pads(fr, wp)

    def split(flow, k, lanes):
        both = jnp.concatenate(flow, axis=0)
        high = both.astype(jnp.bfloat16)
        xh[k : k + 2 * PAD, lanes] = high
        xl[k : k + 2 * PAD, lanes] = (both - high.astype(jnp.float32)).astype(jnp.bfloat16)

    for r in range(0, rows, PAD):
        at = slice(r, r + PAD)
        inside = slice(PAD + r, 2 * PAD + r)
        index = row_start + r + lax.broadcasted_iota(jnp.int32, (PAD, width), 0)
        fac = 1.0 / (1.0 + (index.astype(jnp.float32) + 0.5) / total_rows)
        for c in range(cells):
            w = [[get(v, f, c, r) for f in range(5)] for v in range(2)]
            flows = fluxes(base_ref, c, at, w, (0, 1, 2))
            for f in range(5):
                k = f * span + (c * (rows // PAD) + r // PAD) * 2 * PAD
                for v in range(2):
                    fx[v, f, c, at] = flows[v][0][f]
                    fr[v, f, c, inside] = flows[v][1][f]
                    wp[v, f, c, inside] = w[v][f]
                split([flows[v][2][f] * fac for v in range(2)], k, slice(0, width))
                split([w[v][f] for v in range(2)], k, slice(width, 2 * width))
    for f in range(5):
        both = jnp.dot(xh[f * span : (f + 1) * span], tab_ref[...], preferred_element_type=jnp.float32)
        low = jnp.dot(xl[f * span : (f + 1) * span], tab_ref[:, 0:width], preferred_element_type=jnp.float32)
        ys[...] = (both[:, 0:width] + both[:, width:]) + low
        for v in range(2):
            for r in range(0, rows, PAD):
                at = slice(r, r + PAD)
                ws = [wp[v, f, c, PAD + r : 2 * PAD + r] for c in range(cells)]
                fs = [fx[v, f, c, at] for c in range(cells)]

                def stream(i):
                    total = None
                    for k, a, b in ((1, A1, B1), (-1, -A1, B1), (2, -A2, -B2), (-2, A2, -B2)):
                        if 0 <= i + k < cells:
                            term = a * fs[i + k] + b * ws[i + k]
                            total = term if total is None else total + term
                    return total

                for j in range(2):
                    low_face = dt * stream(j - 2)
                    high_face = dt * stream(cells + j)
                    xp_ref[v, f, j, at] = jnp.where(parity == 0, high_face, low_face)
                    if xd_ref is not None:
                        xd_ref[v, f, j, at] = jnp.where(parity == 0, low_face, high_face)
                for c in range(cells):
                    k = (c * (rows // PAD) + r // PAD) * 2 * PAD + PAD * v
                    total = stream(c) + radial(fr, wp, v, f, c, r, PAD) + CENTRE * ws[c] + ys[k : k + PAD]
                    put(v, f, c, at, start(v, f, c, r) + dt * total)
    if rp_ref is not None:
        put_edges(dt, line, fr, wp, rp_ref, rd_ref)


def add_edges(line, rp_ref, rd_ref, out, cells):
    rows = out.shape[3]
    for v in range(2):
        for f in range(5):
            for c, place in cells:
                k = 2 * ((5 * v + f) * 4 + c)
                if not isinstance(c, int):
                    k = pl.multiple_of(k, 2)
                rp, rd = rp_ref[pl.ds(k, 2)], rd_ref[pl.ds(k, 2)]
                out[v, f, place, 0:2] += jnp.where(line == 0, rd, rp)
                out[v, f, place, rows - 2 : rows] += jnp.where(line == 0, rp, rd)


def add_faces(parity, xp_ref, xd_ref, out):
    cells = out.shape[2]
    for v in range(2):
        for f in range(5):
            for j in range(2):
                out[v, f, (cells - 2) * (1 - parity) + j] += xp_ref[v, f, j]
                out[v, f, (cells - 2) * parity + j] += xd_ref[v, f, j]


def all_cells(fn):
    for v in range(2):
        for f in range(5):
            for c in range(4):
                fn(v, f, c)


def place():
    column = lax.axis_index("gx") % 2
    return column, (column + lax.axis_index("row")) % 2


def load_kernel(w_hbm, rho_hbm, vel_hbm, pr_hbm, tab_hbm,
                own_ref, other_ref, outer_ref, inner_ref, base_ref, send_ref, tab_ref, sems):
    column, half = place()
    outer = 2 * column
    pairs = []
    for side, ref in ((1 - half, send_ref), (half, base_ref)):
        pairs.append((rho_hbm.at[:, side], ref.at[0]))
        pairs.append((vel_hbm.at[:, :, side], ref.at[1:4]))
        pairs.append((pr_hbm.at[:, side], ref.at[4]))
    pairs.append((w_hbm.at[:, :, pl.ds(outer, 2), 1 - half], outer_ref))
    pairs.append((w_hbm.at[:, :, pl.ds(2 - outer, 2), 1 - half], inner_ref))
    pairs.append((w_hbm.at[:, :, :, half], own_ref))
    pairs.append((w_hbm.at[:, :, :, 1 - half], other_ref))
    pairs.append((tab_hbm, tab_ref))
    copies = [pltpu.make_async_copy(a, b, sems.at[i]) for i, (a, b) in enumerate(pairs)]
    for copy in copies:
        copy.start()
    for copy in copies:
        copy.wait()


def own_first_kernel(own_ref, other_ref, base_ref, send_ref, tab_ref,
                     part_ref, xp_ref, xd_ref, rp_ref, rd_ref, rpo_ref, rdo_ref, wp, fr, *scratch):
    column, half = place()
    _, cells, rows, _ = base_ref.shape
    get = lambda v, f, c, r: own_ref[v, f, c, r : r + PAD]

    def put(v, f, c, at, value):
        part_ref[v, f, c, at] = value

    section(0.5 * time_step, column, half, half, get, get, base_ref, tab_ref, put,
            xp_ref, xd_ref, rp_ref, rd_ref, wp, fr, *scratch)
    for c in range(cells):
        for r in (0, rows - PAD):
            w = [[other_ref[v, f, c, r : r + PAD] for f in range(5)] for v in range(2)]
            flows = fluxes(send_ref, c, slice(r, r + PAD), w, (1,))
            for v in range(2):
                for f in range(5):
                    fr[v, f, c, PAD + r : 2 * PAD + r] = flows[v][0][f]
                    wp[v, f, c, PAD + r : 2 * PAD + r] = w[v][f]
    put_edges(0.5 * time_step, 1 - half, fr, wp, rpo_ref, rdo_ref)


def face_kernel(outer_ref, base_ref, xd_ref):
    column, _ = place()
    parity = 1 - column
    dt = 0.5 * time_step
    rows = outer_ref.shape[3]
    for r in range(0, rows, PAD):
        at = slice(r, r + PAD)
        w = [[[outer_ref[v, f, j, at] for f in range(5)] for v in range(2)] for j in range(2)]
        flows = [fluxes(base_ref, 2 * parity + j, at, w[j], (0,)) for j in range(2)]
        for v in range(2):
            for f in range(5):
                f0, f1 = flows[0][v][0][f], flows[1][v][0][f]
                w0, w1 = w[0][v][f], w[1][v][f]
                low = (-A2 * f0 - B2 * w0, (A1 * f0 + B1 * w0) + (-A2 * f1 - B2 * w1))
                high = ((-A1 * f1 + B1 * w1) + (A2 * f0 - B2 * w0), A2 * f1 - B2 * w1)
                for j in range(2):
                    xd_ref[v, f, j, at] = dt * jnp.where(parity == 0, low[j], high[j])


def partner_first_kernel(outer_ref, inner_ref, base_ref, tab_ref, w_ref, part_ref, xp_ref, *scratch):
    column, half = place()
    parity = 1 - column
    for v in range(2):
        for f in range(5):
            for j in range(2):
                w_ref[v, f, 2 * parity + j] = outer_ref[v, f, j]
                w_ref[v, f, 2 - 2 * parity + j] = inner_ref[v, f, j]
    get = lambda v, f, c, r: w_ref[v, f, c, r : r + PAD]

    def put(v, f, c, at, value):
        part_ref[v, f, c, at] = value

    section(0.5 * time_step, parity, half, half, get, get, base_ref, tab_ref, put,
            xp_ref, None, None, None, *scratch)


def second_kernel(own, *refs):
    w_ref, part_ref, xp_in, xd_in, rp_in, rd_in, base_ref, tab_ref = refs[:8]
    refs = refs[8:]
    column, half = place()
    parity = column if own else 1 - column
    if own:
        out_ref, xp_ref, xd_ref, rp_ref, rd_ref, *scratch, s1 = refs
        target = out_ref
    else:
        xp_own, inner_ref, outer_ref, xp_ref, xd_ref, rp_ref, rd_ref, *scratch, s1, target = refs

    def fill(v, f, c):
        s1[v, f, c] = part_ref[v, f, c]

    all_cells(fill)
    add_faces(parity, xp_in, xd_in, s1)
    add_edges(half, rp_in, rd_in, s1, [(c, c) for c in range(4)])
    get = lambda v, f, c, r: s1[v, f, c, r : r + PAD]
    start = lambda v, f, c, r: w_ref[v, f, c, r : r + PAD]

    def put(v, f, c, at, value):
        target[v, f, c, at] = value

    section(time_step, parity, half, half, get, start, base_ref, tab_ref, put,
            xp_ref, xd_ref, rp_ref, rd_ref, *scratch)
    if not own:
        for v in range(2):
            for f in range(5):
                for j in range(2):
                    inner_ref[v, f, j] = target[v, f, 2 - 2 * parity + j] + xp_own[v, f, j]
                    outer_ref[v, f, j] = target[v, f, 2 * parity + j]


def sum_kernel(a_ref, b_ref, out_ref):
    out_ref[...] = a_ref[...] + b_ref[...]


def own_last_kernel(part_ref, xp_ref, xd_ref, rp_ref, rd_ref, out_hbm, value, sem):
    column, half = place()

    def fill(v, f, c):
        value[v, f, c] = part_ref[v, f, c]

    all_cells(fill)
    add_faces(column, xp_ref, xd_ref, value)
    add_edges(half, rp_ref, rd_ref, value, [(c, c) for c in range(4)])
    copy = pltpu.make_async_copy(value, out_hbm.at[:, :, :, half], sem)
    copy.start()
    copy.wait()


def other_last_kernel(outer, back_ref, rp_ref, rd_ref, _, out_hbm, value, sem):
    column, half = place()
    first = 2 * column if outer else 2 - 2 * column
    value[...] = back_ref[...]
    add_edges(1 - half, rp_ref, rd_ref, value, [(first + j, j) for j in range(2)])
    copy = pltpu.make_async_copy(value, out_hbm.at[:, :, pl.ds(first, 2), 1 - half], sem)
    copy.start()
    copy.wait()


def second_kernel_par(*refs):
    refs = list(refs)
    xp_own2 = refs.pop(8)
    second_kernel(False, *refs[:8], xp_own2, *refs[8:])


VM = pl.BlockSpec(memory_space=pltpu.VMEM)
HB = pl.BlockSpec(memory_space=pltpu.HBM)
PARAMS = pltpu.CompilerParams(vmem_limit_bytes=40 << 20)


def local(adjoint_vectors, base_density, base_velocity, base_pressure):
    vectors, fields, cells, both, width = adjoint_vectors.shape
    rows = both // 2
    if cells != 4 or vectors != 2 or rows % PAD:
        raise ValueError("unexpected block")
    f32 = jnp.float32
    shape = lambda *s: jax.ShapeDtypeStruct(s, f32)
    tab = jnp.asarray(theta_table(width))
    block, pair = shape(2, 5, cells, rows, width), shape(2, 5, 2, rows, width)
    base, edge = shape(5, cells, rows, width), shape(20 * cells, width)
    halves = lambda a: a.reshape(a.shape[:-2] + (2, rows, width))
    scratch = [
        pltpu.VMEM((2, 5, cells, rows + 2 * PAD, width), f32),
        pltpu.VMEM((2, 5, cells, rows + 2 * PAD, width), f32),
        pltpu.VMEM((2, 5, cells, rows, width), f32),
        pltpu.VMEM((10 * cells * rows, 2 * width), jnp.bfloat16),
        pltpu.VMEM((10 * cells * rows, 2 * width), jnp.bfloat16),
        pltpu.VMEM((2 * cells * rows, width), f32),
    ]
    whole = pltpu.VMEM((2, 5, cells, rows, width), f32)

    gx, row = lax.axis_size("gx"), lax.axis_size("row")
    partner = [(g, g + 1 - 2 * (g % 2)) for g in range(gx)]
    near = [(g, g - 2 + 4 * (g % 2)) for g in range(gx)]
    far = [(g, g + 2 - 4 * (g % 2)) for g in range(gx)]
    inside = lambda perm: [(a, b) for a, b in perm if 0 <= b < gx]
    trade = lambda value: lax.ppermute(value, "gx", partner)
    send_near = lambda value: lax.ppermute(value, "gx", inside(near))
    send_far = lambda value: lax.ppermute(value, "gx", inside(far))

    def beside(value, cross, flip):
        perm = []
        for g in range(gx):
            for j in range(row):
                side = (g + j + flip) % 2
                k = j - 1 + 2 * side
                if 0 <= k < row:
                    perm.append((g * row + j, (partner[g][1] if cross else g) * row + k))
        return lax.ppermute(value, ("gx", "row"), perm)

    def call(kernel, name, outs, ins, extra=(), **more):
        return pl.pallas_call(
            kernel, name=name, out_shape=outs, in_specs=[VM] * len(ins), out_specs=[VM] * len(outs),
            scratch_shapes=list(scratch) + list(extra), compiler_params=PARAMS, **more,
        )(*ins)

    hbm = lambda a: pltpu.with_memory_space_constraint(a, pltpu.HBM)
    own, other, outer, inner, base_own, base_send, table = pl.pallas_call(
        load_kernel, name="load",
        out_shape=[block, block, pair, pair, base, base, jax.ShapeDtypeStruct(tab.shape, tab.dtype)],
        in_specs=[HB] * 5, out_specs=[VM] * 7, scratch_shapes=[pltpu.SemaphoreType.DMA((11,))],
        compiler_params=PARAMS,
    )(hbm(halves(adjoint_vectors)), hbm(halves(base_density)), hbm(halves(base_velocity)),
      hbm(halves(base_pressure)), hbm(tab))
    base_par, outer, inner = trade(base_send), trade(outer), trade(inner)
    part_own, xp_own, xd_own, rp_own, rd_own, rp_other, rd_other = call(
        own_first_kernel, "own_1", [block, pair, pair, edge, edge, edge, edge],
        (own, other, base_own, base_send, table))
    xd_par_in = send_near(xd_own)
    rd_own_in = beside(rd_own, False, 0)
    rd_par_in = beside(rd_other, True, 1)
    rp_par_in = trade(rp_own)
    xd_par = pl.pallas_call(
        face_kernel, name="face", out_shape=pair, in_specs=[VM] * 2, out_specs=VM, compiler_params=PARAMS,
    )(outer, base_par)
    xd_own_in = send_far(xd_par)
    w_par, part_par, xp_par = call(
        partner_first_kernel, "partner_1", [block, block, pair], (outer, inner, base_par, table))
    part_own, xp_own2, xd_own, rp_own, rd_own = call(
        functools.partial(second_kernel, True), "own_2", [block, pair, pair, edge, edge],
        (own, part_own, xp_par, xd_own_in, rp_other, rd_own_in, base_own, table), (whole,))
    xd_par_in2 = send_near(xd_own)
    rd_own_in = beside(rd_own, False, 0)
    inner, outer, xp_par, xd_par, rp_par, rd_par = call(
        second_kernel_par, "partner_2", [pair, pair, pair, pair, edge, edge],
        (w_par, part_par, xp_own, xd_par_in, rp_par_in, rd_par_in, base_par, table, xp_own2), (whole, whole))
    inner = trade(inner)
    xd_own_in = send_far(xd_par)
    rd_other_in = beside(rd_par, True, 0)
    rp_own_in = trade(rp_par)
    outer = trade(pl.pallas_call(
        sum_kernel, name="sum", out_shape=pair, in_specs=[VM] * 2, out_specs=VM, compiler_params=PARAMS,
    )(outer, xd_par_in2))
    full = shape(2, 5, cells, 2, rows, width)
    out = pl.pallas_call(
        own_last_kernel, name="own_3", out_shape=full, in_specs=[VM] * 5, out_specs=HB,
        scratch_shapes=[whole, pltpu.SemaphoreType.DMA], compiler_params=PARAMS,
    )(part_own, xp_par, xd_own_in, rp_own_in, rd_own_in)
    for name, is_outer, back in (("inner_3", False, inner), ("outer_3", True, outer)):
        out = pl.pallas_call(
            functools.partial(other_last_kernel, is_outer), name=name, out_shape=full,
            in_specs=[VM] * 3 + [HB], out_specs=HB,
            scratch_shapes=[pltpu.VMEM((2, 5, 2, rows, width), f32), pltpu.SemaphoreType.DMA],
            input_output_aliases={3: 0}, compiler_params=PARAMS,
        )(back, rp_own, rd_other_in, out)
    return out.reshape(adjoint_vectors.shape)


def solution(mesh):
    in_specs = (
        P(None, None, "gx", "row", None),
        P("gx", "row", None),
        P(None, "gx", "row", None),
        P("gx", "row", None),
    )
    out_specs = P(None, None, "gx", "row", None)
    return jax.shard_map(local, mesh=mesh, in_specs=in_specs, out_specs=out_specs, check_vma=False)
```

time: 77.5 us -> 60.6 us (0.78)
  Pallas kernels: 0 us -> 10.5 us
  matrix products: 10.1 us -> 0 us
  starting transfers between devices: 35.9 us -> 28.3 us
  other arithmetic: 7.22 us -> 0 us
  local copies, waits for them, and re-layouts: 6.57 us -> 0 us
  waiting for transfers between devices: 16.4 us -> 20.7 us
    pallas_call x0 -> x10, Pallas kernels: none -> 10.5 us  [the longest x4 6.15 us: call(): pl.pallas_call(kernel, name=name, out_shape=outs, in_specs=[VM] * len(ins...]
    dot_general x4 -> x0, matrix products: 10.1 us -> none  [azimuthal(): jnp.dot(flat, table.T, precision=lax.Precision.HIGHEST).reshape(shape)]
    ppermute x12 -> x15, starting transfers between devices: 35.9 us -> 28.3 us  [the longest x4 13.2 us: beside(): return lax.ppermute(value, ('gx', 'row'), perm)]
    ppermute x12 -> x15, waiting for transfers between devices: 16.4 us -> 20.7 us  [the longest x7 15.4 us: local(): trade = lambda value: lax.ppermute(value, 'gx', partner)]
    unnamed x24 -> x0, other arithmetic: 3.66 us -> none
    unnamed x12 -> x0, local copies, waits for them, and re-layouts: 2.57 us -> none
    slice x5 -> x0, local copies, waits for them, and re-layouts: 2.56 us -> none  [the longest x4 1.8 us: with_halo(): initial = lax.slice_in_dim(x, 0, width, axis=dim)]
    concatenate x5 -> x0, other arithmetic: 2.4 us -> none  [the longest x4 1.26 us: with_halo(): x = jnp.concatenate([before, x, after], axis=dim)]
  transfers between devices with their start and end apart: 12 -> 15, of which waited for: 4 -> 6; matrix products, arithmetic and copies ran while one was open for 15% -> 0% of each run, Pallas kernels for 0% -> 13%
where the time goes in v3:
time: 60.6 us; the launch traced here: 59.7 us
  starting transfers between devices  28.3 us (47%)
  waiting for transfers between devices  20.7 us (34%)
  Pallas kernels  10.5 us (17%)
    ppermute x7, waiting for transfers between devices, local(): trade = lambda value: lax.ppermute(value, 'gx', partner)  15.4 us
    ppermute x4, starting transfers between devices, beside(): return lax.ppermute(value, ('gx', 'row'), perm)  13.2 us
    ppermute x2, starting transfers between devices, local(): send_far = lambda value: lax.ppermute(value, 'gx', inside(far))  6.41 us
    pallas_call x4, Pallas kernels, call(): pl.pallas_call(kernel, name=name, out_shape=outs, in_specs=[VM] * len(ins...  6.15 us
    ppermute x4, waiting for transfers between devices, beside(): return lax.ppermute(value, ('gx', 'row'), perm)  5.3 us
    ppermute x7, starting transfers between devices, local(): trade = lambda value: lax.ppermute(value, 'gx', partner)  4.46 us
    ppermute x2, starting transfers between devices, local(): send_near = lambda value: lax.ppermute(value, 'gx', inside(near))  4.17 us
    pallas_call x1, Pallas kernels, local(): pl.pallas_call(load_kernel, name='load', out_shape=[block, block, pair, p...  1.73 us
  transfers between devices with their start and end apart: 15, of which 6 were waited for; matrix products, arithmetic and copies ran while one was open for 0% of the time, Pallas kernels for 13%

profile of v3, /device:TPU:17, one launch (start us, length us, event | category | flops | bytes accessed | tf_op | source)
XLA Modules:
  0.0 59.7 jit_solution(15299754570645908670)
XLA Ops:
  0.0 1.7 %load.1 = (f32[2,5,4,24,128]{4,3,2,1,0:T(8,128)S(1)}, f32[2,5,4,24,128]{4,3,2,1,0:T(8,128)S(1)}, f32[2,5,2,24,128]{4,3,2,1,0:T(8,128)S(1)}, f32[2,5,2,24,128]{4,...) custom-call(f32[2,5,4,2,24,128]{5,4,3,2,1,0:T(8,128)} %bitcast.5, ...), custom_call_target="tpu_custom_call" | custom-call | tf_op jit(solution)/shard_map/load/pallas_call | solution.py:389
  1.7 1.3 %collective-permute-start = (f32[2,5,2,24,128]{4,3,2,1,0:T(8,128)S(1)}, f32[2,5,2,24,128]{4,3,2,1,0:T(8,128)S(1)}, u32[]{:S(2)}, u32[]{:S(2)}) collective-permute-start(f32[2,5,2,24,128]{4,3,2,1,0:T(8,128)S(1)} %get-tuple-element.33), channel_id=1, source_target_pairs={{0,4},{4,0},{8,12},{12,8},{16,20},{20,16},{24,28},{28,24},{1,5},{5... | collective-permute-start | bytes 737288 | tf_op jit(solution)/shard_map/ppermute | solution.py:368
  3.0 0.3 collective-permute-start.2
  3.3 1.2 %collective-permute-start.1 = (f32[2,5,2,24,128]{4,3,2,1,0:T(8,128)S(1)}, f32[2,5,2,24,128]{4,3,2,1,0:T(8,128)S(1)}, u32[]{:S(2)}, u32[]{:S(2)}) collective-permute-start(f32[2,5,2,24,128]{4,3,2,1,0:T(8,128)S(1)} %get-tuple-element.34), channel_id=1, source_target_pairs={{0,4},{4,0},{8,12},{12,8},{16,20},{20,16},{24,28},{28,24},{1,5},{5... | collective-permute-start | bytes 737288 | tf_op jit(solution)/shard_map/ppermute | solution.py:368
  4.5 4.1 %collective-permute-done.outer_ref = f32[2,5,2,24,128]{4,3,2,1,0:T(8,128)S(1)} collective-permute-done((f32[2,5,2,24,128]{4,3,2,1,0:T(8,128)S(1)}, f32[2,5,2,24,128]{4,3,2,1,0:T(8,128)S(1)}, u32[]{:S(2)}, u32[]{:S(2)}) %collective-permute-start) | collective-permute-done | bytes 245792 | tf_op jit(solution)/shard_map/ppermute | solution.py:368
  8.6 5.3 %collective-permute-done.2.base_ref.refs_6_ = f32[5,4,24,128]{3,2,1,0:T(8,128)S(1)} collective-permute-done((f32[5,4,24,128]{3,2,1,0:T(8,128)S(1)}, f32[5,4,24,128]{3,2,1,0:T(8,128)S(1)}, u32[]{:S(2)}, u32[]{:S(2)}) %collective-permute-start.2) | collective-permute-done | bytes 245792 | tf_op jit(solution)/shard_map/ppermute | solution.py:368
  13.9 0.1 face.1
  14.0 3.2 %collective-permute-start.6 = (f32[2,5,2,24,128]{4,3,2,1,0:T(8,128)S(1)}, f32[2,5,2,24,128]{4,3,2,1,0:T(8,128)S(1)}, u32[]{:S(2)}, u32[]{:S(2)}) collective-permute-start(f32[2,5,2,24,128]{4,3,2,1,0:T(8,128)S(1)} %face.1), channel_id=1, source_target_pairs={{0,8},{8,16},{12,4},{16,24},{20,12},{28,20},{1,9},{9,17},{13,5},{1... | collective-permute-start | bytes 737288 | tf_op jit(solution)/shard_map/ppermute | solution.py:370
  17.2 1.7 %own_1.1 = (f32[2,5,4,24,128]{4,3,2,1,0:T(8,128)S(1)}, f32[2,5,2,24,128]{4,3,2,1,0:T(8,128)S(1)}, f32[2,5,2,24,128]{4,3,2,1,0:T(8,128)S(1)}, f32[80,128]{1,0:T(8...) custom-call(f32[2,5,4,24,128]{4,3,2,1,0:T(8,128)S(1)} %get-tuple-element.39.own_ref.refs_0_, ...), custom_call_target="tpu_custom_call" | custom-call | tf_op jit(solution)/shard_map/own_1/pallas_call | solution.py:383
  18.9 6.0 %collective-permute-start.7 = (f32[80,128]{1,0:T(8,128)S(1)}, f32[80,128]{1,0:T(8,128)S(1)}, u32[]{:S(2)}, u32[]{:S(2)}) collective-permute-start(f32[80,128]{1,0:T(8,128)S(1)} %get-tuple-element.49), channel_id=1, source_target_pairs={{1,2},{2,1},{4,5},{5,4},{6,7},{7,6},{9,10},{10,9},{12,13},{13,12},... | collective-permute-start | bytes 122888 | tf_op jit(solution)/shard_map/ppermute | solution.py:380
  24.9 2.1 %collective-permute-start.3 = (f32[2,5,2,24,128]{4,3,2,1,0:T(8,128)S(1)}, f32[2,5,2,24,128]{4,3,2,1,0:T(8,128)S(1)}, u32[]{:S(2)}, u32[]{:S(2)}) collective-permute-start(f32[2,5,2,24,128]{4,3,2,1,0:T(8,128)S(1)} %get-tuple-element.43), channel_id=1, source_target_pairs={{4,12},{8,0},{12,20},{16,8},{20,28},{24,16},{5,13},{9,1},{13,21},{... | collective-permute-start | bytes 737288 | tf_op jit(solution)/shard_map/ppermute | solution.py:369
  27.0 0.0 collective-permute-done.1.inner_ref
  27.0 1.2 %partner_1.1 = (f32[2,5,4,24,128]{4,3,2,1,0:T(8,128)S(1)}, f32[2,5,4,24,128]{4,3,2,1,0:T(8,128)S(1)}, f32[2,5,2,24,128]{4,3,2,1,0:T(8,128)S(1)}) custom-call(f32[2,5,2,24,128]{4,3,2,1,0:T(8,128)S(1)} %collective-permute-done.outer_ref, f32[2,5,2,24,128]{4,3,2,1,0:T(8,128)S(1)} %collective-permute-done.1.inner_ref, ...), custom_call_target="tpu_custom_call" | custom-call | tf_op jit(solution)/shard_map/partner_1/pallas_call | solution.py:383
  28.2 0.0 collective-permute-done.7.refs_5_
  28.3 0.0 collective-permute-done.6.refs_3_
  28.3 1.6 %own_2.1 = (f32[2,5,4,24,128]{4,3,2,1,0:T(8,128)S(1)}, f32[2,5,2,24,128]{4,3,2,1,0:T(8,128)S(1)}, f32[2,5,2,24,128]{4,3,2,1,0:T(8,128)S(1)}, f32[80,128]{1,0:T(8,128)S(1)}, f32[80,128]{1,0:T(8,128)S(1)}) custom-call(f32[2,5,4,24,128]{4,3,2,1,0:T(8,128)S(1)} %get-tuple-element.39.own_ref.refs_0_, f32[2,5,4,24,128]{4,3,2,1,0:T(8,128)S(1)} %get-tuple-element.46.refs_1_, ...), custom_call_target="tpu_custom_call" | custom-call | tf_op jit(solution)/shard_map/own_2/pallas_call | solution.py:383
  29.9 2.1 %collective-permute-start.8 = (f32[2,5,2,24,128]{4,3,2,1,0:T(8,128)S(1)}, f32[2,5,2,24,128]{4,3,2,1,0:T(8,128)S(1)}, u32[]{:S(2)}, u32[]{:S(2)}) collective-permute-start(f32[2,5,2,24,128]{4,3,2,1,0:T(8,128)S(1)} %get-tuple-element.52), channel_id=1, source_target_pairs={{4,12},{8,0},{12,20},{16,8},{20,28},{24,16},{5,13},{9,1},{13,21},{... | collective-permute-start | bytes 737288 | tf_op jit(solution)/shard_map/ppermute | solution.py:369
  32.0 0.1 collective-permute-start.4
  32.1 2.0 %collective-permute-start.5 = (f32[80,128]{1,0:T(8,128)S(1)}, f32[80,128]{1,0:T(8,128)S(1)}, u32[]{:S(2)}, u32[]{:S(2)}) collective-permute-start(f32[80,128]{1,0:T(8,128)S(1)} %get-tuple-element.45), channel_id=1, source_target_pairs={{0,5},{1,4},{2,7},{3,6},{5,2},{6,1},{8,13},{9,12},{10,15},{11,14},... | collective-permute-start | bytes 122888 | tf_op jit(solution)/shard_map/ppermute | solution.py:380
  34.1 1.1 %collective-permute-done.4.refs_4_ = f32[80,128]{1,0:T(8,128)S(1)} collective-permute-done((f32[80,128]{1,0:T(8,128)S(1)}, f32[80,128]{1,0:T(8,128)S(1)}, u32[]{:S(2)}, u32[]{:S(2)}) %collective-permute-start.4) | collective-permute-done | bytes 40992 | tf_op jit(solution)/shard_map/ppermute | solution.py:368
  35.2 3.1 %collective-permute-done.5.refs_5_ = f32[80,128]{1,0:T(8,128)S(1)} collective-permute-done((f32[80,128]{1,0:T(8,128)S(1)}, f32[80,128]{1,0:T(8,128)S(1)}, u32[]{:S(2)}, u32[]{:S(2)}) %collective-permute-start.5) | collective-permute-done | bytes 40992 | tf_op jit(solution)/shard_map/ppermute | solution.py:380
  38.3 0.0 collective-permute-done.3.refs_3_
  38.3 1.7 %partner_2.1 = (f32[2,5,2,24,128]{4,3,2,1,0:T(8,128)S(1)}, f32[2,5,2,24,128]{4,3,2,1,0:T(8,128)S(1)}, f32[2,5,2,24,128]{4,3,2,1,0:T(8,128)S(1)}, f32[2,5,2,24,12...) custom-call(f32[2,5,4,24,128]{4,3,2,1,0:T(8,128)S(1)} %get-tuple-element.37.refs_0_, ...), custom_call_target="tpu_custom_call" | custom-call | tf_op jit(solution)/shard_map/partner_2/pallas_call | solution.py:383
  39.9 3.2 %collective-permute-start.12 = (f32[2,5,2,24,128]{4,3,2,1,0:T(8,128)S(1)}, f32[2,5,2,24,128]{4,3,2,1,0:T(8,128)S(1)}, u32[]{:S(2)}, u32[]{:S(2)}) collective-permute-start(f32[2,5,2,24,128]{4,3,2,1,0:T(8,128)S(1)} %get-tuple-element.58), channel_id=1, source_target_pairs={{0,8},{8,16},{12,4},{16,24},{20,12},{28,20},{1,9},{9,17},{13,5},{1... | collective-permute-start | bytes 737288 | tf_op jit(solution)/shard_map/ppermute | solution.py:370
  43.2 0.1 collective-permute-start.11
  43.2 0.0 collective-permute-done.8.b_ref
  43.3 1.5 %collective-permute-start.9 = (f32[2,5,2,24,128]{4,3,2,1,0:T(8,128)S(1)}, f32[2,5,2,24,128]{4,3,2,1,0:T(8,128)S(1)}, u32[]{:S(2)}, u32[]{:S(2)}) collective-permute-start(f32[2,5,2,24,128]{4,3,2,1,0:T(8,128)S(1)} %sum.1), channel_id=1, source_target_pairs={{0,4},{4,0},{8,12},{12,8},{16,20},{20,16},{24,28},{28,24},{1,5},{5... | collective-permute-start | bytes 737288 | tf_op jit(solution)/shard_map/ppermute | solution.py:368
  44.8 3.3 %collective-permute-start.14 = (f32[80,128]{1,0:T(8,128)S(1)}, f32[80,128]{1,0:T(8,128)S(1)}, u32[]{:S(2)}, u32[]{:S(2)}) collective-permute-start(f32[80,128]{1,0:T(8,128)S(1)} %get-tuple-element.60), channel_id=1, source_target_pairs={{1,2},{2,1},{4,5},{5,4},{6,7},{7,6},{9,10},{10,9},{12,13},{13,12},... | collective-permute-start | bytes 122888 | tf_op jit(solution)/shard_map/ppermute | solution.py:380
  48.1 0.1 collective-permute-start.13
  48.2 2.2 %collective-permute-done.14.rd_ref = f32[80,128]{1,0:T(8,128)S(1)} collective-permute-done((f32[80,128]{1,0:T(8,128)S(1)}, f32[80,128]{1,0:T(8,128)S(1)}, u32[]{:S(2)}, u32[]{:S(2)}) %collective-permute-start.14) | collective-permute-done | bytes 40992 | tf_op jit(solution)/shard_map/ppermute | solution.py:380
  50.4 1.9 %collective-permute-start.10 = (f32[80,128]{1,0:T(8,128)S(1)}, f32[80,128]{1,0:T(8,128)S(1)}, u32[]{:S(2)}, u32[]{:S(2)}) collective-permute-start(f32[80,128]{1,0:T(8,128)S(1)} %get-tuple-element.54), channel_id=1, source_target_pairs={{1,6},{2,5},{4,1},{5,0},{6,3},{7,2},{9,14},{10,13},{12,9},{13,8},{... | collective-permute-start | bytes 122888 | tf_op jit(solution)/shard_map/ppermute | solution.py:380
  52.3 4.9 %collective-permute-done.13.rp_ref = f32[80,128]{1,0:T(8,128)S(1)} collective-permute-done((f32[80,128]{1,0:T(8,128)S(1)}, f32[80,128]{1,0:T(8,128)S(1)}, u32[]{:S(2)}, u32[]{:S(2)}) %collective-permute-start.13) | collective-permute-done | bytes 40992 | tf_op jit(solution)/shard_map/ppermute | solution.py:368
  57.2 0.0 collective-permute-done.12.xd_ref
  57.2 0.9 %own_3.1._ = f32[2,5,4,2,24,128]{5,4,3,2,1,0:T(8,128)} custom-call(f32[2,5,4,24,128]{4,3,2,1,0:T(8,128)S(1)} %get-tuple-element.56.part_ref, f32[2,5,2,24,128]{4,3,2,1,0:T(8,128)S(1)} %get-tuple-element.57.xp_ref, f32[2,5,2,24,128]{4,3,2,1,0:T(8,128)S(1)} %collective-permute-done.12.xd_ref, f32[80,128]{1,0:T(8,128)S(1)} %collective-permute-done.13.rp_ref, ...), custom_call_target="tpu_custom_call" | custom-call | tf_op jit(solution)/shard_map/own_3/pallas_call | solution.py:426
  58.1 0.0 collective-permute-done.10.rd_ref
  58.2 0.0 collective-permute-done.11.back_ref
  58.2 0.8 %inner_3.1._ = f32[2,5,4,2,24,128]{5,4,3,2,1,0:T(8,128)} custom-call(f32[2,5,2,24,128]{4,3,2,1,0:T(8,128)S(1)} %collective-permute-done.11.back_ref, f32[80,128]{1,0:T(8,128)S(1)} %get-tuple-element.53.rp_ref, f32[80,128]{1,0:T(8,128)S(1)} %collective-permute-done.10.rd_ref, f32[2,5,4,2,24,128]{5,4,3,2,1,0:T(8,128)} %own_3.1._), custom_call_target="tpu_custom_call", output_to_operand_aliasing={{}: (3, {})} | custom-call | tf_op jit(solution)/shard_map/inner_3/pallas_call | solution.py:431
  58.9 0.0 collective-permute-done.9.back_ref
  58.9 0.7 %outer_3.1 = f32[2,5,4,2,24,128]{5,4,3,2,1,0:T(8,128)} custom-call(f32[2,5,2,24,128]{4,3,2,1,0:T(8,128)S(1)} %collective-permute-done.9.back_ref, f32[80,128]{1,0:T(8,128)S(1)} %get-tuple-element.53.rp_ref, f32[80,128]{1,0:T(8,128)S(1)} %collective-permute-done.10.rd_ref, f32[2,5,4,2,24,128]{5,4,3,2,1,0:T(8,128)} %inner_3.1._), custom_call_target="tpu_custom_call", output_to_operand_aliasing={{}: (3, {})} | custom-call | tf_op jit(solution)/shard_map/outer_3/pallas_call | solution.py:431
  (1 shorter events, 0.0 us)
Async XLA Ops:
  1.7 6.9 %collective-permute-start = (f32[2,5,2,24,128]{4,3,2,1,0:T(8,128)S(1)}, f32[2,5,2,24,128]{4,3,2,1,0:T(8,128)S(1)}, u32[]{:S(2)}, u32[]{:S(2)}) collective-permute-start(f32[2,5,2,24,128]{4,3,2,1,0:T(8,128)S(1)} %get-tuple-element.33), channel_id=1, source_target_pairs={{0,4},{4,0},{8,12},{12,8},{16,20},{20,16},{24,28},{28,24},{1,5},{5... | collective-permute-start | bytes 737288 | tf_op jit(solution)/shard_map/ppermute | solution.py:368
  3.0 10.9 %collective-permute-start.2 = (f32[5,4,24,128]{3,2,1,0:T(8,128)S(1)}, f32[5,4,24,128]{3,2,1,0:T(8,128)S(1)}, u32[]{:S(2)}, u32[]{:S(2)}) collective-permute-start(f32[5,4,24,128]{3,2,1,0:T(8,128)S(1)} %get-tuple-element.35.send_ref), channel_id=1, source_target_pairs={{0,4},{4,0},{8,12},{12,8},{16,20},{20,16},{24,28},{28,24},{1,5},{5... | collective-permute-start | bytes 737288 | tf_op jit(solution)/shard_map/ppermute | solution.py:368
  3.3 23.8 %collective-permute-start.1 = (f32[2,5,2,24,128]{4,3,2,1,0:T(8,128)S(1)}, f32[2,5,2,24,128]{4,3,2,1,0:T(8,128)S(1)}, u32[]{:S(2)}, u32[]{:S(2)}) collective-permute-start(f32[2,5,2,24,128]{4,3,2,1,0:T(8,128)S(1)} %get-tuple-element.34), channel_id=1, source_target_pairs={{0,4},{4,0},{8,12},{12,8},{16,20},{20,16},{24,28},{28,24},{1,5},{5... | collective-permute-start | bytes 737288 | tf_op jit(solution)/shard_map/ppermute | solution.py:368
  14.0 14.2 %collective-permute-start.6 = (f32[2,5,2,24,128]{4,3,2,1,0:T(8,128)S(1)}, f32[2,5,2,24,128]{4,3,2,1,0:T(8,128)S(1)}, u32[]{:S(2)}, u32[]{:S(2)}) collective-permute-start(f32[2,5,2,24,128]{4,3,2,1,0:T(8,128)S(1)} %face.1), channel_id=1, source_target_pairs={{0,8},{8,16},{12,4},{16,24},{20,12},{28,20},{1,9},{9,17},{13,5},{1... | collective-permute-start | bytes 737288 | tf_op jit(solution)/shard_map/ppermute | solution.py:370
  18.9 9.3 %collective-permute-start.7 = (f32[80,128]{1,0:T(8,128)S(1)}, f32[80,128]{1,0:T(8,128)S(1)}, u32[]{:S(2)}, u32[]{:S(2)}) collective-permute-start(f32[80,128]{1,0:T(8,128)S(1)} %get-tuple-element.49), channel_id=1, source_target_pairs={{1,2},{2,1},{4,5},{5,4},{6,7},{7,6},{9,10},{10,9},{12,13},{13,12},... | collective-permute-start | bytes 122888 | tf_op jit(solution)/shard_map/ppermute | solution.py:380
  24.9 13.3 %collective-permute-start.3 = (f32[2,5,2,24,128]{4,3,2,1,0:T(8,128)S(1)}, f32[2,5,2,24,128]{4,3,2,1,0:T(8,128)S(1)}, u32[]{:S(2)}, u32[]{:S(2)}) collective-permute-start(f32[2,5,2,24,128]{4,3,2,1,0:T(8,128)S(1)} %get-tuple-element.43), channel_id=1, source_target_pairs={{4,12},{8,0},{12,20},{16,8},{20,28},{24,16},{5,13},{9,1},{13,21},{... | collective-permute-start | bytes 737288 | tf_op jit(solution)/shard_map/ppermute | solution.py:369
  29.9 13.4 %collective-permute-start.8 = (f32[2,5,2,24,128]{4,3,2,1,0:T(8,128)S(1)}, f32[2,5,2,24,128]{4,3,2,1,0:T(8,128)S(1)}, u32[]{:S(2)}, u32[]{:S(2)}) collective-permute-start(f32[2,5,2,24,128]{4,3,2,1,0:T(8,128)S(1)} %get-tuple-element.52), channel_id=1, source_target_pairs={{4,12},{8,0},{12,20},{16,8},{20,28},{24,16},{5,13},{9,1},{13,21},{... | collective-permute-start | bytes 737288 | tf_op jit(solution)/shard_map/ppermute | solution.py:369
  32.0 3.2 %collective-permute-start.4 = (f32[80,128]{1,0:T(8,128)S(1)}, f32[80,128]{1,0:T(8,128)S(1)}, u32[]{:S(2)}, u32[]{:S(2)}) collective-permute-start(f32[80,128]{1,0:T(8,128)S(1)} %get-tuple-element.44), channel_id=1, source_target_pairs={{0,4},{4,0},{8,12},{12,8},{16,20},{20,16},{24,28},{28,24},{1,5},{5... | collective-permute-start | bytes 122888 | tf_op jit(solution)/shard_map/ppermute | solution.py:368
  32.1 6.2 %collective-permute-start.5 = (f32[80,128]{1,0:T(8,128)S(1)}, f32[80,128]{1,0:T(8,128)S(1)}, u32[]{:S(2)}, u32[]{:S(2)}) collective-permute-start(f32[80,128]{1,0:T(8,128)S(1)} %get-tuple-element.45), channel_id=1, source_target_pairs={{0,5},{1,4},{2,7},{3,6},{5,2},{6,1},{8,13},{9,12},{10,15},{11,14},... | collective-permute-start | bytes 122888 | tf_op jit(solution)/shard_map/ppermute | solution.py:380
  39.9 17.2 %collective-permute-start.12 = (f32[2,5,2,24,128]{4,3,2,1,0:T(8,128)S(1)}, f32[2,5,2,24,128]{4,3,2,1,0:T(8,128)S(1)}, u32[]{:S(2)}, u32[]{:S(2)}) collective-permute-start(f32[2,5,2,24,128]{4,3,2,1,0:T(8,128)S(1)} %get-tuple-element.58), channel_id=1, source_target_pairs={{0,8},{8,16},{12,4},{16,24},{20,12},{28,20},{1,9},{9,17},{13,5},{1... | collective-permute-start | bytes 737288 | tf_op jit(solution)/shard_map/ppermute | solution.py:370
  43.2 15.0 %collective-permute-start.11 = (f32[2,5,2,24,128]{4,3,2,1,0:T(8,128)S(1)}, f32[2,5,2,24,128]{4,3,2,1,0:T(8,128)S(1)}, u32[]{:S(2)}, u32[]{:S(2)}) collective-permute-start(f32[2,5,2,24,128]{4,3,2,1,0:T(8,128)S(1)} %get-tuple-element.55), channel_id=1, source_target_pairs={{0,4},{4,0},{8,12},{12,8},{16,20},{20,16},{24,28},{28,24},{1,5},{5... | collective-permute-start | bytes 737288 | tf_op jit(solution)/shard_map/ppermute | solution.py:368
  43.3 15.6 %collective-permute-start.9 = (f32[2,5,2,24,128]{4,3,2,1,0:T(8,128)S(1)}, f32[2,5,2,24,128]{4,3,2,1,0:T(8,128)S(1)}, u32[]{:S(2)}, u32[]{:S(2)}) collective-permute-start(f32[2,5,2,24,128]{4,3,2,1,0:T(8,128)S(1)} %sum.1), channel_id=1, source_target_pairs={{0,4},{4,0},{8,12},{12,8},{16,20},{20,16},{24,28},{28,24},{1,5},{5... | collective-permute-start | bytes 737288 | tf_op jit(solution)/shard_map/ppermute | solution.py:368
  44.8 5.6 %collective-permute-start.14 = (f32[80,128]{1,0:T(8,128)S(1)}, f32[80,128]{1,0:T(8,128)S(1)}, u32[]{:S(2)}, u32[]{:S(2)}) collective-permute-start(f32[80,128]{1,0:T(8,128)S(1)} %get-tuple-element.60), channel_id=1, source_target_pairs={{1,2},{2,1},{4,5},{5,4},{6,7},{7,6},{9,10},{10,9},{12,13},{13,12},... | collective-permute-start | bytes 122888 | tf_op jit(solution)/shard_map/ppermute | solution.py:380
  48.1 9.1 %collective-permute-start.13 = (f32[80,128]{1,0:T(8,128)S(1)}, f32[80,128]{1,0:T(8,128)S(1)}, u32[]{:S(2)}, u32[]{:S(2)}) collective-permute-start(f32[80,128]{1,0:T(8,128)S(1)} %get-tuple-element.59), channel_id=1, source_target_pairs={{0,4},{4,0},{8,12},{12,8},{16,20},{20,16},{24,28},{28,24},{1,5},{5... | collective-permute-start | bytes 122888 | tf_op jit(solution)/shard_map/ppermute | solution.py:368
  50.4 7.8 %collective-permute-start.10 = (f32[80,128]{1,0:T(8,128)S(1)}, f32[80,128]{1,0:T(8,128)S(1)}, u32[]{:S(2)}, u32[]{:S(2)}) collective-permute-start(f32[80,128]{1,0:T(8,128)S(1)} %get-tuple-element.54), channel_id=1, source_target_pairs={{1,6},{2,5},{4,1},{5,0},{6,3},{7,2},{9,14},{10,13},{12,9},{13,8},{... | collective-permute-start | bytes 122888 | tf_op jit(solution)/shard_map/ppermute | solution.py:380

commit v4 on v3

--- a/solution.py
+++ b/solution.py
@@ -231,10 +231,11 @@
     put_edges(0.5 * time_step, 1 - half, fr, wp, rpo_ref, rdo_ref)
 
 
-def face_kernel(outer_ref, base_ref, xd_ref):
+def face_kernel(outer_ref, base_ref, _, own_ref, xd_ref, copy_ref):
     column, _ = place()
     parity = 1 - column
     dt = 0.5 * time_step
+    copy_ref[...] = own_ref[...]
     rows = outer_ref.shape[3]
     for r in range(0, rows, PAD):
         at = slice(r, r + PAD)
@@ -250,14 +251,29 @@
                     xd_ref[v, f, j, at] = dt * jnp.where(parity == 0, low[j], high[j])
 
 
-def partner_first_kernel(outer_ref, inner_ref, base_ref, tab_ref, w_ref, part_ref, xp_ref, *scratch):
+def pack_kernel(inner_ref, rp_ref, rd_ref, _, message_ref):
+    rows = inner_ref.shape[3]
+    for v in range(2):
+        for f in range(5):
+            for j in range(2):
+                k = ((5 * v + f) * 2 + j) * rows
+                message_ref[k : k + rows] = inner_ref[v, f, j]
+    n = 20 * rows
+    edge = rp_ref.shape[0]
+    message_ref[n : n + edge] = rp_ref[...]
+    message_ref[n + edge : n + 2 * edge] = rd_ref[...]
+
+
+def partner_first_kernel(outer_ref, message_ref, base_ref, tab_ref, w_ref, part_ref, xp_ref, *scratch):
     column, half = place()
     parity = 1 - column
+    rows = outer_ref.shape[3]
     for v in range(2):
         for f in range(5):
             for j in range(2):
                 w_ref[v, f, 2 * parity + j] = outer_ref[v, f, j]
-                w_ref[v, f, 2 - 2 * parity + j] = inner_ref[v, f, j]
+                k = ((5 * v + f) * 2 + j) * rows
+                w_ref[v, f, 2 - 2 * parity + j] = message_ref[k : k + rows]
     get = lambda v, f, c, r: w_ref[v, f, c, r : r + PAD]
 
     def put(v, f, c, at, value):
@@ -267,71 +283,83 @@
             xp_ref, None, None, None, *scratch)
 
 
-def second_kernel(own, *refs):
-    w_ref, part_ref, xp_in, xd_in, rp_in, rd_in, base_ref, tab_ref = refs[:8]
-    refs = refs[8:]
-    column, half = place()
-    parity = column if own else 1 - column
-    if own:
-        out_ref, xp_ref, xd_ref, rp_ref, rd_ref, *scratch, s1 = refs
-        target = out_ref
-    else:
-        xp_own, inner_ref, outer_ref, xp_ref, xd_ref, rp_ref, rd_ref, *scratch, s1, target = refs
-
+def start_second(parity, half, part_ref, xp_in, xd_in, rp_in, rd_in, s1):
     def fill(v, f, c):
         s1[v, f, c] = part_ref[v, f, c]
 
     all_cells(fill)
     add_faces(parity, xp_in, xd_in, s1)
     add_edges(half, rp_in, rd_in, s1, [(c, c) for c in range(4)])
+
+
+def own_second_kernel(w_ref, part_ref, xp_in, xd_in, rp_in, rd_in, base_ref, tab_ref,
+                      out_ref, xp_ref, xd_ref, rp_ref, rd_ref, *scratch):
+    *scratch, s1 = scratch
+    column, half = place()
+    start_second(column, half, part_ref, xp_in, xd_in, rp_in, rd_in, s1)
     get = lambda v, f, c, r: s1[v, f, c, r : r + PAD]
     start = lambda v, f, c, r: w_ref[v, f, c, r : r + PAD]
 
     def put(v, f, c, at, value):
+        out_ref[v, f, c, at] = value
+
+    section(time_step, column, half, half, get, start, base_ref, tab_ref, put,
+            xp_ref, xd_ref, rp_ref, rd_ref, *scratch)
+
+
+def partner_second_kernel(w_ref, part_ref, xp_in, xd_in, message_in, xp_own, base_ref, tab_ref,
+                          message_ref, outer_ref, xp_ref, xd_ref, rd_ref, *scratch):
+    *scratch, s1, target = scratch
+    column, half = place()
+    parity = 1 - column
+    rows = outer_ref.shape[3]
+    n = 20 * rows
+    edge = rd_ref.shape[0]
+    start_second(parity, half, part_ref, xp_in, xd_in, message_in.at[n : n + edge],
+                 message_in.at[n + edge : n + 2 * edge], s1)
+    get = lambda v, f, c, r: s1[v, f, c, r : r + PAD]
+    start = lambda v, f, c, r: w_ref[v, f, c, r : r + PAD]
+
+    def put(v, f, c, at, value):
         target[v, f, c, at] = value
 
     section(time_step, parity, half, half, get, start, base_ref, tab_ref, put,
-            xp_ref, xd_ref, rp_ref, rd_ref, *scratch)
-    if not own:
-        for v in range(2):
-            for f in range(5):
-                for j in range(2):
-                    inner_ref[v, f, j] = target[v, f, 2 - 2 * parity + j] + xp_own[v, f, j]
-                    outer_ref[v, f, j] = target[v, f, 2 * parity + j]
-
-
-def sum_kernel(a_ref, b_ref, out_ref):
-    out_ref[...] = a_ref[...] + b_ref[...]
-
-
-def own_last_kernel(part_ref, xp_ref, xd_ref, rp_ref, rd_ref, out_hbm, value, sem):
-    column, half = place()
-
-    def fill(v, f, c):
-        value[v, f, c] = part_ref[v, f, c]
-
-    all_cells(fill)
-    add_faces(column, xp_ref, xd_ref, value)
-    add_edges(half, rp_ref, rd_ref, value, [(c, c) for c in range(4)])
+            xp_ref, xd_ref, message_ref.at[n : n + edge], rd_ref, *scratch)
+    for v in range(2):
+        for f in range(5):
+            for j in range(2):
+                k = ((5 * v + f) * 2 + j) * rows
+                message_ref[k : k + rows] = target[v, f, 2 - 2 * parity + j] + xp_own[v, f, j]
+                outer_ref[v, f, j] = target[v, f, 2 * parity + j]
+
+
+def finish_kernel(outer_ref, xd_ref, message_ref):
+    message_ref[...] = outer_ref[...] + xd_ref[...]
+
+
+def own_last_kernel(part_ref, xp_ref, xd_ref, message_ref, rd_ref, out_hbm, value, sem):
+    column, half = place()
+    edge = rd_ref.shape[0]
+    n = message_ref.shape[0] - edge
+    start_second(column, half, part_ref, xp_ref, xd_ref, message_ref.at[n : n + edge], rd_ref, value)
     copy = pltpu.make_async_copy(value, out_hbm.at[:, :, :, half], sem)
     copy.start()
     copy.wait()
 
 
-def other_last_kernel(outer, back_ref, rp_ref, rd_ref, _, out_hbm, value, sem):
-    column, half = place()
-    first = 2 * column if outer else 2 - 2 * column
-    value[...] = back_ref[...]
-    add_edges(1 - half, rp_ref, rd_ref, value, [(first + j, j) for j in range(2)])
-    copy = pltpu.make_async_copy(value, out_hbm.at[:, :, pl.ds(first, 2), 1 - half], sem)
+def other_last_kernel(inner_ref, outer_ref, rp_ref, rd_ref, _, out_hbm, value, sem):
+    column, half = place()
+    rows = value.shape[3]
+    for v in range(2):
+        for f in range(5):
+            for j in range(2):
+                k = ((5 * v + f) * 2 + j) * rows
+                value[v, f, 2 * column + j] = outer_ref[v, f, j]
+                value[v, f, 2 - 2 * column + j] = inner_ref[k : k + rows]
+    add_edges(1 - half, rp_ref, rd_ref, value, [(c, c) for c in range(4)])
+    copy = pltpu.make_async_copy(value, out_hbm.at[:, :, :, 1 - half], sem)
     copy.start()
     copy.wait()
-
-
-def second_kernel_par(*refs):
-    refs = list(refs)
-    xp_own2 = refs.pop(8)
-    second_kernel(False, *refs[:8], xp_own2, *refs[8:])
 
 
 VM = pl.BlockSpec(memory_space=pltpu.VMEM)
@@ -393,47 +421,42 @@
         compiler_params=PARAMS,
     )(hbm(halves(adjoint_vectors)), hbm(halves(base_density)), hbm(halves(base_velocity)),
       hbm(halves(base_pressure)), hbm(tab))
-    base_par, outer, inner = trade(base_send), trade(outer), trade(inner)
+    small = lambda kernel, name, outs, *ins: pl.pallas_call(
+        kernel, name=name, out_shape=outs, in_specs=[VM] * len(ins), out_specs=VM, compiler_params=PARAMS)(*ins)
+    outer, base_par = trade(outer), trade(base_send)
     part_own, xp_own, xd_own, rp_own, rd_own, rp_other, rd_other = call(
         own_first_kernel, "own_1", [block, pair, pair, edge, edge, edge, edge],
         (own, other, base_own, base_send, table))
-    xd_par_in = send_near(xd_own)
     rd_own_in = beside(rd_own, False, 0)
-    rd_par_in = beside(rd_other, True, 1)
-    rp_par_in = trade(rp_own)
-    xd_par = pl.pallas_call(
-        face_kernel, name="face", out_shape=pair, in_specs=[VM] * 2, out_specs=VM, compiler_params=PARAMS,
-    )(outer, base_par)
-    xd_own_in = send_far(xd_par)
+    rd_other_in = beside(rd_other, False, 1)
+    n, e = 20 * rows, 20 * cells
+    packed = small(pack_kernel, "pack", shape(n + 2 * e, width), inner, rp_own, rd_other_in, rd_own_in)
+    message = trade(packed)
+    xd_par, xd_own = pl.pallas_call(
+        face_kernel, name="face", out_shape=[pair, pair], in_specs=[VM] * 4, out_specs=[VM] * 2, compiler_params=PARAMS,
+    )(outer, base_par, packed, xd_own)
+    xd_own_in, xd_par_in = send_far(xd_par), send_near(xd_own)
     w_par, part_par, xp_par = call(
-        partner_first_kernel, "partner_1", [block, block, pair], (outer, inner, base_par, table))
+        partner_first_kernel, "partner_1", [block, block, pair], (outer, message, base_par, table))
     part_own, xp_own2, xd_own, rp_own, rd_own = call(
-        functools.partial(second_kernel, True), "own_2", [block, pair, pair, edge, edge],
+        own_second_kernel, "own_2", [block, pair, pair, edge, edge],
         (own, part_own, xp_par, xd_own_in, rp_other, rd_own_in, base_own, table), (whole,))
     xd_par_in2 = send_near(xd_own)
-    rd_own_in = beside(rd_own, False, 0)
-    inner, outer, xp_par, xd_par, rp_par, rd_par = call(
-        second_kernel_par, "partner_2", [pair, pair, pair, pair, edge, edge],
-        (w_par, part_par, xp_own, xd_par_in, rp_par_in, rd_par_in, base_par, table, xp_own2), (whole, whole))
+    inner, outer, xp_par, xd_par, rd_par = call(
+        partner_second_kernel, "partner_2", [shape(n + e, width), pair, pair, pair, edge],
+        (w_par, part_par, xp_own, xd_par_in, message, xp_own2, base_par, table), (whole, whole))
     inner = trade(inner)
+    outer = trade(small(finish_kernel, "finish", pair, outer, xd_par_in2))
     xd_own_in = send_far(xd_par)
     rd_other_in = beside(rd_par, True, 0)
-    rp_own_in = trade(rp_par)
-    outer = trade(pl.pallas_call(
-        sum_kernel, name="sum", out_shape=pair, in_specs=[VM] * 2, out_specs=VM, compiler_params=PARAMS,
-    )(outer, xd_par_in2))
+    rd_own_in = beside(rd_own, False, 0)
     full = shape(2, 5, cells, 2, rows, width)
+    last = dict(out_shape=full, out_specs=HB, scratch_shapes=[whole, pltpu.SemaphoreType.DMA], compiler_params=PARAMS)
+    out = pl.pallas_call(own_last_kernel, name="own_3", in_specs=[VM] * 5, **last)(
+        part_own, xp_par, xd_own_in, inner, rd_own_in)
     out = pl.pallas_call(
-        own_last_kernel, name="own_3", out_shape=full, in_specs=[VM] * 5, out_specs=HB,
-        scratch_shapes=[whole, pltpu.SemaphoreType.DMA], compiler_params=PARAMS,
-    )(part_own, xp_par, xd_own_in, rp_own_in, rd_own_in)
-    for name, is_outer, back in (("inner_3", False, inner), ("outer_3", True, outer)):
-        out = pl.pallas_call(
-            functools.partial(other_last_kernel, is_outer), name=name, out_shape=full,
-            in_specs=[VM] * 3 + [HB], out_specs=HB,
-            scratch_shapes=[pltpu.VMEM((2, 5, 2, rows, width), f32), pltpu.SemaphoreType.DMA],
-            input_output_aliases={3: 0}, compiler_params=PARAMS,
-        )(back, rp_own, rd_other_in, out)
+        other_last_kernel, name="other_3", in_specs=[VM] * 4 + [HB], input_output_aliases={4: 0}, **last,
+    )(inner, outer, rp_own, rd_other_in, out)
     return out.reshape(adjoint_vectors.shape)
 
 

time: 60.6 us -> 47.1 us (0.78)
  the two profiles are of different devices: /device:TPU:17 before, /device:TPU:1 now
where the time goes in v4:
time: 47.1 us; the launch traced here: 46.8 us
  starting transfers between devices  30 us (64%)
  Pallas kernels  9.89 us (21%)
  waiting for transfers between devices  6.82 us (14%)
    ppermute x4, starting transfers between devices, beside(): return lax.ppermute(value, ('gx', 'row'), perm)  15.2 us
    ppermute x2, starting transfers between devices, local(): send_far = lambda value: lax.ppermute(value, 'gx', inside(far))  6.34 us
    pallas_call x4, Pallas kernels, call(): pl.pallas_call(kernel, name=name, out_shape=outs, in_specs=[VM] * len(ins...  6.15 us
    ppermute x5, starting transfers between devices, local(): trade = lambda value: lax.ppermute(value, 'gx', partner)  5.8 us
    ppermute x5, waiting for transfers between devices, local(): trade = lambda value: lax.ppermute(value, 'gx', partner)  3.73 us
    ppermute x4, waiting for transfers between devices, beside(): return lax.ppermute(value, ('gx', 'row'), perm)  3.07 us
    ppermute x2, starting transfers between devices, local(): send_near = lambda value: lax.ppermute(value, 'gx', inside(near))  2.58 us
    pallas_call x1, Pallas kernels, local(): pl.pallas_call(load_kernel, name='load', out_shape=[block, block, pair, p...  1.73 us
  transfers between devices with their start and end apart: 13, of which 4 were waited for; matrix products, arithmetic and copies ran while one was open for 0% of the time, Pallas kernels for 16%

profile of v4, /device:TPU:1, one launch (start us, length us, event | category | flops | bytes accessed | tf_op | source)
XLA Modules:
  0.0 46.8 jit_solution(7094141253262818941)
XLA Ops:
  0.0 1.7 %load.1 = (f32[2,5,4,24,128]{4,3,2,1,0:T(8,128)S(1)}, f32[2,5,4,24,128]{4,3,2,1,0:T(8,128)S(1)}, f32[2,5,2,24,128]{4,3,2,1,0:T(8,128)S(1)}, f32[2,5,2,24,128]{4,...) custom-call(f32[2,5,4,2,24,128]{5,4,3,2,1,0:T(8,128)} %bitcast.5, ...), custom_call_target="tpu_custom_call" | custom-call | tf_op jit(solution)/shard_map/load/pallas_call | solution.py:417
  1.7 2.1 %collective-permute-start = (f32[2,5,2,24,128]{4,3,2,1,0:T(8,128)S(1)}, f32[2,5,2,24,128]{4,3,2,1,0:T(8,128)S(1)}, u32[]{:S(2)}, u32[]{:S(2)}) collective-permute-start(f32[2,5,2,24,128]{4,3,2,1,0:T(8,128)S(1)} %get-tuple-element.34), channel_id=1, source_target_pairs={{0,4},{4,0},{8,12},{12,8},{16,20},{20,16},{24,28},{28,24},{1,5},{5... | collective-permute-start | bytes 737288 | tf_op jit(solution)/shard_map/ppermute | solution.py:396
  3.8 0.1 collective-permute-start.4
  3.9 1.7 %own_1.1 = (f32[2,5,4,24,128]{4,3,2,1,0:T(8,128)S(1)}, f32[2,5,2,24,128]{4,3,2,1,0:T(8,128)S(1)}, f32[2,5,2,24,128]{4,3,2,1,0:T(8,128)S(1)}, f32[80,128]{1,0:T(8...) custom-call(f32[2,5,4,24,128]{4,3,2,1,0:T(8,128)S(1)} %get-tuple-element.36.own_ref.w_ref, ...), custom_call_target="tpu_custom_call" | custom-call | tf_op jit(solution)/shard_map/own_1/pallas_call | solution.py:411
  5.6 2.9 %collective-permute-start.1 = (f32[80,128]{1,0:T(8,128)S(1)}, f32[80,128]{1,0:T(8,128)S(1)}, u32[]{:S(2)}, u32[]{:S(2)}) collective-permute-start(f32[80,128]{1,0:T(8,128)S(1)} %get-tuple-element.42), channel_id=1, source_target_pairs={{0,1},{1,0},{2,3},{3,2},{5,6},{6,5},{8,9},{9,8},{10,11},{11,10},{1... | collective-permute-start | bytes 122888 | tf_op jit(solution)/shard_map/ppermute | solution.py:408
  8.5 3.5 %collective-permute-start.2 = (f32[80,128]{1,0:T(8,128)S(1)}, f32[80,128]{1,0:T(8,128)S(1)}, u32[]{:S(2)}, u32[]{:S(2)}) collective-permute-start(f32[80,128]{1,0:T(8,128)S(1)} %get-tuple-element.43), channel_id=1, source_target_pairs={{1,2},{2,1},{4,5},{5,4},{6,7},{7,6},{9,10},{10,9},{12,13},{13,12},... | collective-permute-start | bytes 122888 | tf_op jit(solution)/shard_map/ppermute | solution.py:408
  12.0 0.0 collective-permute-done.1.rd_ref
  12.0 2.1 %collective-permute-done.2._.rd_in = f32[80,128]{1,0:T(8,128)S(1)} collective-permute-done((f32[80,128]{1,0:T(8,128)S(1)}, f32[80,128]{1,0:T(8,128)S(1)}, u32[]{:S(2)}, u32[]{:S(2)}) %collective-permute-start.2) | collective-permute-done | bytes 40992 | tf_op jit(solution)/shard_map/ppermute | solution.py:408
  14.1 0.4 collective-permute-start.3
  14.5 0.0 collective-permute-done.outer_ref
  14.5 0.3 collective-permute-done.4.base_ref
  14.8 0.1 face.1
  14.9 3.1 %collective-permute-start.6 = (f32[2,5,2,24,128]{4,3,2,1,0:T(8,128)S(1)}, f32[2,5,2,24,128]{4,3,2,1,0:T(8,128)S(1)}, u32[]{:S(2)}, u32[]{:S(2)}) collective-permute-start(f32[2,5,2,24,128]{4,3,2,1,0:T(8,128)S(1)} %get-tuple-element.51), channel_id=1, source_target_pairs={{0,8},{8,16},{12,4},{16,24},{20,12},{28,20},{1,9},{9,17},{13,5},{1... | collective-permute-start | bytes 737288 | tf_op jit(solution)/shard_map/ppermute | solution.py:398
  18.1 1.3 %collective-permute-start.5 = (f32[2,5,2,24,128]{4,3,2,1,0:T(8,128)S(1)}, f32[2,5,2,24,128]{4,3,2,1,0:T(8,128)S(1)}, u32[]{:S(2)}, u32[]{:S(2)}) collective-permute-start(f32[2,5,2,24,128]{4,3,2,1,0:T(8,128)S(1)} %get-tuple-element.48), channel_id=1, source_target_pairs={{4,12},{8,0},{12,20},{16,8},{20,28},{24,16},{5,13},{9,1},{13,21},{... | collective-permute-start | bytes 737288 | tf_op jit(solution)/shard_map/ppermute | solution.py:397
  19.4 3.4 %collective-permute-done.3.message_ref.message_in = f32[640,128]{1,0:T(8,128)S(1)} collective-permute-done((f32[640,128]{1,0:T(8,128)S(1)}, f32[640,128]{1,0:T(8,128)S(1)}, u32[]{:S(2)}, u32[]{:S(2)}) %collective-permute-start.3) | collective-permute-done | bytes 327712 | tf_op jit(solution)/shard_map/ppermute | solution.py:396
  22.8 1.2 %partner_1.1 = (f32[2,5,4,24,128]{4,3,2,1,0:T(8,128)S(1)}, f32[2,5,4,24,128]{4,3,2,1,0:T(8,128)S(1)}, f32[2,5,2,24,128]{4,3,2,1,0:T(8,128)S(1)}) custom-call(f32[2,5,2,24,128]{4,3,2,1,0:T(8,128)S(1)} %collective-permute-done.outer_ref, f32[640,128]{1,0:T(8,128)S(1)} %collective-permute-done.3.message_ref.message_in, ...), custom_call_target="tpu_custom_call" | custom-call | tf_op jit(solution)/shard_map/partner_1/pallas_call | solution.py:411
  24.0 0.0 collective-permute-done.6.xd_in
  24.0 1.6 %own_2.1 = (f32[2,5,4,24,128]{4,3,2,1,0:T(8,128)S(1)}, f32[2,5,2,24,128]{4,3,2,1,0:T(8,128)S(1)}, f32[2,5,2,24,128]{4,3,2,1,0:T(8,128)S(1)}, f32[80,128]{1,0:T(8,128)S(1)}, f32[80,128]{1,0:T(8,128)S(1)}) custom-call(f32[2,5,4,24,128]{4,3,2,1,0:T(8,128)S(1)} %get-tuple-element.36.own_ref.w_ref, f32[2,5,4,24,128]{4,3,2,1,0:T(8,128)S(1)} %get-tuple-element.49.part_ref, ...), custom_call_target="tpu_custom_call" | custom-call | tf_op jit(solution)/shard_map/own_2/pallas_call | solution.py:411
  25.6 1.3 %collective-permute-start.8 = (f32[2,5,2,24,128]{4,3,2,1,0:T(8,128)S(1)}, f32[2,5,2,24,128]{4,3,2,1,0:T(8,128)S(1)}, u32[]{:S(2)}, u32[]{:S(2)}) collective-permute-start(f32[2,5,2,24,128]{4,3,2,1,0:T(8,128)S(1)} %get-tuple-element.56), channel_id=1, source_target_pairs={{4,12},{8,0},{12,20},{16,8},{20,28},{24,16},{5,13},{9,1},{13,21},{... | collective-permute-start | bytes 737288 | tf_op jit(solution)/shard_map/ppermute | solution.py:397
  26.9 0.0 collective-permute-done.5.xd_in
  26.9 1.7 %partner_2.1 = (f32[560,128]{1,0:T(8,128)S(1)}, f32[2,5,2,24,128]{4,3,2,1,0:T(8,128)S(1)}, f32[2,5,2,24,128]{4,3,2,1,0:T(8,128)S(1)}, f32[2,5,2,24,128]{4,3,2,1,0:T(8,128)S(1)}, f32[80,128]{1,0:T(8,128)S(1)}) custom-call(f32[2,5,4,24,128]{4,3,2,1,0:T(8,128)S(1)} %get-tuple-element.44.w_ref, f32[2,5,4,24,128]{4,3,2,1,0:T(8,128)S(1)} %get-tuple-element.45.part_ref, ...), custom_call_target="tpu_custom_call" | custom-call | tf_op jit(solution)/shard_map/partner_2/pallas_call | solution.py:411
  28.6 3.2 %collective-permute-start.7 = (f32[560,128]{1,0:T(8,128)S(1)}, f32[560,128]{1,0:T(8,128)S(1)}, u32[]{:S(2)}, u32[]{:S(2)}) collective-permute-start(f32[560,128]{1,0:T(8,128)S(1)} %get-tuple-element.54), channel_id=1, source_target_pairs={{0,4},{4,0},{8,12},{12,8},{16,20},{20,16},{24,28},{28,24},{1,5},{5... | collective-permute-start | bytes 860168 | tf_op jit(solution)/shard_map/ppermute | solution.py:396
  31.8 3.2 %collective-permute-start.11 = (f32[2,5,2,24,128]{4,3,2,1,0:T(8,128)S(1)}, f32[2,5,2,24,128]{4,3,2,1,0:T(8,128)S(1)}, u32[]{:S(2)}, u32[]{:S(2)}) collective-permute-start(f32[2,5,2,24,128]{4,3,2,1,0:T(8,128)S(1)} %get-tuple-element.61), channel_id=1, source_target_pairs={{0,8},{8,16},{12,4},{16,24},{20,12},{28,20},{1,9},{9,17},{13,5},{1... | collective-permute-start | bytes 737288 | tf_op jit(solution)/shard_map/ppermute | solution.py:398
  35.0 0.0 collective-permute-done.8.xd_ref
  35.0 0.1 collective-permute-start.9
  35.1 5.5 %collective-permute-start.12 = (f32[80,128]{1,0:T(8,128)S(1)}, f32[80,128]{1,0:T(8,128)S(1)}, u32[]{:S(2)}, u32[]{:S(2)}) collective-permute-start(f32[80,128]{1,0:T(8,128)S(1)} %get-tuple-element.62), channel_id=1, source_target_pairs={{1,2},{2,1},{4,5},{5,4},{6,7},{7,6},{9,10},{10,9},{12,13},{13,12},... | collective-permute-start | bytes 122888 | tf_op jit(solution)/shard_map/ppermute | solution.py:408
  40.6 3.4 %collective-permute-start.10 = (f32[80,128]{1,0:T(8,128)S(1)}, f32[80,128]{1,0:T(8,128)S(1)}, u32[]{:S(2)}, u32[]{:S(2)}) collective-permute-start(f32[80,128]{1,0:T(8,128)S(1)} %get-tuple-element.58), channel_id=1, source_target_pairs={{1,6},{2,5},{4,1},{5,0},{6,3},{7,2},{9,14},{10,13},{12,9},{13,8},{... | collective-permute-start | bytes 122888 | tf_op jit(solution)/shard_map/ppermute | solution.py:408
  44.0 0.0 collective-permute-done.12.rd_ref
  44.0 0.0 collective-permute-done.11.xd_ref
  44.0 0.0 collective-permute-done.7.message_ref.inner_ref
  44.0 0.9 %own_3.1._ = f32[2,5,4,2,24,128]{5,4,3,2,1,0:T(8,128)} custom-call(f32[2,5,4,24,128]{4,3,2,1,0:T(8,128)S(1)} %get-tuple-element.59.part_ref, f32[2,5,2,24,128]{4,3,2,1,0:T(8,128)S(1)} %get-tuple-element.60.xp_ref, f32[2,5,2,24,128]{4,3,2,1,0:T(8,128)S(1)} %collective-permute-done.11.xd_ref, f32[560,128]{1,0:T(8,128)S(1)} %collective-permute-done.7.message_ref.inner_ref, ...), custom_call_target="tpu_custom_call" | custom-call | tf_op jit(solution)/shard_map/own_3/pallas_call | solution.py:455
  45.0 1.0 %collective-permute-done.10.rd_ref = f32[80,128]{1,0:T(8,128)S(1)} collective-permute-done((f32[80,128]{1,0:T(8,128)S(1)}, f32[80,128]{1,0:T(8,128)S(1)}, u32[]{:S(2)}, u32[]{:S(2)}) %collective-permute-start.10) | collective-permute-done | bytes 40992 | tf_op jit(solution)/shard_map/ppermute | solution.py:408
  45.9 0.0 collective-permute-done.9.outer_ref
  46.0 0.9 %other_3.1 = f32[2,5,4,2,24,128]{5,4,3,2,1,0:T(8,128)} custom-call(f32[560,128]{1,0:T(8,128)S(1)} %collective-permute-done.7.message_ref.inner_ref, f32[2,5,2,24,128]{4,3,2,1,0:T(8,128)S(1)} %collective-permute-done.9.outer_ref, f32[80,128]{1,0:T(8,128)S(1)} %get-tuple-element.57.rp_ref, ...), custom_call_target="tpu_custom_call", output_to_operand_aliasing={{}: (4, {})} | custom-call | tf_op jit(solution)/shard_map/other_3/pallas_call | solution.py:457
  (2 shorter events, 0.1 us)
Async XLA Ops:
  1.7 12.7 %collective-permute-start = (f32[2,5,2,24,128]{4,3,2,1,0:T(8,128)S(1)}, f32[2,5,2,24,128]{4,3,2,1,0:T(8,128)S(1)}, u32[]{:S(2)}, u32[]{:S(2)}) collective-permute-start(f32[2,5,2,24,128]{4,3,2,1,0:T(8,128)S(1)} %get-tuple-element.34), channel_id=1, source_target_pairs={{0,4},{4,0},{8,12},{12,8},{16,20},{20,16},{24,28},{28,24},{1,5},{5... | collective-permute-start | bytes 737288 | tf_op jit(solution)/shard_map/ppermute | solution.py:396
  3.8 10.9 %collective-permute-start.4 = (f32[5,4,24,128]{3,2,1,0:T(8,128)S(1)}, f32[5,4,24,128]{3,2,1,0:T(8,128)S(1)}, u32[]{:S(2)}, u32[]{:S(2)}) collective-permute-start(f32[5,4,24,128]{3,2,1,0:T(8,128)S(1)} %get-tuple-element.39.send_ref), channel_id=1, source_target_pairs={{0,4},{4,0},{8,12},{12,8},{16,20},{20,16},{24,28},{28,24},{1,5},{5... | collective-permute-start | bytes 737288 | tf_op jit(solution)/shard_map/ppermute | solution.py:396
  5.6 6.4 %collective-permute-start.1 = (f32[80,128]{1,0:T(8,128)S(1)}, f32[80,128]{1,0:T(8,128)S(1)}, u32[]{:S(2)}, u32[]{:S(2)}) collective-permute-start(f32[80,128]{1,0:T(8,128)S(1)} %get-tuple-element.42), channel_id=1, source_target_pairs={{0,1},{1,0},{2,3},{3,2},{5,6},{6,5},{8,9},{9,8},{10,11},{11,10},{1... | collective-permute-start | bytes 122888 | tf_op jit(solution)/shard_map/ppermute | solution.py:408
  8.5 5.6 %collective-permute-start.2 = (f32[80,128]{1,0:T(8,128)S(1)}, f32[80,128]{1,0:T(8,128)S(1)}, u32[]{:S(2)}, u32[]{:S(2)}) collective-permute-start(f32[80,128]{1,0:T(8,128)S(1)} %get-tuple-element.43), channel_id=1, source_target_pairs={{1,2},{2,1},{4,5},{5,4},{6,7},{7,6},{9,10},{10,9},{12,13},{13,12},... | collective-permute-start | bytes 122888 | tf_op jit(solution)/shard_map/ppermute | solution.py:408
  14.1 8.7 %collective-permute-start.3 = (f32[640,128]{1,0:T(8,128)S(1)}, f32[640,128]{1,0:T(8,128)S(1)}, u32[]{:S(2)}, u32[]{:S(2)}) collective-permute-start(f32[640,128]{1,0:T(8,128)S(1)} %pack.1._), channel_id=1, source_target_pairs={{0,4},{4,0},{8,12},{12,8},{16,20},{20,16},{24,28},{28,24},{1,5},{5... | collective-permute-start | bytes 983048 | tf_op jit(solution)/shard_map/ppermute | solution.py:396
  14.9 9.1 %collective-permute-start.6 = (f32[2,5,2,24,128]{4,3,2,1,0:T(8,128)S(1)}, f32[2,5,2,24,128]{4,3,2,1,0:T(8,128)S(1)}, u32[]{:S(2)}, u32[]{:S(2)}) collective-permute-start(f32[2,5,2,24,128]{4,3,2,1,0:T(8,128)S(1)} %get-tuple-element.51), channel_id=1, source_target_pairs={{0,8},{8,16},{12,4},{16,24},{20,12},{28,20},{1,9},{9,17},{13,5},{1... | collective-permute-start | bytes 737288 | tf_op jit(solution)/shard_map/ppermute | solution.py:398
  18.1 8.8 %collective-permute-start.5 = (f32[2,5,2,24,128]{4,3,2,1,0:T(8,128)S(1)}, f32[2,5,2,24,128]{4,3,2,1,0:T(8,128)S(1)}, u32[]{:S(2)}, u32[]{:S(2)}) collective-permute-start(f32[2,5,2,24,128]{4,3,2,1,0:T(8,128)S(1)} %get-tuple-element.48), channel_id=1, source_target_pairs={{4,12},{8,0},{12,20},{16,8},{20,28},{24,16},{5,13},{9,1},{13,21},{... | collective-permute-start | bytes 737288 | tf_op jit(solution)/shard_map/ppermute | solution.py:397
  25.6 9.4 %collective-permute-start.8 = (f32[2,5,2,24,128]{4,3,2,1,0:T(8,128)S(1)}, f32[2,5,2,24,128]{4,3,2,1,0:T(8,128)S(1)}, u32[]{:S(2)}, u32[]{:S(2)}) collective-permute-start(f32[2,5,2,24,128]{4,3,2,1,0:T(8,128)S(1)} %get-tuple-element.56), channel_id=1, source_target_pairs={{4,12},{8,0},{12,20},{16,8},{20,28},{24,16},{5,13},{9,1},{13,21},{... | collective-permute-start | bytes 737288 | tf_op jit(solution)/shard_map/ppermute | solution.py:397
  28.6 15.4 %collective-permute-start.7 = (f32[560,128]{1,0:T(8,128)S(1)}, f32[560,128]{1,0:T(8,128)S(1)}, u32[]{:S(2)}, u32[]{:S(2)}) collective-permute-start(f32[560,128]{1,0:T(8,128)S(1)} %get-tuple-element.54), channel_id=1, source_target_pairs={{0,4},{4,0},{8,12},{12,8},{16,20},{20,16},{24,28},{28,24},{1,5},{5... | collective-permute-start | bytes 860168 | tf_op jit(solution)/shard_map/ppermute | solution.py:396
  31.8 12.2 %collective-permute-start.11 = (f32[2,5,2,24,128]{4,3,2,1,0:T(8,128)S(1)}, f32[2,5,2,24,128]{4,3,2,1,0:T(8,128)S(1)}, u32[]{:S(2)}, u32[]{:S(2)}) collective-permute-start(f32[2,5,2,24,128]{4,3,2,1,0:T(8,128)S(1)} %get-tuple-element.61), channel_id=1, source_target_pairs={{0,8},{8,16},{12,4},{16,24},{20,12},{28,20},{1,9},{9,17},{13,5},{1... | collective-permute-start | bytes 737288 | tf_op jit(solution)/shard_map/ppermute | solution.py:398
  35.0 10.9 %collective-permute-start.9 = (f32[2,5,2,24,128]{4,3,2,1,0:T(8,128)S(1)}, f32[2,5,2,24,128]{4,3,2,1,0:T(8,128)S(1)}, u32[]{:S(2)}, u32[]{:S(2)}) collective-permute-start(f32[2,5,2,24,128]{4,3,2,1,0:T(8,128)S(1)} %finish.1), channel_id=1, source_target_pairs={{0,4},{4,0},{8,12},{12,8},{16,20},{20,16},{24,28},{28,24},{1,5},{5... | collective-permute-start | bytes 737288 | tf_op jit(solution)/shard_map/ppermute | solution.py:396
  35.1 8.9 %collective-permute-start.12 = (f32[80,128]{1,0:T(8,128)S(1)}, f32[80,128]{1,0:T(8,128)S(1)}, u32[]{:S(2)}, u32[]{:S(2)}) collective-permute-start(f32[80,128]{1,0:T(8,128)S(1)} %get-tuple-element.62), channel_id=1, source_target_pairs={{1,2},{2,1},{4,5},{5,4},{6,7},{7,6},{9,10},{10,9},{12,13},{13,12},... | collective-permute-start | bytes 122888 | tf_op jit(solution)/shard_map/ppermute | solution.py:408
  40.6 5.3 %collective-permute-start.10 = (f32[80,128]{1,0:T(8,128)S(1)}, f32[80,128]{1,0:T(8,128)S(1)}, u32[]{:S(2)}, u32[]{:S(2)}) collective-permute-start(f32[80,128]{1,0:T(8,128)S(1)} %get-tuple-element.58), channel_id=1, source_target_pairs={{1,6},{2,5},{4,1},{5,0},{6,3},{7,2},{9,14},{10,13},{12,9},{13,8},{... | collective-permute-start | bytes 122888 | tf_op jit(solution)/shard_map/ppermute | solution.py:408

commit v5 on v4

v5 whole, which is shorter than its diff:
```python
import functools

import jax
import jax.numpy as jnp
import ml_dtypes
import numpy as np
from jax import lax
from jax.experimental import pallas as pl
from jax.experimental.pallas import tpu as pltpu
from jax.sharding import PartitionSpec as P

gamma_ratio = 1.4
viscosity = 0.1
time_step = 0.3

A1 = 8.0 / 12.0
A2 = 1.0 / 12.0
B1 = viscosity * 16.0 / 12.0
B2 = viscosity / 12.0
CENTRE = -2.0 * viscosity * 30.0 / 12.0
PAD = 8


def theta_table(azimuth):
    spacing = 2.0 * np.pi / azimuth
    index = np.arange(azimuth)
    offset = index[:, None] - index[None, :]
    signs = np.where(offset % 2 == 0, 1.0, -1.0)
    angle = offset * (spacing / 2.0)
    diagonal = offset == 0
    tangent = np.where(diagonal, 1.0, np.tan(angle))
    sine = np.where(diagonal, 1.0, np.sin(angle))
    first = np.where(diagonal, 0.0, 0.5 * signs * spacing / tangent)
    second = np.where(
        diagonal, -(np.pi**2) / 3.0 - spacing**2 / 6.0, -0.5 * signs * spacing**2 / (sine * sine)
    )
    table = np.concatenate([first.T, viscosity * second.T], axis=0).astype(np.float32)
    high = table.astype(ml_dtypes.bfloat16)
    low = (table - high.astype(np.float32)).astype(ml_dtypes.bfloat16)
    return np.concatenate([high, low], axis=1)


def fluxes(base_ref, c, at, w, directions):
    rho, pr = base_ref[0, c, at], base_ref[4, c, at]
    inv = 1.0 / rho
    pg = gamma_ratio * pr
    flows = []
    for v in range(2):
        q = rho * w[v][0] + pg * w[v][4]
        rows = []
        for d in directions:
            speed = base_ref[1 + d, c, at]
            flow = [speed * w[v][f] for f in range(5)]
            flow[1 + d] = flow[1 + d] + q
            flow[4] = flow[4] + w[v][1 + d] * inv
            rows.append(flow)
        flows.append(rows)
    return flows


def radial(fr, wp, v, f, c, r, n):
    base = PAD + r
    sh = lambda buf, k: buf[v, f, c, base + k : base + k + n]
    near = 8.0 * (sh(fr, 1) - sh(fr, -1)) - (sh(fr, 2) - sh(fr, -2))
    return near + B1 * (sh(wp, 1) + sh(wp, -1)) - B2 * (sh(wp, 2) + sh(wp, -2))


def clear_pads(fr, wp):
    _, _, cells, padded, width = fr.shape
    zeros = jnp.zeros((PAD, width), jnp.float32)
    for v in range(2):
        for f in range(5):
            for c in range(cells):
                for buf in (wp, fr):
                    buf[v, f, c, 0:PAD] = zeros
                    buf[v, f, c, padded - PAD : padded] = zeros


def put_edges(dt, line, fr, wp, rp_ref, rd_ref):
    _, _, cells, padded, _ = fr.shape
    for v in range(2):
        for f in range(5):
            for c in range(cells):
                low = dt * radial(fr, wp, v, f, c, -2, 2)
                high = dt * radial(fr, wp, v, f, c, padded - 2 * PAD, 2)
                k = 2 * ((5 * v + f) * cells + c)
                rp_ref[k : k + 2] = jnp.where(line == 0, high, low)
                rd_ref[k : k + 2] = jnp.where(line == 0, low, high)


def section(dt, parity, line, half, get, start, base_ref, tab_ref, put, xp_ref, xd_ref, rp_ref, rd_ref,
            wp, fr, fx, xh, xl, ys):
    _, cells, rows, width = base_ref.shape
    total_rows = 2 * rows * lax.axis_size("row")
    row_start = lax.axis_index("row") * (2 * rows) + half * rows
    span = 2 * cells * rows
    clear_pads(fr, wp)

    def split(flow, k, lanes):
        both = jnp.concatenate(flow, axis=0)
        high = both.astype(jnp.bfloat16)
        xh[k : k + 2 * PAD, lanes] = high
        xl[k : k + 2 * PAD, lanes] = (both - high.astype(jnp.float32)).astype(jnp.bfloat16)

    for r in range(0, rows, PAD):
        at = slice(r, r + PAD)
        inside = slice(PAD + r, 2 * PAD + r)
        index = row_start + r + lax.broadcasted_iota(jnp.int32, (PAD, width), 0)
        fac = 1.0 / (1.0 + (index.astype(jnp.float32) + 0.5) / total_rows)
        for c in range(cells):
            w = [[get(v, f, c, r) for f in range(5)] for v in range(2)]
            flows = fluxes(base_ref, c, at, w, (0, 1, 2))
            for f in range(5):
                k = f * span + (c * (rows // PAD) + r // PAD) * 2 * PAD
                for v in range(2):
                    fx[v, f, c, at] = A2 * flows[v][0][f]
                    fr[v, f, c, inside] = A2 * flows[v][1][f]
                    wp[v, f, c, inside] = w[v][f]
                split([flows[v][2][f] * fac for v in range(2)], k, slice(0, width))
                split([w[v][f] for v in range(2)], k, slice(width, 2 * width))
    both = jnp.dot(xh[...], tab_ref[...], preferred_element_type=jnp.float32)
    low = jnp.dot(xl[...], tab_ref[:, 0:width], preferred_element_type=jnp.float32)
    ys[...] = (both[:, 0:width] + both[:, width:]) + low
    for f in range(5):
        for v in range(2):
            for r in range(0, rows, PAD):
                at = slice(r, r + PAD)
                ws = [wp[v, f, c, PAD + r : 2 * PAD + r] for c in range(cells)]
                fs = [fx[v, f, c, at] for c in range(cells)]
                small = [B2 * w for w in ws]
                far_left = [a - b for a, b in zip(fs, small)]
                far_right = [-a - b for a, b in zip(fs, small)]
                large, steep = [16.0 * b for b in small], [8.0 * a for a in fs]
                left = [b - a for a, b in zip(steep, large)]
                right = [b + a for a, b in zip(steep, large)]

                def stream(i):
                    total = None
                    for k, terms in ((1, right), (-1, left), (2, far_right), (-2, far_left)):
                        if 0 <= i + k < cells:
                            total = terms[i + k] if total is None else total + terms[i + k]
                    return total

                for j in range(2 if xp_ref is not None else 0):
                    low_face = dt * stream(j - 2)
                    high_face = dt * stream(cells + j)
                    xp_ref[v, f, j, at] = jnp.where(parity == 0, high_face, low_face)
                    if xd_ref is not None:
                        xd_ref[v, f, j, at] = jnp.where(parity == 0, low_face, high_face)
                for c in range(cells):
                    k = f * span + (c * (rows // PAD) + r // PAD) * 2 * PAD + PAD * v
                    total = stream(c) + radial(fr, wp, v, f, c, r, PAD) + CENTRE * ws[c] + ys[k : k + PAD]
                    put(v, f, c, at, start(v, f, c, r) + dt * total)
    if rp_ref is not None:
        put_edges(dt, line, fr, wp, rp_ref, rd_ref)


def add_edges(line, rp_ref, rd_ref, out, cells):
    rows = out.shape[3]
    for v in range(2):
        for f in range(5):
            for c, place in cells:
                k = 2 * ((5 * v + f) * 4 + c)
                if not isinstance(c, int):
                    k = pl.multiple_of(k, 2)
                rp, rd = rp_ref[pl.ds(k, 2)], rd_ref[pl.ds(k, 2)]
                out[v, f, place, 0:2] += jnp.where(line == 0, rd, rp)
                out[v, f, place, rows - 2 : rows] += jnp.where(line == 0, rp, rd)


def add_faces(parity, xp_ref, xd, out):
    cells = out.shape[2]
    for v in range(2):
        for f in range(5):
            for j in range(2):
                out[v, f, (cells - 2) * (1 - parity) + j] += xp_ref[v, f, j]
                out[v, f, (cells - 2) * parity + j] += xd(v, f, j)


def all_cells(fn):
    for v in range(2):
        for f in range(5):
            for c in range(4):
                fn(v, f, c)


def pick(which, first_ref, second_ref):
    return lambda *at: jnp.where(which == 0, first_ref[at], second_ref[at])


def z_side():
    return (lax.axis_index("gx") // 2 + lax.axis_index("gx")) % 2


def place():
    column = lax.axis_index("gx") % 2
    return column, (column + lax.axis_index("row")) % 2


def load_kernel(w_hbm, rho_hbm, vel_hbm, pr_hbm, tab_hbm,
                own_ref, other_ref, outer_ref, base_ref, send_ref, rest_ref, tab_ref, sems):
    column, half = place()
    outer, inner = pl.ds(2 * column, 2), pl.ds(2 - 2 * column, 2)
    side = 1 - half
    pairs = []
    for v in range(2):
        for f in range(5):
            k = 2 * (5 * v + f)
            pairs.append((w_hbm.at[v, f, outer, side], outer_ref.at[k : k + 2]))
            pairs.append((w_hbm.at[v, f, inner, side], rest_ref.at[14 + k : 16 + k]))
    for ref, first, cells in ((outer_ref, 20, outer), (rest_ref, 0, inner)):
        pairs.append((rho_hbm.at[cells, side], ref.at[first : first + 2]))
        pairs.append((vel_hbm.at[0, cells, side], ref.at[first + 2 : first + 4]))
        pairs.append((pr_hbm.at[cells, side], ref.at[first + 4 : first + 6]))
    pairs.append((vel_hbm.at[1, :, side], rest_ref.at[6:10]))
    pairs.append((vel_hbm.at[2, :, side], rest_ref.at[10:14]))
    for part, ref in ((half, base_ref), (side, send_ref)):
        pairs.append((rho_hbm.at[:, part], ref.at[0]))
        pairs.append((vel_hbm.at[:, :, part], ref.at[1:4]))
        pairs.append((pr_hbm.at[:, part], ref.at[4]))
    pairs.append((w_hbm.at[:, :, :, half], own_ref))
    pairs.append((w_hbm.at[:, :, :, side], other_ref))
    pairs.append((tab_hbm, tab_ref))
    copies = [pltpu.make_async_copy(a, b, sems.at[i]) for i, (a, b) in enumerate(pairs)]
    for copy in copies:
        copy.start()
    for copy in copies:
        copy.wait()


def own_first_kernel(own_ref, other_ref, base_ref, send_ref, tab_ref,
                     part_ref, xp_ref, xd_ref, rp_ref, rd_ref, rpo_ref, rdo_ref, wp, fr, *scratch):
    *scratch, rd_own, rd_other = scratch
    column, half = place()
    _, cells, rows, _ = base_ref.shape
    get = lambda v, f, c, r: own_ref[v, f, c, r : r + PAD]

    def put(v, f, c, at, value):
        part_ref[v, f, c, at] = value

    section(0.5 * time_step, column, half, half, get, get, base_ref, tab_ref, put,
            xp_ref, xd_ref, rp_ref, rd_own, wp, fr, *scratch)
    for c in range(cells):
        for r in (0, rows - PAD):
            w = [[other_ref[v, f, c, r : r + PAD] for f in range(5)] for v in range(2)]
            flows = fluxes(send_ref, c, slice(r, r + PAD), w, (1,))
            for v in range(2):
                for f in range(5):
                    fr[v, f, c, PAD + r : 2 * PAD + r] = A2 * flows[v][0][f]
                    wp[v, f, c, PAD + r : 2 * PAD + r] = w[v][f]
    put_edges(0.5 * time_step, 1 - half, fr, wp, rpo_ref, rd_other)
    rd_ref[...] = jnp.where(column == 0, rd_other[...], rd_own[...])
    rdo_ref[...] = jnp.where(column == 0, rd_own[...], rd_other[...])


def pair_face(dt, high_side, v, w, base, put):
    flows = []
    for j in range(2):
        rho, speed, pr = base[j]
        flow = [speed * w[j][f] for f in range(5)]
        flow[1] = flow[1] + (rho * w[j][0] + gamma_ratio * pr * w[j][4])
        flow[4] = flow[4] + w[j][1] / rho
        flows.append(flow)
    for f in range(5):
        f0, f1, w0, w1 = flows[0][f], flows[1][f], w[0][f], w[1][f]
        low = (-A2 * f0 - B2 * w0, (A1 * f0 + B1 * w0) + (-A2 * f1 - B2 * w1))
        high = ((-A1 * f1 + B1 * w1) + (A2 * f0 - B2 * w0), A2 * f1 - B2 * w1)
        for j in range(2):
            put(v, f, j, dt * jnp.where(high_side, high[j], low[j]))


def face_kernel(outer_ref, own_ref, _, first_ref, second_ref):
    column, _ = place()
    rows = outer_ref.shape[1]
    for r in range(0, rows, PAD):
        at = slice(r, r + PAD)
        base = [[outer_ref[20 + 2 * i + j, at] for i in range(3)] for j in range(2)]

        def put(v, f, j, value):
            own = own_ref[v, f, j, at]
            first_ref[v, f, j, at] = jnp.where(z_side() == 0, value, own)
            second_ref[v, f, j, at] = jnp.where(z_side() == 0, own, value)

        for v in range(2):
            w = [[outer_ref[2 * (5 * v + f) + j, at] for f in range(5)] for j in range(2)]
            pair_face(0.5 * time_step, column == 0, v, w, base, put)


def second_face(parity, outer, part_ref, x_in, rp_in, rd_in, base_ref, put, s2):
    _, half = place()
    first = 2 * parity if outer else 2 - 2 * parity
    rows = part_ref.shape[3]
    for v in range(2):
        for f in range(5):
            for j in range(2):
                s2[v, f, j] = part_ref[v, f, first + j] + x_in(v, f, j)
    add_edges(half, rp_in, rd_in, s2, [(first + j, j) for j in range(2)])
    for r in range(0, rows, PAD):
        at = slice(r, r + PAD)
        base = [[base_ref[i, first + j, at] for i in (0, 1, 4)] for j in range(2)]
        for v in range(2):
            w = [[s2[v, f, j, at] for f in range(5)] for j in range(2)]
            pair_face(time_step, (parity == 1) if outer else (parity == 0), v, w, base,
                      lambda v, f, j, value: put(v, f, j, at, value))


def outer_faces_kernel(part_own, part_par, first_in, second_in, rp_own, rd_own, message_in, base_own, base_par,
                       first_ref, second_ref, s2, face):
    column, _ = place()
    side = z_side()
    edge = rp_own.shape[0]

    def keep(v, f, j, at, value):
        face[v, f, j, at] = value

    def put(v, f, j, at, value):
        own = face[v, f, j, at]
        first_ref[v, f, j, at] = jnp.where(side == 0, value, own)
        second_ref[v, f, j, at] = jnp.where(side == 0, own, value)

    second_face(column, True, part_own, pick(side, second_in, first_in), rp_own, rd_own, base_own, keep, s2)
    second_face(1 - column, True, part_par, pick(side, first_in, second_in), message_in.at[0:edge],
                message_in.at[edge : 2 * edge], base_par, put, s2)


def pack_kernel(rp_ref, first_ref, second_ref, message_ref, rd_ref):
    column, _ = place()
    edge = rp_ref.shape[0]
    message_ref[0:edge] = rp_ref[...]
    message_ref[edge : 2 * edge] = jnp.where(column == 0, first_ref[...], second_ref[...])
    rd_ref[...] = jnp.where(column == 0, second_ref[...], first_ref[...])


def partner_first_kernel(outer_ref, rest_ref, tab_ref, w_ref, base_ref, part_ref, xp_ref, *scratch):
    column, half = place()
    parity = 1 - column
    first, second = 2 * parity, 2 - 2 * parity
    for j in range(2):
        for v in range(2):
            for f in range(5):
                k = 2 * (5 * v + f) + j
                w_ref[v, f, first + j] = outer_ref[k]
                w_ref[v, f, second + j] = rest_ref[14 + k]
        for i, field in enumerate((0, 1, 4)):
            base_ref[field, first + j] = outer_ref[20 + 2 * i + j]
            base_ref[field, second + j] = rest_ref[2 * i + j]
    for c in range(4):
        base_ref[2, c] = rest_ref[6 + c]
        base_ref[3, c] = rest_ref[10 + c]
    get = lambda v, f, c, r: w_ref[v, f, c, r : r + PAD]

    def put(v, f, c, at, value):
        part_ref[v, f, c, at] = value

    section(0.5 * time_step, parity, half, half, get, get, base_ref, tab_ref, put,
            xp_ref, None, None, None, *scratch)


def start_second(parity, half, part_ref, xp_in, xd, rp_in, rd_in, s1):
    def fill(v, f, c):
        s1[v, f, c] = part_ref[v, f, c]

    all_cells(fill)
    add_faces(parity, xp_in, xd, s1)
    add_edges(half, rp_in, rd_in, s1, [(c, c) for c in range(4)])


def own_second_kernel(w_ref, part_ref, xp_in, first_in, second_in, rp_in, rd_in, base_ref, tab_ref, _,
                      out_ref, rp_ref, rd_ref, *scratch):
    *scratch, s1 = scratch
    column, half = place()
    start_second(column, half, part_ref, xp_in, pick(z_side(), second_in, first_in), rp_in, rd_in, s1)
    get = lambda v, f, c, r: s1[v, f, c, r : r + PAD]
    start = lambda v, f, c, r: w_ref[v, f, c, r : r + PAD]

    def put(v, f, c, at, value):
        out_ref[v, f, c, at] = value

    section(time_step, column, half, half, get, start, base_ref, tab_ref, put,
            None, None, rp_ref, rd_ref, *scratch)


def partner_second_kernel(w_ref, part_ref, xp_in, first_in, second_in, message_in, part_own, xp_par, rp_own, rd_own, base_own,
                          base_ref, tab_ref, message_ref, outer_ref, xp_ref, rd_ref, *scratch):
    *scratch, s1, target, s2, xp_own = scratch
    column, half = place()

    def keep(v, f, j, at, value):
        xp_own[v, f, j, at] = value

    second_face(column, False, part_own, lambda *at: xp_par[at], rp_own, rd_own, base_own, keep, s2)
    parity = 1 - column
    rows = outer_ref.shape[3]
    n = 20 * rows
    edge = rd_ref.shape[0]
    start_second(parity, half, part_ref, xp_in, pick(z_side(), first_in, second_in), message_in.at[0:edge], message_in.at[edge : 2 * edge], s1)
    get = lambda v, f, c, r: s1[v, f, c, r : r + PAD]
    start = lambda v, f, c, r: w_ref[v, f, c, r : r + PAD]

    def put(v, f, c, at, value):
        target[v, f, c, at] = value

    section(time_step, parity, half, half, get, start, base_ref, tab_ref, put,
            xp_ref, None, message_ref.at[n : n + edge], rd_ref, *scratch)
    for v in range(2):
        for f in range(5):
            for j in range(2):
                k = ((5 * v + f) * 2 + j) * rows
                message_ref[k : k + rows] = target[v, f, 2 - 2 * parity + j] + xp_own[v, f, j]
                outer_ref[v, f, j] = target[v, f, 2 * parity + j]


def finish_kernel(outer_ref, first_in, second_in, message_ref):
    message_ref[...] = outer_ref[...] + jnp.where(z_side() == 0, first_in[...], second_in[...])


def own_last_kernel(part_ref, xp_ref, first_in, second_in, message_ref, rd_ref, out_hbm, value, sem):
    column, half = place()
    edge = rd_ref.shape[0]
    n = message_ref.shape[0] - edge
    start_second(column, half, part_ref, xp_ref, pick(z_side(), second_in, first_in), message_ref.at[n : n + edge],
                 rd_ref, value)
    copy = pltpu.make_async_copy(value, out_hbm.at[:, :, :, half], sem)
    copy.start()
    copy.wait()


def other_last_kernel(inner_ref, outer_ref, rp_ref, rd_ref, _, out_hbm, value, sem):
    column, half = place()
    rows = value.shape[3]
    for v in range(2):
        for f in range(5):
            for j in range(2):
                k = ((5 * v + f) * 2 + j) * rows
                value[v, f, 2 * column + j] = outer_ref[v, f, j]
                value[v, f, 2 - 2 * column + j] = inner_ref[k : k + rows]
    add_edges(1 - half, rp_ref, rd_ref, value, [(c, c) for c in range(4)])
    copy = pltpu.make_async_copy(value, out_hbm.at[:, :, :, 1 - half], sem)
    copy.start()
    copy.wait()


VM = pl.BlockSpec(memory_space=pltpu.VMEM)
HB = pl.BlockSpec(memory_space=pltpu.HBM)
PARAMS = pltpu.CompilerParams(vmem_limit_bytes=40 << 20)


def local(adjoint_vectors, base_density, base_velocity, base_pressure):
    vectors, fields, cells, both, width = adjoint_vectors.shape
    rows = both // 2
    if cells != 4 or vectors != 2 or rows % PAD:
        raise ValueError("unexpected block")
    f32 = jnp.float32
    shape = lambda *s: jax.ShapeDtypeStruct(s, f32)
    tab = jnp.asarray(theta_table(width))
    block, pair = shape(2, 5, cells, rows, width), shape(2, 5, 2, rows, width)
    base, edge = shape(5, cells, rows, width), shape(20 * cells, width)
    halves = lambda a: a.reshape(a.shape[:-2] + (2, rows, width))
    scratch = [
        pltpu.VMEM((2, 5, cells, rows + 2 * PAD, width), f32),
        pltpu.VMEM((2, 5, cells, rows + 2 * PAD, width), f32),
        pltpu.VMEM((2, 5, cells, rows, width), f32),
        pltpu.VMEM((10 * cells * rows, 2 * width), jnp.bfloat16),
        pltpu.VMEM((10 * cells * rows, 2 * width), jnp.bfloat16),
        pltpu.VMEM((10 * cells * rows, width), f32),
    ]
    whole = pltpu.VMEM((2, 5, cells, rows, width), f32)

    gx, row = lax.axis_size("gx"), lax.axis_size("row")
    partner = [(g, g + 1 - 2 * (g % 2)) for g in range(gx)]
    trade = lambda value: lax.ppermute(value, "gx", partner)

    def swaps(axis, apart):
        size = lax.axis_size(axis)
        found = ([], [])
        for i in range(size - apart):
            found[(i // apart) % 2].extend([(i, i + apart), (i + apart, i)])
        return found

    z_swaps, row_swaps = swaps("gx", 2), swaps("row", 1)

    def swap_both(pairs, axis, first, second):
        return lax.ppermute(first, axis, pairs[0]), lax.ppermute(second, axis, pairs[1])

    def beside(value, cross, flip):
        perm = []
        for g in range(gx):
            for j in range(row):
                side = (g + j + flip) % 2
                k = j - 1 + 2 * side
                if 0 <= k < row:
                    perm.append((g * row + j, (partner[g][1] if cross else g) * row + k))
        return lax.ppermute(value, ("gx", "row"), perm)

    def call(kernel, name, outs, ins, extra=(), **more):
        return pl.pallas_call(
            kernel, name=name, out_shape=outs, in_specs=[VM] * len(ins), out_specs=[VM] * len(outs),
            scratch_shapes=list(scratch) + list(extra), compiler_params=PARAMS, **more,
        )(*ins)

    hbm = lambda a: pltpu.with_memory_space_constraint(a, pltpu.HBM)
    small = lambda kernel, name, outs, *ins, extra=(): pl.pallas_call(
        kernel, name=name, out_shape=outs, in_specs=[VM] * len(ins),
        out_specs=[VM] * len(outs) if isinstance(outs, list) else VM, scratch_shapes=extra, compiler_params=PARAMS)(*ins)
    duo = pltpu.VMEM(pair.shape, f32)
    n, e = 20 * rows, 20 * cells
    own, other, outer, base_own, base_send, rest, table = pl.pallas_call(
        load_kernel, name="load",
        out_shape=[block, block, shape(26, rows, width), base, base, shape(34, rows, width),
                   jax.ShapeDtypeStruct(tab.shape, tab.dtype)],
        in_specs=[HB] * 5, out_specs=[VM] * 7, scratch_shapes=[pltpu.SemaphoreType.DMA((37,))],
        compiler_params=PARAMS,
    )(hbm(halves(adjoint_vectors)), hbm(halves(base_density)), hbm(halves(base_velocity)),
      hbm(halves(base_pressure)), hbm(tab))
    outer, rest = trade(outer), trade(rest)
    part_own, xp_own, xd_own, rp_own, first, rp_other, second = call(
        own_first_kernel, "own_1", [block, pair, pair, edge, edge, edge, edge],
        (own, other, base_own, base_send, table), (pltpu.VMEM(edge.shape, f32), pltpu.VMEM(edge.shape, f32)))
    message, rd_own_in = small(
        pack_kernel, "pack", [shape(2 * e, width), edge], rp_own, *swap_both(row_swaps, "row", first, second))
    faces = swap_both(z_swaps, "gx", *small(face_kernel, "face", [pair, pair], outer, xd_own, message))
    message = trade(message)
    w_par, base_par, part_par, xp_par = call(
        partner_first_kernel, "partner_1", [block, base, block, pair], (outer, rest, table))
    faces2 = swap_both(z_swaps, "gx", *small(
        outer_faces_kernel, "outer_faces", [pair, pair], part_own, part_par, *faces, rp_other, rd_own_in, message,
        base_own, base_par, extra=[duo, duo]))
    inner, outer, xp_par2, rd_par = call(
        partner_second_kernel, "partner_2", [shape(n + e, width), pair, pair, edge],
        (w_par, part_par, xp_own, *faces, message, part_own, xp_par, rp_other, rd_own_in, base_own, base_par, table),
        (whole, whole, duo, duo))
    inner = trade(inner)
    outer = small(finish_kernel, "finish", pair, outer, *faces2)
    part_own, rp_own, rd_own = call(
        own_second_kernel, "own_2", [block, edge, edge],
        (own, part_own, xp_par, *faces, rp_other, rd_own_in, base_own, table, outer), (whole,))
    outer = trade(outer)
    rd_other_in = beside(rd_par, True, 0)
    rd_own_in = beside(rd_own, False, 0)
    xp_par = xp_par2
    full = shape(2, 5, cells, 2, rows, width)
    last = dict(out_shape=full, out_specs=HB, scratch_shapes=[whole, pltpu.SemaphoreType.DMA], compiler_params=PARAMS)
    out = pl.pallas_call(own_last_kernel, name="own_3", in_specs=[VM] * 6, **last)(
        part_own, xp_par, *faces2, inner, rd_own_in)
    out = pl.pallas_call(
        other_last_kernel, name="other_3", in_specs=[VM] * 4 + [HB], input_output_aliases={4: 0}, **last,
    )(inner, outer, rp_own, rd_other_in, out)
    return out.reshape(adjoint_vectors.shape)


def solution(mesh):
    in_specs = (
        P(None, None, "gx", "row", None),
        P("gx", "row", None),
        P(None, "gx", "row", None),
        P("gx", "row", None),
    )
    out_specs = P(None, None, "gx", "row", None)
    return jax.shard_map(local, mesh=mesh, in_specs=in_specs, out_specs=out_specs, check_vma=False)
```

time: 47.1 us -> 45.7 us (0.970)
  the two profiles are of different devices: /device:TPU:1 before, /device:TPU:17 now
where the time goes in v5:
time: 45.7 us; the launch traced here: 45.5 us
  starting transfers between devices  24.1 us (53%)
  waiting for transfers between devices  10.7 us (23%)
  Pallas kernels  10.5 us (23%)
    ppermute x2, starting transfers between devices, beside(): return lax.ppermute(value, ('gx', 'row'), perm)  8.3 us
    ppermute x3, starting transfers between devices, swap_both(): lax.ppermute(second, axis, pairs[1])  6.86 us
    pallas_call x4, Pallas kernels, call(): pl.pallas_call(kernel, name=name, out_shape=outs, in_specs=[VM] * len(ins...  6.07 us
    ppermute x5, starting transfers between devices, local(): trade = lambda value: lax.ppermute(value, 'gx', partner)  5.32 us
    ppermute x3, waiting for transfers between devices, swap_both(): lax.ppermute(second, axis, pairs[1])  5.13 us
    ppermute x3, starting transfers between devices, swap_both(): lax.ppermute(first, axis, pairs[0])  3.64 us
    ppermute x5, waiting for transfers between devices, local(): trade = lambda value: lax.ppermute(value, 'gx', partner)  3.21 us
    ppermute x2, waiting for transfers between devices, beside(): return lax.ppermute(value, ('gx', 'row'), perm)  2.39 us
  transfers between devices with their start and end apart: 13, of which 6 were waited for; matrix products, arithmetic and copies ran while one was open for 0% of the time, Pallas kernels for 16%

profile of v5, /device:TPU:17, one launch (start us, length us, event | category | flops | bytes accessed | tf_op | source)
XLA Modules:
  0.0 45.5 jit_solution(15687461823593251939)
XLA Ops:
  0.0 2.0 %load.1 = (f32[2,5,4,24,128]{4,3,2,1,0:T(8,128)S(1)}, f32[2,5,4,24,128]{4,3,2,1,0:T(8,128)S(1)}, f32[26,24,128]{2,1,0:T(8,128)S(1)}, f32[5,4,24,128]{3,2,1,0:T(8...) custom-call(f32[2,5,4,2,24,128]{5,4,3,2,1,0:T(8,128)} %bitcast.5, ...), custom_call_target="tpu_custom_call" | custom-call | tf_op jit(solution)/shard_map/load/pallas_call | solution.py:507
  2.0 1.3 %collective-permute-start = (f32[26,24,128]{2,1,0:T(8,128)S(1)}, f32[26,24,128]{2,1,0:T(8,128)S(1)}, u32[]{:S(2)}, u32[]{:S(2)}) collective-permute-start(f32[26,24,128]{2,1,0:T(8,128)S(1)} %get-tuple-element.36), channel_id=1, source_target_pairs={{0,4},{4,0},{8,12},{12,8},{16,20},{20,16},{24,28},{28,24},{1,5},{5... | collective-permute-start | bytes 958472 | tf_op jit(solution)/shard_map/ppermute | solution.py:471
  3.3 0.3 collective-permute-start.1
  3.5 1.6 %own_1.1 = (f32[2,5,4,24,128]{4,3,2,1,0:T(8,128)S(1)}, f32[2,5,2,24,128]{4,3,2,1,0:T(8,128)S(1)}, f32[2,5,2,24,128]{4,3,2,1,0:T(8,128)S(1)}, f32[80,128]{1,0:T(8...) custom-call(f32[2,5,4,24,128]{4,3,2,1,0:T(8,128)S(1)} %get-tuple-element.41.own_ref.w_ref, ...), custom_call_target="tpu_custom_call" | custom-call | tf_op jit(solution)/shard_map/own_1/pallas_call | solution.py:496
  5.2 1.3 %collective-permute-start.2 = (f32[80,128]{1,0:T(8,128)S(1)}, f32[80,128]{1,0:T(8,128)S(1)}, u32[]{:S(2)}, u32[]{:S(2)}) collective-permute-start(f32[80,128]{1,0:T(8,128)S(1)} %get-tuple-element.48), channel_id=1, source_target_pairs={{0,1},{1,0},{2,3},{3,2},{4,5},{5,4},{6,7},{7,6},{8,9},{9,8},{10,11... | collective-permute-start | bytes 122888 | tf_op jit(solution)/shard_map/ppermute | solution.py:483
  6.5 3.0 %collective-permute-start.3 = (f32[80,128]{1,0:T(8,128)S(1)}, f32[80,128]{1,0:T(8,128)S(1)}, u32[]{:S(2)}, u32[]{:S(2)}) collective-permute-start(f32[80,128]{1,0:T(8,128)S(1)} %get-tuple-element.49), channel_id=1, source_target_pairs={{1,2},{2,1},{5,6},{6,5},{9,10},{10,9},{13,14},{14,13},{17,18},{18,... | collective-permute-start | bytes 122888 | tf_op jit(solution)/shard_map/ppermute | solution.py:483
  9.5 0.0 collective-permute-done.2.first_ref
  9.5 2.5 %collective-permute-done.3.second_ref = f32[80,128]{1,0:T(8,128)S(1)} collective-permute-done((f32[80,128]{1,0:T(8,128)S(1)}, f32[80,128]{1,0:T(8,128)S(1)}, u32[]{:S(2)}, u32[]{:S(2)}) %collective-permute-start.3) | collective-permute-done | bytes 40992 | tf_op jit(solution)/shard_map/ppermute | solution.py:483
  12.1 0.0 collective-permute-done.outer_ref
  12.1 0.1 face.1
  12.2 1.4 %collective-permute-start.4 = (f32[2,5,2,24,128]{4,3,2,1,0:T(8,128)S(1)}, f32[2,5,2,24,128]{4,3,2,1,0:T(8,128)S(1)}, u32[]{:S(2)}, u32[]{:S(2)}) collective-permute-start(f32[2,5,2,24,128]{4,3,2,1,0:T(8,128)S(1)} %get-tuple-element.51), channel_id=1, source_target_pairs={{0,8},{8,0},{4,12},{12,4},{16,24},{24,16},{20,28},{28,20},{1,9},{9... | collective-permute-start | bytes 737288 | tf_op jit(solution)/shard_map/ppermute | solution.py:483
  13.6 1.9 %collective-permute-start.5 = (f32[2,5,2,24,128]{4,3,2,1,0:T(8,128)S(1)}, f32[2,5,2,24,128]{4,3,2,1,0:T(8,128)S(1)}, u32[]{:S(2)}, u32[]{:S(2)}) collective-permute-start(f32[2,5,2,24,128]{4,3,2,1,0:T(8,128)S(1)} %get-tuple-element.52), channel_id=1, source_target_pairs={{8,16},{16,8},{12,20},{20,12},{9,17},{17,9},{13,21},{21,13},{10,18... | collective-permute-start | bytes 737288 | tf_op jit(solution)/shard_map/ppermute | solution.py:483
  15.5 1.3 %collective-permute-start.6 = (f32[160,128]{1,0:T(8,128)S(1)}, f32[160,128]{1,0:T(8,128)S(1)}, u32[]{:S(2)}, u32[]{:S(2)}) collective-permute-start(f32[160,128]{1,0:T(8,128)S(1)} %get-tuple-element.50._), channel_id=1, source_target_pairs={{0,4},{4,0},{8,12},{12,8},{16,20},{20,16},{24,28},{28,24},{1,5},{5... | collective-permute-start | bytes 245768 | tf_op jit(solution)/shard_map/ppermute | solution.py:471
  16.8 2.6 %collective-permute-done.1.rest_ref = f32[34,24,128]{2,1,0:T(8,128)S(1)} collective-permute-done((f32[34,24,128]{2,1,0:T(8,128)S(1)}, f32[34,24,128]{2,1,0:T(8,128)S(1)}, u32[]{:S(2)}, u32[]{:S(2)}) %collective-permute-start.1) | collective-permute-done | bytes 417824 | tf_op jit(solution)/shard_map/ppermute | solution.py:471
  19.4 1.2 %partner_1.1 = (f32[2,5,4,24,128]{4,3,2,1,0:T(8,128)S(1)}, f32[5,4,24,128]{3,2,1,0:T(8,128)S(1)}, f32[2,5,4,24,128]{4,3,2,1,0:T(8,128)S(1)}, f32[2,5,2,24,128]{4,3,2,1,0:T(8,128)S(1)}) custom-call(f32[26,24,128]{2,1,0:T(8,128)S(1)} %collective-permute-done.outer_ref, f32[34,24,128]{2,1,0:T(8,128)S(1)} %collective-permute-done.1.rest_ref, ...), custom_call_target="tpu_custom_call" | custom-call | tf_op jit(solution)/shard_map/partner_1/pallas_call | solution.py:496
  20.6 0.6 %collective-permute-done.6.message_in = f32[160,128]{1,0:T(8,128)S(1)} collective-permute-done((f32[160,128]{1,0:T(8,128)S(1)}, f32[160,128]{1,0:T(8,128)S(1)}, u32[]{:S(2)}, u32[]{:S(2)}) %collective-permute-start.6) | collective-permute-done | bytes 81952 | tf_op jit(solution)/shard_map/ppermute | solution.py:471
  21.2 0.0 collective-permute-done.4.first_in
  21.2 0.4 collective-permute-done.5.second_in
  21.6 0.4 outer_faces.1
  22.0 1.0 %collective-permute-start.8 = (f32[2,5,2,24,128]{4,3,2,1,0:T(8,128)S(1)}, f32[2,5,2,24,128]{4,3,2,1,0:T(8,128)S(1)}, u32[]{:S(2)}, u32[]{:S(2)}) collective-permute-start(f32[2,5,2,24,128]{4,3,2,1,0:T(8,128)S(1)} %get-tuple-element.60), channel_id=1, source_target_pairs={{0,8},{8,0},{4,12},{12,4},{16,24},{24,16},{20,28},{28,20},{1,9},{9... | collective-permute-start | bytes 737288 | tf_op jit(solution)/shard_map/ppermute | solution.py:483
  22.9 1.9 %collective-permute-start.9 = (f32[2,5,2,24,128]{4,3,2,1,0:T(8,128)S(1)}, f32[2,5,2,24,128]{4,3,2,1,0:T(8,128)S(1)}, u32[]{:S(2)}, u32[]{:S(2)}) collective-permute-start(f32[2,5,2,24,128]{4,3,2,1,0:T(8,128)S(1)} %get-tuple-element.61), channel_id=1, source_target_pairs={{8,16},{16,8},{12,20},{20,12},{9,17},{17,9},{13,21},{21,13},{10,18... | collective-permute-start | bytes 737288 | tf_op jit(solution)/shard_map/ppermute | solution.py:483
  24.9 1.8 %partner_2.1 = (f32[560,128]{1,0:T(8,128)S(1)}, f32[2,5,2,24,128]{4,3,2,1,0:T(8,128)S(1)}, f32[2,5,2,24,128]{4,3,2,1,0:T(8,128)S(1)}, f32[80,128]{1,0:T(8,128)S(1)}) custom-call(f32[2,5,4,24,128]{4,3,2,1,0:T(8,128)S(1)} %get-tuple-element.39.w_ref, f32[2,5,4,24,128]{4,3,2,1,0:T(8,128)S(1)} %get-tuple-element.40.part_ref.part_par, ...), custom_call_target="tpu_custom_call" | custom-call | tf_op jit(solution)/shard_map/partner_2/pallas_call | solution.py:496
  26.7 1.2 %collective-permute-start.7 = (f32[560,128]{1,0:T(8,128)S(1)}, f32[560,128]{1,0:T(8,128)S(1)}, u32[]{:S(2)}, u32[]{:S(2)}) collective-permute-start(f32[560,128]{1,0:T(8,128)S(1)} %get-tuple-element.58), channel_id=1, source_target_pairs={{0,4},{4,0},{8,12},{12,8},{16,20},{20,16},{24,28},{28,24},{1,5},{5... | collective-permute-start | bytes 860168 | tf_op jit(solution)/shard_map/ppermute | solution.py:471
  27.9 0.0 collective-permute-done.8.first_in
  27.9 2.2 %collective-permute-done.9.second_in = f32[2,5,2,24,128]{4,3,2,1,0:T(8,128)S(1)} collective-permute-done((f32[2,5,2,24,128]{4,3,2,1,0:T(8,128)S(1)}, f32[2,5,2,24,128]{4,3,2,1,0:T(8,128)S(1)}, u32[]{:S(2)}, u32[]{:S(2)}) %collective-permute-start.9) | collective-permute-done | bytes 245792 | tf_op jit(solution)/shard_map/ppermute | solution.py:483
  30.1 1.3 %collective-permute-start.10 = (f32[2,5,2,24,128]{4,3,2,1,0:T(8,128)S(1)}, f32[2,5,2,24,128]{4,3,2,1,0:T(8,128)S(1)}, u32[]{:S(2)}, u32[]{:S(2)}) collective-permute-start(f32[2,5,2,24,128]{4,3,2,1,0:T(8,128)S(1)} %finish.1._), channel_id=1, source_target_pairs={{0,4},{4,0},{8,12},{12,8},{16,20},{20,16},{24,28},{28,24},{1,5},{5... | collective-permute-start | bytes 737288 | tf_op jit(solution)/shard_map/ppermute | solution.py:471
  31.4 1.5 %own_2.1 = (f32[2,5,4,24,128]{4,3,2,1,0:T(8,128)S(1)}, f32[80,128]{1,0:T(8,128)S(1)}, f32[80,128]{1,0:T(8,128)S(1)}) custom-call(f32[2,5,4,24,128]{4,3,2,1,0:T(8,128)S(1)} %get-tuple-element.41.own_ref.w_ref, f32[2,5,4,24,128]{4,3,2,1,0:T(8,128)S(1)} %get-tuple-element.53.part_own.part_ref, f32[2,5,2,24,128]{4,3,2,1,0:T(8,128)S(1)} %get-tuple-element.54.xp_par.xp_in, ...), custom_call_target="tpu_custom_call" | custom-call | tf_op jit(solution)/shard_map/own_2/pallas_call | solution.py:496
  32.9 6.4 %collective-permute-start.12 = (f32[80,128]{1,0:T(8,128)S(1)}, f32[80,128]{1,0:T(8,128)S(1)}, u32[]{:S(2)}, u32[]{:S(2)}) collective-permute-start(f32[80,128]{1,0:T(8,128)S(1)} %get-tuple-element.66), channel_id=1, source_target_pairs={{1,2},{2,1},{4,5},{5,4},{6,7},{7,6},{9,10},{10,9},{12,13},{13,12},... | collective-permute-start | bytes 122888 | tf_op jit(solution)/shard_map/ppermute | solution.py:493
  39.3 1.9 %collective-permute-start.11 = (f32[80,128]{1,0:T(8,128)S(1)}, f32[80,128]{1,0:T(8,128)S(1)}, u32[]{:S(2)}, u32[]{:S(2)}) collective-permute-start(f32[80,128]{1,0:T(8,128)S(1)} %get-tuple-element.63), channel_id=1, source_target_pairs={{1,6},{2,5},{4,1},{5,0},{6,3},{7,2},{9,14},{10,13},{12,9},{13,8},{... | collective-permute-start | bytes 122888 | tf_op jit(solution)/shard_map/ppermute | solution.py:493
  41.2 0.0 collective-permute-done.7.message_ref.inner_ref
  41.2 0.0 collective-permute-done.12.rd_ref
  41.2 1.0 %own_3.1._ = f32[2,5,4,2,24,128]{5,4,3,2,1,0:T(8,128)} custom-call(f32[2,5,4,24,128]{4,3,2,1,0:T(8,128)S(1)} %get-tuple-element.64.part_ref, f32[2,5,2,24,128]{4,3,2,1,0:T(8,128)S(1)} %get-tuple-element.65.xp_ref, f32[2,5,2,24,128]{4,3,2,1,0:T(8,128)S(1)} %collective-permute-done.8.first_in, f32[2,5,2,24,128]{4,3,2,1,0:T(8,128)S(1)} %collective-permute-done.9.second_in, ...), custom_call_target="tpu_custom_call" | custom-call | tf_op jit(solution)/shard_map/own_3/pallas_call | solution.py:543
  42.2 2.4 %collective-permute-done.11.rd_ref = f32[80,128]{1,0:T(8,128)S(1)} collective-permute-done((f32[80,128]{1,0:T(8,128)S(1)}, f32[80,128]{1,0:T(8,128)S(1)}, u32[]{:S(2)}, u32[]{:S(2)}) %collective-permute-start.11) | collective-permute-done | bytes 40992 | tf_op jit(solution)/shard_map/ppermute | solution.py:493
  44.6 0.0 collective-permute-done.10.outer_ref
  44.6 0.9 %other_3.1 = f32[2,5,4,2,24,128]{5,4,3,2,1,0:T(8,128)} custom-call(f32[560,128]{1,0:T(8,128)S(1)} %collective-permute-done.7.message_ref.inner_ref, f32[2,5,2,24,128]{4,3,2,1,0:T(8,128)S(1)} %collective-permute-done.10.outer_ref, f32[80,128]{1,0:T(8,128)S(1)} %get-tuple-element.62.rp_ref, ...), custom_call_target="tpu_custom_call", output_to_operand_aliasing={{}: (4, {})} | custom-call | tf_op jit(solution)/shard_map/other_3/pallas_call | solution.py:545
  (2 shorter events, 0.1 us)
Async XLA Ops:
  2.0 10.1 %collective-permute-start = (f32[26,24,128]{2,1,0:T(8,128)S(1)}, f32[26,24,128]{2,1,0:T(8,128)S(1)}, u32[]{:S(2)}, u32[]{:S(2)}) collective-permute-start(f32[26,24,128]{2,1,0:T(8,128)S(1)} %get-tuple-element.36), channel_id=1, source_target_pairs={{0,4},{4,0},{8,12},{12,8},{16,20},{20,16},{24,28},{28,24},{1,5},{5... | collective-permute-start | bytes 958472 | tf_op jit(solution)/shard_map/ppermute | solution.py:471
  3.3 16.2 %collective-permute-start.1 = (f32[34,24,128]{2,1,0:T(8,128)S(1)}, f32[34,24,128]{2,1,0:T(8,128)S(1)}, u32[]{:S(2)}, u32[]{:S(2)}) collective-permute-start(f32[34,24,128]{2,1,0:T(8,128)S(1)} %get-tuple-element.37), channel_id=1, source_target_pairs={{0,4},{4,0},{8,12},{12,8},{16,20},{20,16},{24,28},{28,24},{1,5},{5... | collective-permute-start | bytes 1253384 | tf_op jit(solution)/shard_map/ppermute | solution.py:471
  5.2 4.3 %collective-permute-start.2 = (f32[80,128]{1,0:T(8,128)S(1)}, f32[80,128]{1,0:T(8,128)S(1)}, u32[]{:S(2)}, u32[]{:S(2)}) collective-permute-start(f32[80,128]{1,0:T(8,128)S(1)} %get-tuple-element.48), channel_id=1, source_target_pairs={{0,1},{1,0},{2,3},{3,2},{4,5},{5,4},{6,7},{7,6},{8,9},{9,8},{10,11... | collective-permute-start | bytes 122888 | tf_op jit(solution)/shard_map/ppermute | solution.py:483
  6.5 5.6 %collective-permute-start.3 = (f32[80,128]{1,0:T(8,128)S(1)}, f32[80,128]{1,0:T(8,128)S(1)}, u32[]{:S(2)}, u32[]{:S(2)}) collective-permute-start(f32[80,128]{1,0:T(8,128)S(1)} %get-tuple-element.49), channel_id=1, source_target_pairs={{1,2},{2,1},{5,6},{6,5},{9,10},{10,9},{13,14},{14,13},{17,18},{18,... | collective-permute-start | bytes 122888 | tf_op jit(solution)/shard_map/ppermute | solution.py:483
  12.2 9.0 %collective-permute-start.4 = (f32[2,5,2,24,128]{4,3,2,1,0:T(8,128)S(1)}, f32[2,5,2,24,128]{4,3,2,1,0:T(8,128)S(1)}, u32[]{:S(2)}, u32[]{:S(2)}) collective-permute-start(f32[2,5,2,24,128]{4,3,2,1,0:T(8,128)S(1)} %get-tuple-element.51), channel_id=1, source_target_pairs={{0,8},{8,0},{4,12},{12,4},{16,24},{24,16},{20,28},{28,20},{1,9},{9... | collective-permute-start | bytes 737288 | tf_op jit(solution)/shard_map/ppermute | solution.py:483
  13.6 8.0 %collective-permute-start.5 = (f32[2,5,2,24,128]{4,3,2,1,0:T(8,128)S(1)}, f32[2,5,2,24,128]{4,3,2,1,0:T(8,128)S(1)}, u32[]{:S(2)}, u32[]{:S(2)}) collective-permute-start(f32[2,5,2,24,128]{4,3,2,1,0:T(8,128)S(1)} %get-tuple-element.52), channel_id=1, source_target_pairs={{8,16},{16,8},{12,20},{20,12},{9,17},{17,9},{13,21},{21,13},{10,18... | collective-permute-start | bytes 737288 | tf_op jit(solution)/shard_map/ppermute | solution.py:483
  15.5 5.7 %collective-permute-start.6 = (f32[160,128]{1,0:T(8,128)S(1)}, f32[160,128]{1,0:T(8,128)S(1)}, u32[]{:S(2)}, u32[]{:S(2)}) collective-permute-start(f32[160,128]{1,0:T(8,128)S(1)} %get-tuple-element.50._), channel_id=1, source_target_pairs={{0,4},{4,0},{8,12},{12,8},{16,20},{20,16},{24,28},{28,24},{1,5},{5... | collective-permute-start | bytes 245768 | tf_op jit(solution)/shard_map/ppermute | solution.py:471
  22.0 5.9 %collective-permute-start.8 = (f32[2,5,2,24,128]{4,3,2,1,0:T(8,128)S(1)}, f32[2,5,2,24,128]{4,3,2,1,0:T(8,128)S(1)}, u32[]{:S(2)}, u32[]{:S(2)}) collective-permute-start(f32[2,5,2,24,128]{4,3,2,1,0:T(8,128)S(1)} %get-tuple-element.60), channel_id=1, source_target_pairs={{0,8},{8,0},{4,12},{12,4},{16,24},{24,16},{20,28},{28,20},{1,9},{9... | collective-permute-start | bytes 737288 | tf_op jit(solution)/shard_map/ppermute | solution.py:483
  22.9 7.1 %collective-permute-start.9 = (f32[2,5,2,24,128]{4,3,2,1,0:T(8,128)S(1)}, f32[2,5,2,24,128]{4,3,2,1,0:T(8,128)S(1)}, u32[]{:S(2)}, u32[]{:S(2)}) collective-permute-start(f32[2,5,2,24,128]{4,3,2,1,0:T(8,128)S(1)} %get-tuple-element.61), channel_id=1, source_target_pairs={{8,16},{16,8},{12,20},{20,12},{9,17},{17,9},{13,21},{21,13},{10,18... | collective-permute-start | bytes 737288 | tf_op jit(solution)/shard_map/ppermute | solution.py:483
  26.7 14.6 %collective-permute-start.7 = (f32[560,128]{1,0:T(8,128)S(1)}, f32[560,128]{1,0:T(8,128)S(1)}, u32[]{:S(2)}, u32[]{:S(2)}) collective-permute-start(f32[560,128]{1,0:T(8,128)S(1)} %get-tuple-element.58), channel_id=1, source_target_pairs={{0,4},{4,0},{8,12},{12,8},{16,20},{20,16},{24,28},{28,24},{1,5},{5... | collective-permute-start | bytes 860168 | tf_op jit(solution)/shard_map/ppermute | solution.py:471
  30.1 14.5 %collective-permute-start.10 = (f32[2,5,2,24,128]{4,3,2,1,0:T(8,128)S(1)}, f32[2,5,2,24,128]{4,3,2,1,0:T(8,128)S(1)}, u32[]{:S(2)}, u32[]{:S(2)}) collective-permute-start(f32[2,5,2,24,128]{4,3,2,1,0:T(8,128)S(1)} %finish.1._), channel_id=1, source_target_pairs={{0,4},{4,0},{8,12},{12,8},{16,20},{20,16},{24,28},{28,24},{1,5},{5... | collective-permute-start | bytes 737288 | tf_op jit(solution)/shard_map/ppermute | solution.py:471
  32.9 8.3 %collective-permute-start.12 = (f32[80,128]{1,0:T(8,128)S(1)}, f32[80,128]{1,0:T(8,128)S(1)}, u32[]{:S(2)}, u32[]{:S(2)}) collective-permute-start(f32[80,128]{1,0:T(8,128)S(1)} %get-tuple-element.66), channel_id=1, source_target_pairs={{1,2},{2,1},{4,5},{5,4},{6,7},{7,6},{9,10},{10,9},{12,13},{13,12},... | collective-permute-start | bytes 122888 | tf_op jit(solution)/shard_map/ppermute | solution.py:493
  39.3 5.3 %collective-permute-start.11 = (f32[80,128]{1,0:T(8,128)S(1)}, f32[80,128]{1,0:T(8,128)S(1)}, u32[]{:S(2)}, u32[]{:S(2)}) collective-permute-start(f32[80,128]{1,0:T(8,128)S(1)} %get-tuple-element.63), channel_id=1, source_target_pairs={{1,6},{2,5},{4,1},{5,0},{6,3},{7,2},{9,14},{10,13},{12,9},{13,8},{... | collective-permute-start | bytes 122888 | tf_op jit(solution)/shard_map/ppermute | solution.py:493

commit v6 on v5

--- a/solution.py
+++ b/solution.py
@@ -410,7 +410,7 @@
                 outer_ref[v, f, j] = target[v, f, 2 * parity + j]
 
 
-def finish_kernel(outer_ref, first_in, second_in, message_ref):
+def finish_kernel(outer_ref, first_in, second_in, _, message_ref):
     message_ref[...] = outer_ref[...] + jnp.where(z_side() == 0, first_in[...], second_in[...])
 
 
@@ -530,10 +530,10 @@
         (w_par, part_par, xp_own, *faces, message, part_own, xp_par, rp_other, rd_own_in, base_own, base_par, table),
         (whole, whole, duo, duo))
     inner = trade(inner)
-    outer = small(finish_kernel, "finish", pair, outer, *faces2)
     part_own, rp_own, rd_own = call(
         own_second_kernel, "own_2", [block, edge, edge],
-        (own, part_own, xp_par, *faces, rp_other, rd_own_in, base_own, table, outer), (whole,))
+        (own, part_own, xp_par, *faces, rp_other, rd_own_in, base_own, table, rd_par), (whole,))
+    outer = small(finish_kernel, "finish", pair, outer, *faces2, rd_own)
     outer = trade(outer)
     rd_other_in = beside(rd_par, True, 0)
     rd_own_in = beside(rd_own, False, 0)

time: 45.7 us -> 44.3 us (0.969)
  waiting for transfers between devices: 10.7 us -> 9.28 us
    ppermute x3, waiting for transfers between devices: 5.13 us -> 3.67 us  [swap_both(): lax.ppermute(second, axis, pairs[1])]
  transfers between devices with their start and end apart: 13 -> 13, of which waited for: 6 -> 6; matrix products, arithmetic and copies ran while one was open for 0% -> 0% of each run, Pallas kernels for 16% -> 17%
where the time goes in v6:
time: 44.3 us; the launch traced here: 44 us
  starting transfers between devices  24.1 us (54%)
  Pallas kernels  10.5 us (24%)
  waiting for transfers between devices  9.28 us (21%)
    ppermute x2, starting transfers between devices, beside(): return lax.ppermute(value, ('gx', 'row'), perm)  8.3 us
    ppermute x3, starting transfers between devices, swap_both(): lax.ppermute(second, axis, pairs[1])  6.86 us
    pallas_call x4, Pallas kernels, call(): pl.pallas_call(kernel, name=name, out_shape=outs, in_specs=[VM] * len(ins...  6.1 us
    ppermute x5, starting transfers between devices, local(): trade = lambda value: lax.ppermute(value, 'gx', partner)  5.33 us
    ppermute x3, waiting for transfers between devices, swap_both(): lax.ppermute(second, axis, pairs[1])  3.67 us
    ppermute x3, starting transfers between devices, swap_both(): lax.ppermute(first, axis, pairs[0])  3.62 us
    ppermute x5, waiting for transfers between devices, local(): trade = lambda value: lax.ppermute(value, 'gx', partner)  3.19 us
    ppermute x2, waiting for transfers between devices, beside(): return lax.ppermute(value, ('gx', 'row'), perm)  2.41 us
  transfers between devices with their start and end apart: 13, of which 6 were waited for; matrix products, arithmetic and copies ran while one was open for 0% of the time, Pallas kernels for 17%

profile of v6, /device:TPU:17, one launch (start us, length us, event | category | flops | bytes accessed | tf_op | source)
XLA Modules:
  0.0 44.0 jit_solution(6145198821895522055)
XLA Ops:
  0.0 2.0 %load.1 = (f32[2,5,4,24,128]{4,3,2,1,0:T(8,128)S(1)}, f32[2,5,4,24,128]{4,3,2,1,0:T(8,128)S(1)}, f32[26,24,128]{2,1,0:T(8,128)S(1)}, f32[5,4,24,128]{3,2,1,0:T(8...) custom-call(f32[2,5,4,2,24,128]{5,4,3,2,1,0:T(8,128)} %bitcast.5, ...), custom_call_target="tpu_custom_call" | custom-call | tf_op jit(solution)/shard_map/load/pallas_call | solution.py:507
  2.0 1.3 %collective-permute-start = (f32[26,24,128]{2,1,0:T(8,128)S(1)}, f32[26,24,128]{2,1,0:T(8,128)S(1)}, u32[]{:S(2)}, u32[]{:S(2)}) collective-permute-start(f32[26,24,128]{2,1,0:T(8,128)S(1)} %get-tuple-element.36), channel_id=1, source_target_pairs={{0,4},{4,0},{8,12},{12,8},{16,20},{20,16},{24,28},{28,24},{1,5},{5... | collective-permute-start | bytes 958472 | tf_op jit(solution)/shard_map/ppermute | solution.py:471
  3.3 0.3 collective-permute-start.1
  3.5 1.6 %own_1.1 = (f32[2,5,4,24,128]{4,3,2,1,0:T(8,128)S(1)}, f32[2,5,2,24,128]{4,3,2,1,0:T(8,128)S(1)}, f32[2,5,2,24,128]{4,3,2,1,0:T(8,128)S(1)}, f32[80,128]{1,0:T(8...) custom-call(f32[2,5,4,24,128]{4,3,2,1,0:T(8,128)S(1)} %get-tuple-element.41.own_ref.w_ref, ...), custom_call_target="tpu_custom_call" | custom-call | tf_op jit(solution)/shard_map/own_1/pallas_call | solution.py:496
  5.2 1.3 %collective-permute-start.2 = (f32[80,128]{1,0:T(8,128)S(1)}, f32[80,128]{1,0:T(8,128)S(1)}, u32[]{:S(2)}, u32[]{:S(2)}) collective-permute-start(f32[80,128]{1,0:T(8,128)S(1)} %get-tuple-element.48), channel_id=1, source_target_pairs={{0,1},{1,0},{2,3},{3,2},{4,5},{5,4},{6,7},{7,6},{8,9},{9,8},{10,11... | collective-permute-start | bytes 122888 | tf_op jit(solution)/shard_map/ppermute | solution.py:483
  6.5 3.0 %collective-permute-start.3 = (f32[80,128]{1,0:T(8,128)S(1)}, f32[80,128]{1,0:T(8,128)S(1)}, u32[]{:S(2)}, u32[]{:S(2)}) collective-permute-start(f32[80,128]{1,0:T(8,128)S(1)} %get-tuple-element.49), channel_id=1, source_target_pairs={{1,2},{2,1},{5,6},{6,5},{9,10},{10,9},{13,14},{14,13},{17,18},{18,... | collective-permute-start | bytes 122888 | tf_op jit(solution)/shard_map/ppermute | solution.py:483
  9.5 0.0 collective-permute-done.2.first_ref
  9.5 2.5 %collective-permute-done.3.second_ref = f32[80,128]{1,0:T(8,128)S(1)} collective-permute-done((f32[80,128]{1,0:T(8,128)S(1)}, f32[80,128]{1,0:T(8,128)S(1)}, u32[]{:S(2)}, u32[]{:S(2)}) %collective-permute-start.3) | collective-permute-done | bytes 40992 | tf_op jit(solution)/shard_map/ppermute | solution.py:483
  12.1 0.0 collective-permute-done.outer_ref
  12.1 0.1 face.1
  12.2 1.4 %collective-permute-start.4 = (f32[2,5,2,24,128]{4,3,2,1,0:T(8,128)S(1)}, f32[2,5,2,24,128]{4,3,2,1,0:T(8,128)S(1)}, u32[]{:S(2)}, u32[]{:S(2)}) collective-permute-start(f32[2,5,2,24,128]{4,3,2,1,0:T(8,128)S(1)} %get-tuple-element.51), channel_id=1, source_target_pairs={{0,8},{8,0},{4,12},{12,4},{16,24},{24,16},{20,28},{28,20},{1,9},{9... | collective-permute-start | bytes 737288 | tf_op jit(solution)/shard_map/ppermute | solution.py:483
  13.6 1.9 %collective-permute-start.5 = (f32[2,5,2,24,128]{4,3,2,1,0:T(8,128)S(1)}, f32[2,5,2,24,128]{4,3,2,1,0:T(8,128)S(1)}, u32[]{:S(2)}, u32[]{:S(2)}) collective-permute-start(f32[2,5,2,24,128]{4,3,2,1,0:T(8,128)S(1)} %get-tuple-element.52), channel_id=1, source_target_pairs={{8,16},{16,8},{12,20},{20,12},{9,17},{17,9},{13,21},{21,13},{10,18... | collective-permute-start | bytes 737288 | tf_op jit(solution)/shard_map/ppermute | solution.py:483
  15.5 1.3 %collective-permute-start.6 = (f32[160,128]{1,0:T(8,128)S(1)}, f32[160,128]{1,0:T(8,128)S(1)}, u32[]{:S(2)}, u32[]{:S(2)}) collective-permute-start(f32[160,128]{1,0:T(8,128)S(1)} %get-tuple-element.50._), channel_id=1, source_target_pairs={{0,4},{4,0},{8,12},{12,8},{16,20},{20,16},{24,28},{28,24},{1,5},{5... | collective-permute-start | bytes 245768 | tf_op jit(solution)/shard_map/ppermute | solution.py:471
  16.8 2.6 %collective-permute-done.1.rest_ref = f32[34,24,128]{2,1,0:T(8,128)S(1)} collective-permute-done((f32[34,24,128]{2,1,0:T(8,128)S(1)}, f32[34,24,128]{2,1,0:T(8,128)S(1)}, u32[]{:S(2)}, u32[]{:S(2)}) %collective-permute-start.1) | collective-permute-done | bytes 417824 | tf_op jit(solution)/shard_map/ppermute | solution.py:471
  19.4 1.2 %partner_1.1 = (f32[2,5,4,24,128]{4,3,2,1,0:T(8,128)S(1)}, f32[5,4,24,128]{3,2,1,0:T(8,128)S(1)}, f32[2,5,4,24,128]{4,3,2,1,0:T(8,128)S(1)}, f32[2,5,2,24,128]{4,3,2,1,0:T(8,128)S(1)}) custom-call(f32[26,24,128]{2,1,0:T(8,128)S(1)} %collective-permute-done.outer_ref, f32[34,24,128]{2,1,0:T(8,128)S(1)} %collective-permute-done.1.rest_ref, ...), custom_call_target="tpu_custom_call" | custom-call | tf_op jit(solution)/shard_map/partner_1/pallas_call | solution.py:496
  20.6 0.6 %collective-permute-done.6.message_in = f32[160,128]{1,0:T(8,128)S(1)} collective-permute-done((f32[160,128]{1,0:T(8,128)S(1)}, f32[160,128]{1,0:T(8,128)S(1)}, u32[]{:S(2)}, u32[]{:S(2)}) %collective-permute-start.6) | collective-permute-done | bytes 81952 | tf_op jit(solution)/shard_map/ppermute | solution.py:471
  21.2 0.0 collective-permute-done.4.first_in
  21.2 0.4 collective-permute-done.5.second_in
  21.6 0.4 outer_faces.1
  22.0 1.0 %collective-permute-start.8 = (f32[2,5,2,24,128]{4,3,2,1,0:T(8,128)S(1)}, f32[2,5,2,24,128]{4,3,2,1,0:T(8,128)S(1)}, u32[]{:S(2)}, u32[]{:S(2)}) collective-permute-start(f32[2,5,2,24,128]{4,3,2,1,0:T(8,128)S(1)} %get-tuple-element.60), channel_id=1, source_target_pairs={{0,8},{8,0},{4,12},{12,4},{16,24},{24,16},{20,28},{28,20},{1,9},{9... | collective-permute-start | bytes 737288 | tf_op jit(solution)/shard_map/ppermute | solution.py:483
  22.9 1.9 %collective-permute-start.9 = (f32[2,5,2,24,128]{4,3,2,1,0:T(8,128)S(1)}, f32[2,5,2,24,128]{4,3,2,1,0:T(8,128)S(1)}, u32[]{:S(2)}, u32[]{:S(2)}) collective-permute-start(f32[2,5,2,24,128]{4,3,2,1,0:T(8,128)S(1)} %get-tuple-element.61), channel_id=1, source_target_pairs={{8,16},{16,8},{12,20},{20,12},{9,17},{17,9},{13,21},{21,13},{10,18... | collective-permute-start | bytes 737288 | tf_op jit(solution)/shard_map/ppermute | solution.py:483
  24.9 1.8 %partner_2.1 = (f32[560,128]{1,0:T(8,128)S(1)}, f32[2,5,2,24,128]{4,3,2,1,0:T(8,128)S(1)}, f32[2,5,2,24,128]{4,3,2,1,0:T(8,128)S(1)}, f32[80,128]{1,0:T(8,128)S(1)}) custom-call(f32[2,5,4,24,128]{4,3,2,1,0:T(8,128)S(1)} %get-tuple-element.39.w_ref, f32[2,5,4,24,128]{4,3,2,1,0:T(8,128)S(1)} %get-tuple-element.40.part_ref.part_par, ...), custom_call_target="tpu_custom_call" | custom-call | tf_op jit(solution)/shard_map/partner_2/pallas_call | solution.py:496
  26.7 1.2 %collective-permute-start.7 = (f32[560,128]{1,0:T(8,128)S(1)}, f32[560,128]{1,0:T(8,128)S(1)}, u32[]{:S(2)}, u32[]{:S(2)}) collective-permute-start(f32[560,128]{1,0:T(8,128)S(1)} %get-tuple-element.58), channel_id=1, source_target_pairs={{0,4},{4,0},{8,12},{12,8},{16,20},{20,16},{24,28},{28,24},{1,5},{5... | collective-permute-start | bytes 860168 | tf_op jit(solution)/shard_map/ppermute | solution.py:471
  27.9 1.5 %own_2.1 = (f32[2,5,4,24,128]{4,3,2,1,0:T(8,128)S(1)}, f32[80,128]{1,0:T(8,128)S(1)}, f32[80,128]{1,0:T(8,128)S(1)}) custom-call(f32[2,5,4,24,128]{4,3,2,1,0:T(8,128)S(1)} %get-tuple-element.41.own_ref.w_ref, f32[2,5,4,24,128]{4,3,2,1,0:T(8,128)S(1)} %get-tuple-element.53.part_own.part_ref, f32[2,5,2,24,128]{4,3,2,1,0:T(8,128)S(1)} %get-tuple-element.54.xp_par.xp_in, ...), custom_call_target="tpu_custom_call" | custom-call | tf_op jit(solution)/shard_map/own_2/pallas_call | solution.py:496
  29.4 0.0 collective-permute-done.8.first_in
  29.4 0.7 %collective-permute-done.9.second_in = f32[2,5,2,24,128]{4,3,2,1,0:T(8,128)S(1)} collective-permute-done((f32[2,5,2,24,128]{4,3,2,1,0:T(8,128)S(1)}, f32[2,5,2,24,128]{4,3,2,1,0:T(8,128)S(1)}, u32[]{:S(2)}, u32[]{:S(2)}) %collective-permute-start.9) | collective-permute-done | bytes 245792 | tf_op jit(solution)/shard_map/ppermute | solution.py:483
  30.1 0.1 finish.1
  30.1 1.3 %collective-permute-start.10 = (f32[2,5,2,24,128]{4,3,2,1,0:T(8,128)S(1)}, f32[2,5,2,24,128]{4,3,2,1,0:T(8,128)S(1)}, u32[]{:S(2)}, u32[]{:S(2)}) collective-permute-start(f32[2,5,2,24,128]{4,3,2,1,0:T(8,128)S(1)} %finish.1), channel_id=1, source_target_pairs={{0,4},{4,0},{8,12},{12,8},{16,20},{20,16},{24,28},{28,24},{1,5},{5... | collective-permute-start | bytes 737288 | tf_op jit(solution)/shard_map/ppermute | solution.py:471
  31.4 6.4 %collective-permute-start.12 = (f32[80,128]{1,0:T(8,128)S(1)}, f32[80,128]{1,0:T(8,128)S(1)}, u32[]{:S(2)}, u32[]{:S(2)}) collective-permute-start(f32[80,128]{1,0:T(8,128)S(1)} %get-tuple-element.63._), channel_id=1, source_target_pairs={{1,2},{2,1},{4,5},{5,4},{6,7},{7,6},{9,10},{10,9},{12,13},{13,12},... | collective-permute-start | bytes 122888 | tf_op jit(solution)/shard_map/ppermute | solution.py:493
  37.8 1.9 %collective-permute-start.11 = (f32[80,128]{1,0:T(8,128)S(1)}, f32[80,128]{1,0:T(8,128)S(1)}, u32[]{:S(2)}, u32[]{:S(2)}) collective-permute-start(f32[80,128]{1,0:T(8,128)S(1)} %get-tuple-element.62._), channel_id=1, source_target_pairs={{1,6},{2,5},{4,1},{5,0},{6,3},{7,2},{9,14},{10,13},{12,9},{13,8},{... | collective-permute-start | bytes 122888 | tf_op jit(solution)/shard_map/ppermute | solution.py:493
  39.7 0.0 collective-permute-done.12.rd_ref
  39.8 0.0 collective-permute-done.7.message_ref.inner_ref
  39.8 1.0 %own_3.1._ = f32[2,5,4,2,24,128]{5,4,3,2,1,0:T(8,128)} custom-call(f32[2,5,4,24,128]{4,3,2,1,0:T(8,128)S(1)} %get-tuple-element.65.part_ref, f32[2,5,2,24,128]{4,3,2,1,0:T(8,128)S(1)} %get-tuple-element.66.xp_ref, f32[2,5,2,24,128]{4,3,2,1,0:T(8,128)S(1)} %collective-permute-done.8.first_in, f32[2,5,2,24,128]{4,3,2,1,0:T(8,128)S(1)} %collective-permute-done.9.second_in, ...), custom_call_target="tpu_custom_call" | custom-call | tf_op jit(solution)/shard_map/own_3/pallas_call | solution.py:543
  40.8 2.4 %collective-permute-done.11.rd_ref = f32[80,128]{1,0:T(8,128)S(1)} collective-permute-done((f32[80,128]{1,0:T(8,128)S(1)}, f32[80,128]{1,0:T(8,128)S(1)}, u32[]{:S(2)}, u32[]{:S(2)}) %collective-permute-start.11) | collective-permute-done | bytes 40992 | tf_op jit(solution)/shard_map/ppermute | solution.py:493
  43.1 0.0 collective-permute-done.10.outer_ref
  43.1 0.9 %other_3.1 = f32[2,5,4,2,24,128]{5,4,3,2,1,0:T(8,128)} custom-call(f32[560,128]{1,0:T(8,128)S(1)} %collective-permute-done.7.message_ref.inner_ref, f32[2,5,2,24,128]{4,3,2,1,0:T(8,128)S(1)} %collective-permute-done.10.outer_ref, f32[80,128]{1,0:T(8,128)S(1)} %get-tuple-element.64.rp_ref, ...), custom_call_target="tpu_custom_call", output_to_operand_aliasing={{}: (4, {})} | custom-call | tf_op jit(solution)/shard_map/other_3/pallas_call | solution.py:545
  (1 shorter events, 0.0 us)
Async XLA Ops:
  2.0 10.1 %collective-permute-start = (f32[26,24,128]{2,1,0:T(8,128)S(1)}, f32[26,24,128]{2,1,0:T(8,128)S(1)}, u32[]{:S(2)}, u32[]{:S(2)}) collective-permute-start(f32[26,24,128]{2,1,0:T(8,128)S(1)} %get-tuple-element.36), channel_id=1, source_target_pairs={{0,4},{4,0},{8,12},{12,8},{16,20},{20,16},{24,28},{28,24},{1,5},{5... | collective-permute-start | bytes 958472 | tf_op jit(solution)/shard_map/ppermute | solution.py:471
  3.3 16.2 %collective-permute-start.1 = (f32[34,24,128]{2,1,0:T(8,128)S(1)}, f32[34,24,128]{2,1,0:T(8,128)S(1)}, u32[]{:S(2)}, u32[]{:S(2)}) collective-permute-start(f32[34,24,128]{2,1,0:T(8,128)S(1)} %get-tuple-element.37), channel_id=1, source_target_pairs={{0,4},{4,0},{8,12},{12,8},{16,20},{20,16},{24,28},{28,24},{1,5},{5... | collective-permute-start | bytes 1253384 | tf_op jit(solution)/shard_map/ppermute | solution.py:471
  5.2 4.3 %collective-permute-start.2 = (f32[80,128]{1,0:T(8,128)S(1)}, f32[80,128]{1,0:T(8,128)S(1)}, u32[]{:S(2)}, u32[]{:S(2)}) collective-permute-start(f32[80,128]{1,0:T(8,128)S(1)} %get-tuple-element.48), channel_id=1, source_target_pairs={{0,1},{1,0},{2,3},{3,2},{4,5},{5,4},{6,7},{7,6},{8,9},{9,8},{10,11... | collective-permute-start | bytes 122888 | tf_op jit(solution)/shard_map/ppermute | solution.py:483
  6.5 5.6 %collective-permute-start.3 = (f32[80,128]{1,0:T(8,128)S(1)}, f32[80,128]{1,0:T(8,128)S(1)}, u32[]{:S(2)}, u32[]{:S(2)}) collective-permute-start(f32[80,128]{1,0:T(8,128)S(1)} %get-tuple-element.49), channel_id=1, source_target_pairs={{1,2},{2,1},{5,6},{6,5},{9,10},{10,9},{13,14},{14,13},{17,18},{18,... | collective-permute-start | bytes 122888 | tf_op jit(solution)/shard_map/ppermute | solution.py:483
  12.2 9.0 %collective-permute-start.4 = (f32[2,5,2,24,128]{4,3,2,1,0:T(8,128)S(1)}, f32[2,5,2,24,128]{4,3,2,1,0:T(8,128)S(1)}, u32[]{:S(2)}, u32[]{:S(2)}) collective-permute-start(f32[2,5,2,24,128]{4,3,2,1,0:T(8,128)S(1)} %get-tuple-element.51), channel_id=1, source_target_pairs={{0,8},{8,0},{4,12},{12,4},{16,24},{24,16},{20,28},{28,20},{1,9},{9... | collective-permute-start | bytes 737288 | tf_op jit(solution)/shard_map/ppermute | solution.py:483
  13.6 8.0 %collective-permute-start.5 = (f32[2,5,2,24,128]{4,3,2,1,0:T(8,128)S(1)}, f32[2,5,2,24,128]{4,3,2,1,0:T(8,128)S(1)}, u32[]{:S(2)}, u32[]{:S(2)}) collective-permute-start(f32[2,5,2,24,128]{4,3,2,1,0:T(8,128)S(1)} %get-tuple-element.52), channel_id=1, source_target_pairs={{8,16},{16,8},{12,20},{20,12},{9,17},{17,9},{13,21},{21,13},{10,18... | collective-permute-start | bytes 737288 | tf_op jit(solution)/shard_map/ppermute | solution.py:483
  15.5 5.7 %collective-permute-start.6 = (f32[160,128]{1,0:T(8,128)S(1)}, f32[160,128]{1,0:T(8,128)S(1)}, u32[]{:S(2)}, u32[]{:S(2)}) collective-permute-start(f32[160,128]{1,0:T(8,128)S(1)} %get-tuple-element.50._), channel_id=1, source_target_pairs={{0,4},{4,0},{8,12},{12,8},{16,20},{20,16},{24,28},{28,24},{1,5},{5... | collective-permute-start | bytes 245768 | tf_op jit(solution)/shard_map/ppermute | solution.py:471
  22.0 7.4 %collective-permute-start.8 = (f32[2,5,2,24,128]{4,3,2,1,0:T(8,128)S(1)}, f32[2,5,2,24,128]{4,3,2,1,0:T(8,128)S(1)}, u32[]{:S(2)}, u32[]{:S(2)}) collective-permute-start(f32[2,5,2,24,128]{4,3,2,1,0:T(8,128)S(1)} %get-tuple-element.60), channel_id=1, source_target_pairs={{0,8},{8,0},{4,12},{12,4},{16,24},{24,16},{20,28},{28,20},{1,9},{9... | collective-permute-start | bytes 737288 | tf_op jit(solution)/shard_map/ppermute | solution.py:483
  22.9 7.1 %collective-permute-start.9 = (f32[2,5,2,24,128]{4,3,2,1,0:T(8,128)S(1)}, f32[2,5,2,24,128]{4,3,2,1,0:T(8,128)S(1)}, u32[]{:S(2)}, u32[]{:S(2)}) collective-permute-start(f32[2,5,2,24,128]{4,3,2,1,0:T(8,128)S(1)} %get-tuple-element.61), channel_id=1, source_target_pairs={{8,16},{16,8},{12,20},{20,12},{9,17},{17,9},{13,21},{21,13},{10,18... | collective-permute-start | bytes 737288 | tf_op jit(solution)/shard_map/ppermute | solution.py:483
  26.7 13.1 %collective-permute-start.7 = (f32[560,128]{1,0:T(8,128)S(1)}, f32[560,128]{1,0:T(8,128)S(1)}, u32[]{:S(2)}, u32[]{:S(2)}) collective-permute-start(f32[560,128]{1,0:T(8,128)S(1)} %get-tuple-element.58), channel_id=1, source_target_pairs={{0,4},{4,0},{8,12},{12,8},{16,20},{20,16},{24,28},{28,24},{1,5},{5... | collective-permute-start | bytes 860168 | tf_op jit(solution)/shard_map/ppermute | solution.py:471
  30.1 13.0 %collective-permute-start.10 = (f32[2,5,2,24,128]{4,3,2,1,0:T(8,128)S(1)}, f32[2,5,2,24,128]{4,3,2,1,0:T(8,128)S(1)}, u32[]{:S(2)}, u32[]{:S(2)}) collective-permute-start(f32[2,5,2,24,128]{4,3,2,1,0:T(8,128)S(1)} %finish.1), channel_id=1, source_target_pairs={{0,4},{4,0},{8,12},{12,8},{16,20},{20,16},{24,28},{28,24},{1,5},{5... | collective-permute-start | bytes 737288 | tf_op jit(solution)/shard_map/ppermute | solution.py:471
  31.4 8.4 %collective-permute-start.12 = (f32[80,128]{1,0:T(8,128)S(1)}, f32[80,128]{1,0:T(8,128)S(1)}, u32[]{:S(2)}, u32[]{:S(2)}) collective-permute-start(f32[80,128]{1,0:T(8,128)S(1)} %get-tuple-element.63._), channel_id=1, source_target_pairs={{1,2},{2,1},{4,5},{5,4},{6,7},{7,6},{9,10},{10,9},{12,13},{13,12},... | collective-permute-start | bytes 122888 | tf_op jit(solution)/shard_map/ppermute | solution.py:493
  37.8 5.3 %collective-permute-start.11 = (f32[80,128]{1,0:T(8,128)S(1)}, f32[80,128]{1,0:T(8,128)S(1)}, u32[]{:S(2)}, u32[]{:S(2)}) collective-permute-start(f32[80,128]{1,0:T(8,128)S(1)} %get-tuple-element.62._), channel_id=1, source_target_pairs={{1,6},{2,5},{4,1},{5,0},{6,3},{7,2},{9,14},{10,13},{12,9},{13,8},{... | collective-permute-start | bytes 122888 | tf_op jit(solution)/shard_map/ppermute | solution.py:493

commit v7 on v6

--- a/solution.py
+++ b/solution.py
@@ -425,19 +425,26 @@
     copy.wait()
 
 
-def other_last_kernel(inner_ref, outer_ref, rp_ref, rd_ref, _, out_hbm, value, sem):
-    column, half = place()
+def other_last_kernel(inner_ref, outer_ref, rp_ref, rd_ref, _, out_hbm, value, sems):
+    column, half = place()
+    side = 1 - half
     rows = value.shape[3]
+    copies = []
     for v in range(2):
         for f in range(5):
             for j in range(2):
                 k = ((5 * v + f) * 2 + j) * rows
                 value[v, f, 2 * column + j] = outer_ref[v, f, j]
                 value[v, f, 2 - 2 * column + j] = inner_ref[k : k + rows]
-    add_edges(1 - half, rp_ref, rd_ref, value, [(c, c) for c in range(4)])
-    copy = pltpu.make_async_copy(value, out_hbm.at[:, :, :, 1 - half], sem)
-    copy.start()
-    copy.wait()
+            for c in range(4):
+                k = 2 * ((5 * v + f) * 4 + c)
+                rp, rd = rp_ref[k : k + 2], rd_ref[k : k + 2]
+                value[v, f, c, 0:2] += jnp.where(side == 0, rd, rp)
+                value[v, f, c, rows - 2 : rows] += jnp.where(side == 0, rp, rd)
+        copies.append(pltpu.make_async_copy(value.at[v], out_hbm.at[v, :, :, side], sems.at[v]))
+        copies[v].start()
+    for copy in copies:
+        copy.wait()
 
 
 VM = pl.BlockSpec(memory_space=pltpu.VMEM)
@@ -539,11 +546,12 @@
     rd_own_in = beside(rd_own, False, 0)
     xp_par = xp_par2
     full = shape(2, 5, cells, 2, rows, width)
-    last = dict(out_shape=full, out_specs=HB, scratch_shapes=[whole, pltpu.SemaphoreType.DMA], compiler_params=PARAMS)
-    out = pl.pallas_call(own_last_kernel, name="own_3", in_specs=[VM] * 6, **last)(
+    last = dict(out_shape=full, out_specs=HB, compiler_params=PARAMS)
+    out = pl.pallas_call(own_last_kernel, name="own_3", in_specs=[VM] * 6, scratch_shapes=[whole, pltpu.SemaphoreType.DMA], **last)(
         part_own, xp_par, *faces2, inner, rd_own_in)
     out = pl.pallas_call(
-        other_last_kernel, name="other_3", in_specs=[VM] * 4 + [HB], input_output_aliases={4: 0}, **last,
+        other_last_kernel, name="other_3", in_specs=[VM] * 4 + [HB], input_output_aliases={4: 0},
+        scratch_shapes=[whole, pltpu.SemaphoreType.DMA((2,))], **last,
     )(inner, outer, rp_own, rd_other_in, out)
     return out.reshape(adjoint_vectors.shape)
 

time: 44.3 us -> 44.3 us (level)
  no operation moved by 1% of the time
where the time goes in v7:
time: 44.3 us; the launch traced here: 44 us
  starting transfers between devices  24.1 us (54%)
  Pallas kernels  10.5 us (24%)
  waiting for transfers between devices  9.28 us (21%)
    ppermute x2, starting transfers between devices, beside(): return lax.ppermute(value, ('gx', 'row'), perm)  8.3 us
    ppermute x3, starting transfers between devices, swap_both(): lax.ppermute(second, axis, pairs[1])  6.86 us
    pallas_call x4, Pallas kernels, call(): pl.pallas_call(kernel, name=name, out_shape=outs, in_specs=[VM] * len(ins...  6.1 us
    ppermute x5, starting transfers between devices, local(): trade = lambda value: lax.ppermute(value, 'gx', partner)  5.33 us
    ppermute x3, waiting for transfers between devices, swap_both(): lax.ppermute(second, axis, pairs[1])  3.67 us
    ppermute x3, starting transfers between devices, swap_both(): lax.ppermute(first, axis, pairs[0])  3.62 us
    ppermute x5, waiting for transfers between devices, local(): trade = lambda value: lax.ppermute(value, 'gx', partner)  3.19 us
    ppermute x2, waiting for transfers between devices, beside(): return lax.ppermute(value, ('gx', 'row'), perm)  2.41 us
  transfers between devices with their start and end apart: 13, of which 6 were waited for; matrix products, arithmetic and copies ran while one was open for 0% of the time, Pallas kernels for 17%

profile of v7, /device:TPU:17, one launch (start us, length us, event | category | flops | bytes accessed | tf_op | source)
XLA Modules:
  0.0 44.0 jit_solution(6368030993855020038)
XLA Ops:
  0.0 2.0 %load.1 = (f32[2,5,4,24,128]{4,3,2,1,0:T(8,128)S(1)}, f32[2,5,4,24,128]{4,3,2,1,0:T(8,128)S(1)}, f32[26,24,128]{2,1,0:T(8,128)S(1)}, f32[5,4,24,128]{3,2,1,0:T(8...) custom-call(f32[2,5,4,2,24,128]{5,4,3,2,1,0:T(8,128)} %bitcast.5, ...), custom_call_target="tpu_custom_call" | custom-call | tf_op jit(solution)/shard_map/load/pallas_call | solution.py:514
  2.0 1.3 %collective-permute-start = (f32[26,24,128]{2,1,0:T(8,128)S(1)}, f32[26,24,128]{2,1,0:T(8,128)S(1)}, u32[]{:S(2)}, u32[]{:S(2)}) collective-permute-start(f32[26,24,128]{2,1,0:T(8,128)S(1)} %get-tuple-element.36), channel_id=1, source_target_pairs={{0,4},{4,0},{8,12},{12,8},{16,20},{20,16},{24,28},{28,24},{1,5},{5... | collective-permute-start | bytes 958472 | tf_op jit(solution)/shard_map/ppermute | solution.py:478
  3.3 0.3 collective-permute-start.1
  3.5 1.6 %own_1.1 = (f32[2,5,4,24,128]{4,3,2,1,0:T(8,128)S(1)}, f32[2,5,2,24,128]{4,3,2,1,0:T(8,128)S(1)}, f32[2,5,2,24,128]{4,3,2,1,0:T(8,128)S(1)}, f32[80,128]{1,0:T(8...) custom-call(f32[2,5,4,24,128]{4,3,2,1,0:T(8,128)S(1)} %get-tuple-element.41.own_ref.w_ref, ...), custom_call_target="tpu_custom_call" | custom-call | tf_op jit(solution)/shard_map/own_1/pallas_call | solution.py:503
  5.2 1.3 %collective-permute-start.2 = (f32[80,128]{1,0:T(8,128)S(1)}, f32[80,128]{1,0:T(8,128)S(1)}, u32[]{:S(2)}, u32[]{:S(2)}) collective-permute-start(f32[80,128]{1,0:T(8,128)S(1)} %get-tuple-element.48), channel_id=1, source_target_pairs={{0,1},{1,0},{2,3},{3,2},{4,5},{5,4},{6,7},{7,6},{8,9},{9,8},{10,11... | collective-permute-start | bytes 122888 | tf_op jit(solution)/shard_map/ppermute | solution.py:490
  6.5 3.0 %collective-permute-start.3 = (f32[80,128]{1,0:T(8,128)S(1)}, f32[80,128]{1,0:T(8,128)S(1)}, u32[]{:S(2)}, u32[]{:S(2)}) collective-permute-start(f32[80,128]{1,0:T(8,128)S(1)} %get-tuple-element.49), channel_id=1, source_target_pairs={{1,2},{2,1},{5,6},{6,5},{9,10},{10,9},{13,14},{14,13},{17,18},{18,... | collective-permute-start | bytes 122888 | tf_op jit(solution)/shard_map/ppermute | solution.py:490
  9.5 0.0 collective-permute-done.2.first_ref
  9.5 2.5 %collective-permute-done.3.second_ref = f32[80,128]{1,0:T(8,128)S(1)} collective-permute-done((f32[80,128]{1,0:T(8,128)S(1)}, f32[80,128]{1,0:T(8,128)S(1)}, u32[]{:S(2)}, u32[]{:S(2)}) %collective-permute-start.3) | collective-permute-done | bytes 40992 | tf_op jit(solution)/shard_map/ppermute | solution.py:490
  12.1 0.0 collective-permute-done.outer_ref
  12.1 0.1 face.1
  12.2 1.4 %collective-permute-start.4 = (f32[2,5,2,24,128]{4,3,2,1,0:T(8,128)S(1)}, f32[2,5,2,24,128]{4,3,2,1,0:T(8,128)S(1)}, u32[]{:S(2)}, u32[]{:S(2)}) collective-permute-start(f32[2,5,2,24,128]{4,3,2,1,0:T(8,128)S(1)} %get-tuple-element.51), channel_id=1, source_target_pairs={{0,8},{8,0},{4,12},{12,4},{16,24},{24,16},{20,28},{28,20},{1,9},{9... | collective-permute-start | bytes 737288 | tf_op jit(solution)/shard_map/ppermute | solution.py:490
  13.6 1.9 %collective-permute-start.5 = (f32[2,5,2,24,128]{4,3,2,1,0:T(8,128)S(1)}, f32[2,5,2,24,128]{4,3,2,1,0:T(8,128)S(1)}, u32[]{:S(2)}, u32[]{:S(2)}) collective-permute-start(f32[2,5,2,24,128]{4,3,2,1,0:T(8,128)S(1)} %get-tuple-element.52), channel_id=1, source_target_pairs={{8,16},{16,8},{12,20},{20,12},{9,17},{17,9},{13,21},{21,13},{10,18... | collective-permute-start | bytes 737288 | tf_op jit(solution)/shard_map/ppermute | solution.py:490
  15.5 1.3 %collective-permute-start.6 = (f32[160,128]{1,0:T(8,128)S(1)}, f32[160,128]{1,0:T(8,128)S(1)}, u32[]{:S(2)}, u32[]{:S(2)}) collective-permute-start(f32[160,128]{1,0:T(8,128)S(1)} %get-tuple-element.50._), channel_id=1, source_target_pairs={{0,4},{4,0},{8,12},{12,8},{16,20},{20,16},{24,28},{28,24},{1,5},{5... | collective-permute-start | bytes 245768 | tf_op jit(solution)/shard_map/ppermute | solution.py:478
  16.8 2.6 %collective-permute-done.1.rest_ref = f32[34,24,128]{2,1,0:T(8,128)S(1)} collective-permute-done((f32[34,24,128]{2,1,0:T(8,128)S(1)}, f32[34,24,128]{2,1,0:T(8,128)S(1)}, u32[]{:S(2)}, u32[]{:S(2)}) %collective-permute-start.1) | collective-permute-done | bytes 417824 | tf_op jit(solution)/shard_map/ppermute | solution.py:478
  19.4 1.2 %partner_1.1 = (f32[2,5,4,24,128]{4,3,2,1,0:T(8,128)S(1)}, f32[5,4,24,128]{3,2,1,0:T(8,128)S(1)}, f32[2,5,4,24,128]{4,3,2,1,0:T(8,128)S(1)}, f32[2,5,2,24,128]{4,3,2,1,0:T(8,128)S(1)}) custom-call(f32[26,24,128]{2,1,0:T(8,128)S(1)} %collective-permute-done.outer_ref, f32[34,24,128]{2,1,0:T(8,128)S(1)} %collective-permute-done.1.rest_ref, ...), custom_call_target="tpu_custom_call" | custom-call | tf_op jit(solution)/shard_map/partner_1/pallas_call | solution.py:503
  20.6 0.6 %collective-permute-done.6.message_in = f32[160,128]{1,0:T(8,128)S(1)} collective-permute-done((f32[160,128]{1,0:T(8,128)S(1)}, f32[160,128]{1,0:T(8,128)S(1)}, u32[]{:S(2)}, u32[]{:S(2)}) %collective-permute-start.6) | collective-permute-done | bytes 81952 | tf_op jit(solution)/shard_map/ppermute | solution.py:478
  21.2 0.0 collective-permute-done.4.first_in
  21.2 0.4 collective-permute-done.5.second_in
  21.6 0.4 outer_faces.1
  22.0 1.0 %collective-permute-start.8 = (f32[2,5,2,24,128]{4,3,2,1,0:T(8,128)S(1)}, f32[2,5,2,24,128]{4,3,2,1,0:T(8,128)S(1)}, u32[]{:S(2)}, u32[]{:S(2)}) collective-permute-start(f32[2,5,2,24,128]{4,3,2,1,0:T(8,128)S(1)} %get-tuple-element.60), channel_id=1, source_target_pairs={{0,8},{8,0},{4,12},{12,4},{16,24},{24,16},{20,28},{28,20},{1,9},{9... | collective-permute-start | bytes 737288 | tf_op jit(solution)/shard_map/ppermute | solution.py:490
  22.9 1.9 %collective-permute-start.9 = (f32[2,5,2,24,128]{4,3,2,1,0:T(8,128)S(1)}, f32[2,5,2,24,128]{4,3,2,1,0:T(8,128)S(1)}, u32[]{:S(2)}, u32[]{:S(2)}) collective-permute-start(f32[2,5,2,24,128]{4,3,2,1,0:T(8,128)S(1)} %get-tuple-element.61), channel_id=1, source_target_pairs={{8,16},{16,8},{12,20},{20,12},{9,17},{17,9},{13,21},{21,13},{10,18... | collective-permute-start | bytes 737288 | tf_op jit(solution)/shard_map/ppermute | solution.py:490
  24.9 1.8 %partner_2.1 = (f32[560,128]{1,0:T(8,128)S(1)}, f32[2,5,2,24,128]{4,3,2,1,0:T(8,128)S(1)}, f32[2,5,2,24,128]{4,3,2,1,0:T(8,128)S(1)}, f32[80,128]{1,0:T(8,128)S(1)}) custom-call(f32[2,5,4,24,128]{4,3,2,1,0:T(8,128)S(1)} %get-tuple-element.39.w_ref, f32[2,5,4,24,128]{4,3,2,1,0:T(8,128)S(1)} %get-tuple-element.40.part_ref.part_par, ...), custom_call_target="tpu_custom_call" | custom-call | tf_op jit(solution)/shard_map/partner_2/pallas_call | solution.py:503
  26.7 1.2 %collective-permute-start.7 = (f32[560,128]{1,0:T(8,128)S(1)}, f32[560,128]{1,0:T(8,128)S(1)}, u32[]{:S(2)}, u32[]{:S(2)}) collective-permute-start(f32[560,128]{1,0:T(8,128)S(1)} %get-tuple-element.58), channel_id=1, source_target_pairs={{0,4},{4,0},{8,12},{12,8},{16,20},{20,16},{24,28},{28,24},{1,5},{5... | collective-permute-start | bytes 860168 | tf_op jit(solution)/shard_map/ppermute | solution.py:478
  27.9 1.5 %own_2.1 = (f32[2,5,4,24,128]{4,3,2,1,0:T(8,128)S(1)}, f32[80,128]{1,0:T(8,128)S(1)}, f32[80,128]{1,0:T(8,128)S(1)}) custom-call(f32[2,5,4,24,128]{4,3,2,1,0:T(8,128)S(1)} %get-tuple-element.41.own_ref.w_ref, f32[2,5,4,24,128]{4,3,2,1,0:T(8,128)S(1)} %get-tuple-element.53.part_own.part_ref, f32[2,5,2,24,128]{4,3,2,1,0:T(8,128)S(1)} %get-tuple-element.54.xp_par.xp_in, ...), custom_call_target="tpu_custom_call" | custom-call | tf_op jit(solution)/shard_map/own_2/pallas_call | solution.py:503
  29.4 0.0 collective-permute-done.8.first_in
  29.4 0.7 %collective-permute-done.9.second_in = f32[2,5,2,24,128]{4,3,2,1,0:T(8,128)S(1)} collective-permute-done((f32[2,5,2,24,128]{4,3,2,1,0:T(8,128)S(1)}, f32[2,5,2,24,128]{4,3,2,1,0:T(8,128)S(1)}, u32[]{:S(2)}, u32[]{:S(2)}) %collective-permute-start.9) | collective-permute-done | bytes 245792 | tf_op jit(solution)/shard_map/ppermute | solution.py:490
  30.1 0.1 finish.1
  30.1 1.3 %collective-permute-start.10 = (f32[2,5,2,24,128]{4,3,2,1,0:T(8,128)S(1)}, f32[2,5,2,24,128]{4,3,2,1,0:T(8,128)S(1)}, u32[]{:S(2)}, u32[]{:S(2)}) collective-permute-start(f32[2,5,2,24,128]{4,3,2,1,0:T(8,128)S(1)} %finish.1), channel_id=1, source_target_pairs={{0,4},{4,0},{8,12},{12,8},{16,20},{20,16},{24,28},{28,24},{1,5},{5... | collective-permute-start | bytes 737288 | tf_op jit(solution)/shard_map/ppermute | solution.py:478
  31.4 6.4 %collective-permute-start.12 = (f32[80,128]{1,0:T(8,128)S(1)}, f32[80,128]{1,0:T(8,128)S(1)}, u32[]{:S(2)}, u32[]{:S(2)}) collective-permute-start(f32[80,128]{1,0:T(8,128)S(1)} %get-tuple-element.63._), channel_id=1, source_target_pairs={{1,2},{2,1},{4,5},{5,4},{6,7},{7,6},{9,10},{10,9},{12,13},{13,12},... | collective-permute-start | bytes 122888 | tf_op jit(solution)/shard_map/ppermute | solution.py:500
  37.8 1.9 %collective-permute-start.11 = (f32[80,128]{1,0:T(8,128)S(1)}, f32[80,128]{1,0:T(8,128)S(1)}, u32[]{:S(2)}, u32[]{:S(2)}) collective-permute-start(f32[80,128]{1,0:T(8,128)S(1)} %get-tuple-element.62._), channel_id=1, source_target_pairs={{1,6},{2,5},{4,1},{5,0},{6,3},{7,2},{9,14},{10,13},{12,9},{13,8},{... | collective-permute-start | bytes 122888 | tf_op jit(solution)/shard_map/ppermute | solution.py:500
  39.7 0.0 collective-permute-done.12.rd_ref
  39.8 0.0 collective-permute-done.7.message_ref.inner_ref
  39.8 1.0 %own_3.1._ = f32[2,5,4,2,24,128]{5,4,3,2,1,0:T(8,128)} custom-call(f32[2,5,4,24,128]{4,3,2,1,0:T(8,128)S(1)} %get-tuple-element.65.part_ref, f32[2,5,2,24,128]{4,3,2,1,0:T(8,128)S(1)} %get-tuple-element.66.xp_ref, f32[2,5,2,24,128]{4,3,2,1,0:T(8,128)S(1)} %collective-permute-done.8.first_in, f32[2,5,2,24,128]{4,3,2,1,0:T(8,128)S(1)} %collective-permute-done.9.second_in, ...), custom_call_target="tpu_custom_call" | custom-call | tf_op jit(solution)/shard_map/own_3/pallas_call | solution.py:550
  40.8 2.4 %collective-permute-done.11.rd_ref = f32[80,128]{1,0:T(8,128)S(1)} collective-permute-done((f32[80,128]{1,0:T(8,128)S(1)}, f32[80,128]{1,0:T(8,128)S(1)}, u32[]{:S(2)}, u32[]{:S(2)}) %collective-permute-start.11) | collective-permute-done | bytes 40992 | tf_op jit(solution)/shard_map/ppermute | solution.py:500
  43.1 0.0 collective-permute-done.10.outer_ref
  43.1 0.9 %other_3.1 = f32[2,5,4,2,24,128]{5,4,3,2,1,0:T(8,128)} custom-call(f32[560,128]{1,0:T(8,128)S(1)} %collective-permute-done.7.message_ref.inner_ref, f32[2,5,2,24,128]{4,3,2,1,0:T(8,128)S(1)} %collective-permute-done.10.outer_ref, f32[80,128]{1,0:T(8,128)S(1)} %get-tuple-element.64.rp_ref, ...), custom_call_target="tpu_custom_call", output_to_operand_aliasing={{}: (4, {})} | custom-call | tf_op jit(solution)/shard_map/other_3/pallas_call | solution.py:552
  (1 shorter events, 0.0 us)
Async XLA Ops:
  2.0 10.1 %collective-permute-start = (f32[26,24,128]{2,1,0:T(8,128)S(1)}, f32[26,24,128]{2,1,0:T(8,128)S(1)}, u32[]{:S(2)}, u32[]{:S(2)}) collective-permute-start(f32[26,24,128]{2,1,0:T(8,128)S(1)} %get-tuple-element.36), channel_id=1, source_target_pairs={{0,4},{4,0},{8,12},{12,8},{16,20},{20,16},{24,28},{28,24},{1,5},{5... | collective-permute-start | bytes 958472 | tf_op jit(solution)/shard_map/ppermute | solution.py:478
  3.3 16.2 %collective-permute-start.1 = (f32[34,24,128]{2,1,0:T(8,128)S(1)}, f32[34,24,128]{2,1,0:T(8,128)S(1)}, u32[]{:S(2)}, u32[]{:S(2)}) collective-permute-start(f32[34,24,128]{2,1,0:T(8,128)S(1)} %get-tuple-element.37), channel_id=1, source_target_pairs={{0,4},{4,0},{8,12},{12,8},{16,20},{20,16},{24,28},{28,24},{1,5},{5... | collective-permute-start | bytes 1253384 | tf_op jit(solution)/shard_map/ppermute | solution.py:478
  5.2 4.3 %collective-permute-start.2 = (f32[80,128]{1,0:T(8,128)S(1)}, f32[80,128]{1,0:T(8,128)S(1)}, u32[]{:S(2)}, u32[]{:S(2)}) collective-permute-start(f32[80,128]{1,0:T(8,128)S(1)} %get-tuple-element.48), channel_id=1, source_target_pairs={{0,1},{1,0},{2,3},{3,2},{4,5},{5,4},{6,7},{7,6},{8,9},{9,8},{10,11... | collective-permute-start | bytes 122888 | tf_op jit(solution)/shard_map/ppermute | solution.py:490
  6.5 5.6 %collective-permute-start.3 = (f32[80,128]{1,0:T(8,128)S(1)}, f32[80,128]{1,0:T(8,128)S(1)}, u32[]{:S(2)}, u32[]{:S(2)}) collective-permute-start(f32[80,128]{1,0:T(8,128)S(1)} %get-tuple-element.49), channel_id=1, source_target_pairs={{1,2},{2,1},{5,6},{6,5},{9,10},{10,9},{13,14},{14,13},{17,18},{18,... | collective-permute-start | bytes 122888 | tf_op jit(solution)/shard_map/ppermute | solution.py:490
  12.2 9.0 %collective-permute-start.4 = (f32[2,5,2,24,128]{4,3,2,1,0:T(8,128)S(1)}, f32[2,5,2,24,128]{4,3,2,1,0:T(8,128)S(1)}, u32[]{:S(2)}, u32[]{:S(2)}) collective-permute-start(f32[2,5,2,24,128]{4,3,2,1,0:T(8,128)S(1)} %get-tuple-element.51), channel_id=1, source_target_pairs={{0,8},{8,0},{4,12},{12,4},{16,24},{24,16},{20,28},{28,20},{1,9},{9... | collective-permute-start | bytes 737288 | tf_op jit(solution)/shard_map/ppermute | solution.py:490
  13.6 8.0 %collective-permute-start.5 = (f32[2,5,2,24,128]{4,3,2,1,0:T(8,128)S(1)}, f32[2,5,2,24,128]{4,3,2,1,0:T(8,128)S(1)}, u32[]{:S(2)}, u32[]{:S(2)}) collective-permute-start(f32[2,5,2,24,128]{4,3,2,1,0:T(8,128)S(1)} %get-tuple-element.52), channel_id=1, source_target_pairs={{8,16},{16,8},{12,20},{20,12},{9,17},{17,9},{13,21},{21,13},{10,18... | collective-permute-start | bytes 737288 | tf_op jit(solution)/shard_map/ppermute | solution.py:490
  15.5 5.7 %collective-permute-start.6 = (f32[160,128]{1,0:T(8,128)S(1)}, f32[160,128]{1,0:T(8,128)S(1)}, u32[]{:S(2)}, u32[]{:S(2)}) collective-permute-start(f32[160,128]{1,0:T(8,128)S(1)} %get-tuple-element.50._), channel_id=1, source_target_pairs={{0,4},{4,0},{8,12},{12,8},{16,20},{20,16},{24,28},{28,24},{1,5},{5... | collective-permute-start | bytes 245768 | tf_op jit(solution)/shard_map/ppermute | solution.py:478
  22.0 7.4 %collective-permute-start.8 = (f32[2,5,2,24,128]{4,3,2,1,0:T(8,128)S(1)}, f32[2,5,2,24,128]{4,3,2,1,0:T(8,128)S(1)}, u32[]{:S(2)}, u32[]{:S(2)}) collective-permute-start(f32[2,5,2,24,128]{4,3,2,1,0:T(8,128)S(1)} %get-tuple-element.60), channel_id=1, source_target_pairs={{0,8},{8,0},{4,12},{12,4},{16,24},{24,16},{20,28},{28,20},{1,9},{9... | collective-permute-start | bytes 737288 | tf_op jit(solution)/shard_map/ppermute | solution.py:490
  22.9 7.1 %collective-permute-start.9 = (f32[2,5,2,24,128]{4,3,2,1,0:T(8,128)S(1)}, f32[2,5,2,24,128]{4,3,2,1,0:T(8,128)S(1)}, u32[]{:S(2)}, u32[]{:S(2)}) collective-permute-start(f32[2,5,2,24,128]{4,3,2,1,0:T(8,128)S(1)} %get-tuple-element.61), channel_id=1, source_target_pairs={{8,16},{16,8},{12,20},{20,12},{9,17},{17,9},{13,21},{21,13},{10,18... | collective-permute-start | bytes 737288 | tf_op jit(solution)/shard_map/ppermute | solution.py:490
  26.7 13.1 %collective-permute-start.7 = (f32[560,128]{1,0:T(8,128)S(1)}, f32[560,128]{1,0:T(8,128)S(1)}, u32[]{:S(2)}, u32[]{:S(2)}) collective-permute-start(f32[560,128]{1,0:T(8,128)S(1)} %get-tuple-element.58), channel_id=1, source_target_pairs={{0,4},{4,0},{8,12},{12,8},{16,20},{20,16},{24,28},{28,24},{1,5},{5... | collective-permute-start | bytes 860168 | tf_op jit(solution)/shard_map/ppermute | solution.py:478
  30.1 13.0 %collective-permute-start.10 = (f32[2,5,2,24,128]{4,3,2,1,0:T(8,128)S(1)}, f32[2,5,2,24,128]{4,3,2,1,0:T(8,128)S(1)}, u32[]{:S(2)}, u32[]{:S(2)}) collective-permute-start(f32[2,5,2,24,128]{4,3,2,1,0:T(8,128)S(1)} %finish.1), channel_id=1, source_target_pairs={{0,4},{4,0},{8,12},{12,8},{16,20},{20,16},{24,28},{28,24},{1,5},{5... | collective-permute-start | bytes 737288 | tf_op jit(solution)/shard_map/ppermute | solution.py:478
  31.4 8.4 %collective-permute-start.12 = (f32[80,128]{1,0:T(8,128)S(1)}, f32[80,128]{1,0:T(8,128)S(1)}, u32[]{:S(2)}, u32[]{:S(2)}) collective-permute-start(f32[80,128]{1,0:T(8,128)S(1)} %get-tuple-element.63._), channel_id=1, source_target_pairs={{1,2},{2,1},{4,5},{5,4},{6,7},{7,6},{9,10},{10,9},{12,13},{13,12},... | collective-permute-start | bytes 122888 | tf_op jit(solution)/shard_map/ppermute | solution.py:500
  37.8 5.3 %collective-permute-start.11 = (f32[80,128]{1,0:T(8,128)S(1)}, f32[80,128]{1,0:T(8,128)S(1)}, u32[]{:S(2)}, u32[]{:S(2)}) collective-permute-start(f32[80,128]{1,0:T(8,128)S(1)} %get-tuple-element.62._), channel_id=1, source_target_pairs={{1,6},{2,5},{4,1},{5,0},{6,3},{7,2},{9,14},{10,13},{12,9},{13,8},{... | collective-permute-start | bytes 122888 | tf_op jit(solution)/shard_map/ppermute | solution.py:500
